TPU v7x, 128 devices: a whole 4x4x4 slice. The times are simulated.
128 devices in a mesh: row: 16 (over x, y), col: 8 (over z, core).
Axes of the slice: x: 4, y: 4, z: 4, core: 2. Of those that a mesh axis runs over, the one named last changes fastest.
Arguments:
- tiles: bfloat16 [65536, 128, 128], P(('row', 'col'))
- row_tiles: int32 [65536], P(('row', 'col')), may hold values from 0 to 255, as said below
- col_tiles: int32 [65536], P(('row', 'col')), may hold values from 0 to 4095, as said below
- counts: int32 [128], P(('row', 'col')), may hold values from 128 to 512, as said below
- right_basis: float32 [100, 524288], P(None, ('row', 'col'))
- left_basis: float32 [100, 524288], P(None, ('row', 'col'))
- start: float32 [524288], P(('row', 'col'))
Outputs:
- left_vectors: float32 [2, 524288], P(None, ('row', 'col'))
- right_vectors: float32 [2, 524288], P(None, ('row', 'col'))
- coefficients: float32 [5], replicated
Inputs may be any that keep to these rules, and one draw needn't show every extreme that they name: `row_tiles`: tile rows lie within a row group. `col_tiles`: device d owns tile columns d * 32 up to (d + 1) * 32 - 1. The 512 slots of one device name at most 8 distinct tile columns owned by any one device; in every draw some owner receives exactly 8 distinct live tile columns from every device. `counts`: slots at or beyond a block's count hold no part of the matrix; in every draw some block has 512 live slots.
All inputs are finite; a program needn't handle non-finite values.
Results may differ from a plain program's by a relative error of at most 0.0045.
The roundings to bfloat16 on the way count: a program that leaves them out, or rounds other values in their place, can miss the bound.
Values may be sent and summed in bfloat16 or wider, within the bound.
No kernel may reach another device: no remote copies, remote signals or barrier semaphores. Data moves between devices by JAX's collectives and lax.ppermute only.
A program may use at most 128 MiB of HBM per device.

v0:
```python
import functools

import jax
import jax.numpy as jnp
from jax import lax
from jax.experimental import pallas as pl
from jax.experimental.pallas import tpu as pltpu
from jax.sharding import Mesh
from jax.sharding import PartitionSpec as P

PEER_TILES = 8
COL = ("col_0", "col_1")
ALL = ("row_0", "row_1", "col_0", "col_1")
HIGH = lax.Precision.HIGHEST
F32, BF16, I32 = jnp.float32, jnp.bfloat16, jnp.int32

DEV = 128
OWN = 32
TILE = 128
SLOTS = 512
GROUP = 256
NAMED = DEV * PEER_TILES
PLACE = 104
EXTRA = PEER_TILES + 3


def iota(shape, dim):
    return lax.broadcasted_iota(I32, shape, dim)


def one_hot(condition):
    return jnp.where(condition, 1.0, 0.0).astype(BF16)


def dot(a, b, ca=1, cb=0, precision=None):
    return lax.dot_general(
        a, b, (((ca,), (cb,)), ((), ())), precision=precision, preferred_element_type=F32
    )


def selected(hot, value):
    first = value.astype(BF16)
    rest = value - first.astype(F32)
    second = rest.astype(BF16)
    third = (rest - second.astype(F32)).astype(BF16)
    return dot(hot, third) + dot(hot, second) + dot(hot, first)


def products_row(basis, vector, held):
    size = basis.shape[0]
    total = basis[:, 0:TILE] * vector[0:1, :]
    for k in range(1, OWN):
        total = total + basis[:, k * TILE : (k + 1) * TILE] * vector[k : k + 1, :]
    held[...] = jnp.zeros_like(held)
    held[0:size, :] = total
    row = dot(jnp.ones((8, TILE), F32), held[...], 1, 1, HIGH)[0:1, :]
    square = jnp.sum(vector * vector, keepdims=True)
    return jnp.where(iota((1, TILE), 1) == size, square, row)


def coefficients_of(total, size, row_total):
    lane = iota((1, TILE), 1)
    projection = jnp.where(lane < size, total, 0.0)
    square = jnp.sum(jnp.where(lane == size, total, 0.0), axis=1, keepdims=True)
    coeffs = projection / row_total
    diagonal = iota((size, TILE), 0) == iota((size, TILE), 1)
    column = jnp.sum(jnp.where(diagonal, coeffs, 0.0), axis=1, keepdims=True)
    return projection, square, coeffs, column


def subtract_basis(out, vector, basis, column):
    wide = jnp.broadcast_to(column, (column.shape[0], TILE))
    for k in range(OWN):
        part = jnp.sum(basis[:, k * TILE : (k + 1) * TILE] * wide, axis=0, keepdims=True)
        out[k : k + 1, :] = vector[k : k + 1, :] - part


def norm_of(projection, square, coeffs, column, gram, row_total):
    size = column.shape[0]
    applied = jnp.sum(gram[0:size, :] * coeffs, axis=1, keepdims=True)
    quadratic = jnp.sum(applied * column, axis=0, keepdims=True)
    linear = jnp.sum(coeffs * projection, axis=1, keepdims=True)
    left = jnp.maximum(square - 2.0 * linear + quadratic, 0.0)
    return jnp.sqrt(left / row_total + 1e-06)


def first_sums(col_row, basis, start, out, held):
    owner, place = col_row[...] // OWN, col_row[...] % OWN
    owners = one_hot(iota((DEV, SLOTS), 0) == owner)
    places = one_hot(iota((OWN, SLOTS), 0) == place)
    touched = dot(places, owners, 1, 1) > 0.5
    below = one_hot(iota((OWN, OWN), 1) < iota((OWN, OWN), 0))
    rank = dot(below, one_hot(touched))
    row = products_row(basis, start[...], held)
    held[...] = jnp.zeros_like(held)
    number = (iota((OWN, DEV), 0) + 1).astype(F32)
    for k in range(PEER_TILES):
        here = touched & (rank > k - 0.5) & (rank < k + 0.5)
        named = jnp.sum(jnp.where(here, number, 0.0), axis=0, keepdims=True)
        held[PLACE + k : PLACE + k + 1, :] = named - 1.0
    out[:, 0, :] = held[...].T + row


def tables(counts, col_row, col_col, right, left, pos_row, pos_col, gram_r, gram_l):
    count = counts[0]
    owner, place = col_row[...] // OWN, col_row[...] % OWN
    owners = one_hot(iota((DEV, SLOTS), 0) == owner)
    in_place = iota((OWN, SLOTS), 0) == place
    touched = one_hot(dot(one_hot(in_place), owners, 1, 1) > 0.5)
    below = one_hot(iota((OWN, OWN), 1) < iota((OWN, OWN), 0))
    rank = dot(below, touched).astype(BF16)
    mine = dot(rank, owners)
    mine = jnp.sum(jnp.where(in_place, mine, 0.0), axis=0, keepdims=True)
    position = owner * PEER_TILES + mine.astype(I32)
    pos_row[...] = jnp.where(iota((1, SLOTS), 1) < count, position, -1)
    owner, place = col_col[...] // OWN, col_col[...] % OWN
    owners = one_hot(iota((SLOTS, DEV), 1) == owner)
    mine = dot(owners, rank, 1, 1)
    mine = jnp.where(iota((SLOTS, OWN), 1) == place, mine, 0.0)
    position = owner * PEER_TILES + jnp.sum(mine, axis=1, keepdims=True).astype(I32)
    pos_col[...] = jnp.where(iota((SLOTS, 1), 0) < count, position, -1)
    for basis, gram in ((right, gram_r), (left, gram_l)):
        size = basis.shape[0]
        gram[...] = jnp.zeros_like(gram)
        gram[0:size, 0:size] = dot(basis[...], basis[...], 1, 1, HIGH)


def place_row_of(arrived):
    lane = iota((DEV, NAMED), 0)
    spread = dot(arrived.astype(BF16), one_hot(lane - PLACE == iota((DEV, NAMED), 1) % PEER_TILES))
    own = iota((DEV, NAMED), 1) // PEER_TILES == lane
    row = jnp.sum(jnp.where(own, spread, 0.0), axis=0, keepdims=True)
    return jnp.round(row).astype(I32)


def first_vector(row_total, arrived, start, basis, gram_r, gram_l, rest, send, place_row):
    size = basis.shape[0]
    got = arrived[:, 0, :]
    total = jnp.sum(got, axis=0, keepdims=True)
    _, _, _, column = coefficients_of(total, size, row_total)
    subtract_basis(rest, start, basis, column)
    vector = rest[...]
    named = place_row_of(got)
    place_row[...] = named
    hot = jnp.where(iota((OWN, NAMED), 0) == named, 1.0, 0.0)
    blocks = dot(hot, vector, 0, 0, HIGH).reshape(DEV, PEER_TILES, TILE)
    for k in range(PEER_TILES):
        send[:, k, 0, :] = blocks[:, k, :]
    square = jnp.sum(vector * vector, keepdims=True)
    send[:, PEER_TILES, 0, :] = jnp.broadcast_to(square, (DEV, TILE))
    send[:, PEER_TILES + 1, 0, :] = gram_r[...]
    send[:, PEER_TILES + 2, 0, :] = gram_l[...]


def tiles_times(sources, tiles, products):
    many = 16

    def step(i, carry):
        at = pl.multiple_of(i * many, many)
        block = tiles[pl.ds(at, many)].reshape(many * TILE, TILE)
        wide = dot(sources[pl.ds(at, many), :], block, 1, 1)
        row = iota((many, TILE), 0)
        total = jnp.where(row == 0, wide[:, 0:TILE], 0.0)
        for j in range(1, many):
            total = jnp.where(row == j, wide[:, j * TILE : (j + 1) * TILE], total)
        products[pl.ds(at, many), :] = total
        return carry

    lax.fori_loop(0, SLOTS // many, step, 0, unroll=4)


def times_tiles(sources, tiles, products):
    many = 16

    def step(i, carry):
        at = pl.multiple_of(i * many, many)
        block = tiles[pl.ds(at, many)].reshape(many * TILE, TILE)
        mine = sources[pl.ds(at, many), :]
        row = iota((many, TILE), 0)
        parts = [jnp.where(row == j, mine, jnp.zeros_like(mine)) for j in range(many)]
        products[pl.ds(at, many), :] = dot(jnp.concatenate(parts, axis=1), block)
        return carry

    lax.fori_loop(0, SLOTS // many, step, 0, unroll=4)


def summed_by_row(row_row, products, out):
    rows = one_hot(iota((GROUP, SLOTS), 0) == row_row[...])
    out[...] = selected(rows, products[...]).reshape(out.shape)


def rows_product_first(
    row_total, arrived, pos_col, row_row, tiles, out, norm, grams, sources, products
):
    total = jnp.sum(arrived[:, PEER_TILES, 0, :], axis=0, keepdims=True)
    size = jnp.sqrt(total / row_total + 1e-06)
    norm[...] = size
    grams[0:1, :] = jnp.sum(arrived[:, PEER_TILES + 1, 0, :], axis=0, keepdims=True)
    grams[1:2, :] = jnp.sum(arrived[:, PEER_TILES + 2, 0, :], axis=0, keepdims=True)
    values = jnp.zeros((SLOTS, TILE), F32)
    for k in range(PEER_TILES):
        vector = (arrived[:, k, 0, :] / size).astype(BF16)
        hot = one_hot(iota((SLOTS, DEV), 1) * PEER_TILES + k == pos_col[...])
        values = values + dot(hot, vector)
    sources[...] = values.astype(BF16)
    tiles_times(sources, tiles, products)
    summed_by_row(row_row, products, out)


def rows_product(arrived, pos_col, row_row, tiles, out, sources, products):
    hot = one_hot(iota((SLOTS, NAMED), 1) == pos_col[...])
    vector = arrived[...].reshape(NAMED, TILE)
    sources[...] = dot(hot, vector).astype(BF16)
    tiles_times(sources, tiles, products)
    summed_by_row(row_row, products, out)


def column_product(arrived, row_col, pos_row, tiles, out, sources, products):
    hot = one_hot(iota((SLOTS, GROUP), 1) == row_col[...])
    vector = arrived[...].reshape(GROUP, TILE)
    sources[...] = dot(hot, vector).astype(BF16)
    times_tiles(sources, tiles, products)
    hot = one_hot(iota((NAMED, SLOTS), 0) == pos_row[...])
    out[...] = selected(hot, products[...]).reshape(out.shape)


def image_sums_first(arrived, basis, grams, image, out, held):
    vector = jnp.sum(arrived[...], axis=0)
    image[...] = vector
    row = products_row(basis, vector, held)
    out[:, 0, 0:TILE] = jnp.broadcast_to(row, (DEV, TILE))
    out[:, 0, TILE : 2 * TILE] = jnp.broadcast_to(grams[0:1, :], (DEV, TILE))
    out[:, 0, 2 * TILE : 3 * TILE] = jnp.broadcast_to(grams[1:2, :], (DEV, TILE))


def image_sums(arrived, basis, earlier, factor, image, out, held):
    vector = jnp.sum(arrived[...], axis=0) - factor[...] * earlier[...]
    image[...] = vector
    out[:, 0, :] = jnp.broadcast_to(products_row(basis, vector, held), (DEV, TILE))


def back_sums(divide, arrived, basis, place_row, earlier, by, factor, back, out, held):
    hot = one_hot(iota((OWN, NAMED), 0) == place_row[...])
    before = earlier[...] / by[...] if divide else earlier[...]
    vector = selected(hot, arrived[...].reshape(NAMED, TILE)) - factor[...] * before
    back[...] = vector
    out[:, 0, :] = jnp.broadcast_to(products_row(basis, vector, held), (DEV, TILE))


def left_vector_first(row_total, arrived, image, basis, new, copies, norm, gram_r, gram_l):
    got = arrived[:, 0, :]
    gram_r[...] = got[:, TILE : 2 * TILE]
    gram_l[...] = got[:, 2 * TILE : 3 * TILE]
    total = jnp.sum(got[:, 0:TILE], axis=0, keepdims=True)
    finish(row_total, total, image, basis, gram_l, new, norm)
    copies[...] = jnp.broadcast_to(new[...].astype(BF16), copies.shape)


def finish(row_total, total, vector, basis, gram, new, norm):
    size = basis.shape[0]
    projection, square, coeffs, column = coefficients_of(total, size, row_total)
    factor = norm_of(projection, square, coeffs, column, gram, row_total)
    norm[...] = jnp.broadcast_to(factor, (1, TILE))
    subtract_basis(new, vector, basis, column)
    new[...] = new[...] / factor


def lines(out, at, vector):
    for k in range(OWN):
        out[at : at + 1, k * TILE : (k + 1) * TILE] = vector[k : k + 1, :]


def left_vector(row_total, arrived, image, basis, gram, earlier, new_pair, copies, norm, new):
    total = jnp.sum(arrived[:, 0, :], axis=0, keepdims=True)
    finish(row_total, total, image, basis, gram, new, norm)
    copies[...] = jnp.broadcast_to(new[...].astype(BF16), copies.shape)
    lines(new_pair, 0, earlier)
    lines(new_pair, 1, new)


def right_vector(row_total, arrived, back, basis, gram, place_row, new, send, norm):
    total = jnp.sum(arrived[:, 0, :], axis=0, keepdims=True)
    finish(row_total, total, back, basis, gram, new, norm)
    hot = one_hot(iota((OWN, NAMED), 0) == place_row[...])
    blocks = dot(hot, new[...].astype(BF16), 0, 0)
    send[...] = blocks.astype(BF16).reshape(send.shape)


def last_vector(row_total, arrived, back, basis, gram, earlier, *rest):
    norms, (new_pair, factors, new, norm) = rest[:4], rest[4:]
    total = jnp.sum(arrived[:, 0, :], axis=0, keepdims=True)
    finish(row_total, total, back, basis, gram, new, norm)
    lines(new_pair, 0, earlier)
    lines(new_pair, 1, new)
    for i, value in enumerate((*norms, norm)):
        factors[i] = jnp.max(value[...])


VMEM = pl.BlockSpec(memory_space=pltpu.VMEM)
SMEM = pl.BlockSpec(memory_space=pltpu.SMEM)


def call(body, outs, args, scratch=(), in_specs=None, out_specs=None, mib=24):
    shapes = [jax.ShapeDtypeStruct(s, d) for s, d in outs]
    return pl.pallas_call(
        body,
        out_shape=shapes,
        in_specs=in_specs or [VMEM] * len(args),
        out_specs=out_specs or [VMEM] * len(outs),
        scratch_shapes=[pltpu.VMEM(s, d) for s, d in scratch],
        compiler_params=pltpu.CompilerParams(vmem_limit_bytes=mib << 20),
    )(*args)


def to_all(value):
    return lax.all_to_all(value, ALL, 0, 0, tiled=True)


def in_group(value):
    return lax.all_to_all(value, COL, 0, 0, tiled=True)


def shards(tiles, row_tiles, col_tiles, counts, right_basis, left_basis, start):
    row_total = float(start.shape[0] * DEV)
    with_total = lambda body: functools.partial(body, row_total)
    own = ((OWN, TILE), F32)
    line = ((1, TILE), F32)
    square = ((DEV, TILE), F32)
    sums = ((DEV, 1, TILE), F32)
    blocks = (DEV, PEER_TILES, TILE)
    in_rows = ((8, OWN, TILE), F32)
    copied = ((8, OWN, TILE), BF16)
    work = [((SLOTS, TILE), BF16), ((SLOTS, TILE), F32)]
    right, left = right_basis, left_basis
    begin = start.reshape(OWN, TILE)
    col_row, col_col = col_tiles.reshape(1, SLOTS), col_tiles.reshape(SLOTS, 1)
    row_row, row_col = row_tiles.reshape(1, SLOTS), row_tiles.reshape(SLOTS, 1)

    (pay,) = call(first_sums, [sums], (col_row, right, begin), [square])
    arrived = to_all(pay)
    pos_row, pos_col, gram_r, gram_l = call(
        tables,
        [((1, SLOTS), I32), ((SLOTS, 1), I32), square, square],
        (counts, col_row, col_col, right, left),
        in_specs=[SMEM] + [VMEM] * 4,
    )
    rest, send, place_row = call(
        with_total(first_vector),
        [own, ((DEV, EXTRA, 1, TILE), F32), ((1, NAMED), I32)],
        (arrived, begin, right, gram_r, gram_l),
    )
    partial, beta_zero, grams = call(
        with_total(rows_product_first),
        [in_rows, line, ((2, TILE), F32)],
        (to_all(send), pos_col, row_row, tiles),
        work,
    )
    image, pay = call(
        image_sums_first,
        [own, ((DEV, 1, 3 * TILE), F32)],
        (in_group(partial), left, grams),
        [square],
    )
    left_one, copies, alpha_one, gram_r, gram_l = call(
        with_total(left_vector_first),
        [own, copied, line, square, square],
        (to_all(pay), image, left),
    )
    (outgoing,) = call(
        column_product, [(blocks, F32)], (in_group(copies), row_col, pos_row, tiles), work
    )
    back, pay = call(
        functools.partial(back_sums, True),
        [own, sums],
        (to_all(outgoing), right, place_row, rest, beta_zero, alpha_one),
        [square],
    )
    right_two, send, beta_one = call(
        with_total(right_vector),
        [own, (blocks, BF16), line],
        (to_all(pay), back, right, gram_r, place_row),
    )
    (partial,) = call(rows_product, [in_rows], (to_all(send), pos_col, row_row, tiles), work)
    image, pay = call(
        image_sums, [own, sums], (in_group(partial), left, left_one, beta_one), [square]
    )
    lefts, copies, alpha_two = call(
        with_total(left_vector),
        [((2, OWN * TILE), F32), copied, line],
        (to_all(pay), image, left, gram_l, left_one),
        [own],
    )
    (outgoing,) = call(
        column_product, [(blocks, F32)], (in_group(copies), row_col, pos_row, tiles), work
    )
    back, pay = call(
        functools.partial(back_sums, False),
        [own, sums],
        (to_all(outgoing), right, place_row, right_two, beta_one, alpha_two),
        [square],
    )
    rights, factors = call(
        with_total(last_vector),
        [((2, OWN * TILE), F32), ((5,), F32)],
        (to_all(pay), back, right, gram_r, right_two, beta_zero, alpha_one, beta_one, alpha_two),
        [own, line],
        out_specs=[VMEM, SMEM],
    )
    return lefts, rights, factors


def solution(mesh):
    torus = Mesh(mesh.devices.reshape(4, 4, 4, 2), ALL)
    placed = (
        P(ALL, None, None),
        P(ALL),
        P(ALL),
        P(ALL),
        P(None, ALL),
        P(None, ALL),
        P(ALL),
    )
    return jax.shard_map(
        shards,
        mesh=torus,
        in_specs=placed,
        out_specs=(P(None, ALL), P(None, ALL), P()),
        check_vma=False,
    )
```

profile of v0, /device:TPU:1, one launch (start us, length us, event | category | flops | bytes accessed | tf_op | source)
XLA Modules:
  0.0 243.3 jit_solution(3828401816182591676)
XLA Ops:
  0.7 1.5 copy-done.4
  3.5 1.1 shard_map.94
  4.6 11.5 %all-to-all-start = ((f32[128,1,128]{2,1,0:T(1,128)}), f32[128,1,128]{2,1,0:T(1,128)S(1)}, u32[]{:S(2)}, u32[]{:S(2)}) async-start(f32[128,1,128]{2,1,0:T(1,128)} %shard_map.94), calls=%async_computation | async-start | bytes 131072 | tf_op jit(solution)/shard_map/all_to_all | solution.py:316
  17.0 1.4 copy-done.6
  18.4 3.2 %shard_map.95 = (s32[1,512]{1,0:T(1,128)S(1)}, s32[512,1]{1,0:T(8,128)S(1)}, f32[128,128]{1,0:T(8,128)S(1)}, f32[128,128]{1,0:T(8,128)S(1)}) custom-call(s32[1]{0:T(128)S(6)} %copy.13.counts, s32[1,512]{1,0:T(1,128)S(1)} %bitcast.9, s32[512,1]{1,0:T(8,128)S(1)} %copy.10.col_col, f32[100,4096]{1,0:T(8,128)S(1)} %copy-done.5, f32[100,4096]{1,0:T(8,128)S(1)} %copy-done.6), custom_call_target="tpu_custom_call" | custom-call | tf_op jit(solution)/shard_map/pallas_call | solution.py:305
  22.9 2.6 %all-to-all-done.arrived = f32[128,1,128]{2,1,0:T(1,128)S(1)} async-done(((f32[128,1,128]{2,1,0:T(1,128)}), f32[128,1,128]{2,1,0:T(1,128)S(1)}, u32[]{:S(2)}, u32[]{:S(2)}) %all-to-all-start) | async-done | bytes 65568 | tf_op jit(solution)/shard_map/all_to_all | solution.py:316
  25.5 1.0 shard_map.96
  26.5 22.8 %all_to_all.65.arrived = f32[128,11,1,128]{3,2,1,0:T(1,128)S(1)} all-to-all(f32[128,11,1,128]{3,2,1,0:T(1,128)S(1)} %get-tuple-element.36), channel_id=1, replica_groups=mesh['row_0'=4,'row_1'=4,'col_0'=4,'col_1'=2] {'row_0','row_1','col_0','..., dimensions={0} | all-to-all | bytes 1441792 | tf_op jit(solution)/shard_map/all_to_all | solution.py:316
  49.3 5.8 %copy-done = bf16[512,128,128]{2,1,0:T(8,128)(2,1)S(1)} copy-done((bf16[512,128,128]{2,1,0:T(8,128)(2,1)S(1)}, bf16[512,128,128]{2,1,0:T(8,128)(2,1)}, u32[]{:S(2)}) %copy-start) | copy-done | bytes 16777240
  55.1 6.2 %shard_map.97 = (f32[8,32,128]{2,1,0:T(8,128)S(1)}, f32[1,128]{1,0:T(1,128)S(1)}, f32[2,128]{1,0:T(2,128)S(1)}) custom-call(f32[128,11,1,128]{3,2,1,0:T(1,128)S(1)} %all_to_all.65.arrived, s32[512,1]{1,0:T(8,128)S(1)} %copy-done.11, s32[1,512]{1,0:T(1,128)S(1)} %bitcast.11, bf16[512,128,128]{2,1,0:T(8,128)(2,1)S(1)} %copy-done), custom_call_target="tpu_custom_call" | custom-call | tf_op jit(solution)/shard_map/pallas_call | solution.py:305
  61.4 8.8 %all_to_all.66.arrived = f32[8,32,128]{2,1,0:T(8,128)S(1)} all-to-all(f32[8,32,128]{2,1,0:T(8,128)S(1)} %get-tuple-element.38), channel_id=1, replica_groups=mesh['row_0'=4,'row_1'=4,'col_0'=4,'col_1'=2] {'col_0','col_1'}, dimensions={0} | all-to-all | bytes 262144 | tf_op jit(solution)/shard_map/all_to_all | solution.py:320
  70.6 14.3 %all_to_all.67.arrived = f32[128,1,384]{2,1,0:T(1,128)S(1)} all-to-all(f32[128,1,384]{2,1,0:T(1,128)S(1)} %get-tuple-element.40), channel_id=1, replica_groups=mesh['row_0'=4,'row_1'=4,'col_0'=4,'col_1'=2] {'row_0','row_1','col_0','..., dimensions={0} | all-to-all | bytes 393216 | tf_op jit(solution)/shard_map/all_to_all | solution.py:316
  87.0 4.2 %all-to-all-start.4 = ((bf16[8,32,128]{2,1,0:T(8,128)(2,1)}), bf16[8,32,128]{2,1,0:T(8,128)(2,1)S(1)}, u32[]{:S(2)}, u32[]{:S(2)}) async-start(bf16[8,32,128]{2,1,0:T(8,128)(2,1)} %copy-done.17), calls=%async_computation.4 | async-start | bytes 131072 | tf_op jit(solution)/shard_map/all_to_all | solution.py:320
  91.2 1.6 copy.11.row_col
  92.8 3.3 %all-to-all-done.4.arrived = bf16[8,32,128]{2,1,0:T(8,128)(2,1)S(1)} async-done(((bf16[8,32,128]{2,1,0:T(8,128)(2,1)}), bf16[8,32,128]{2,1,0:T(8,128)(2,1)S(1)}, u32[]{:S(2)}, u32[]{:S(2)}) %all-to-all-start.4) | async-done | bytes 65568 | tf_op jit(solution)/shard_map/all_to_all | solution.py:320
  96.1 5.8 %copy-done.1 = bf16[512,128,128]{2,1,0:T(8,128)(2,1)S(1)} copy-done((bf16[512,128,128]{2,1,0:T(8,128)(2,1)S(1)}, bf16[512,128,128]{2,1,0:T(8,128)(2,1)}, u32[]{:S(2)}) %copy-start.1) | copy-done | bytes 16777240
  101.9 0.9 copy-done.8
  103.5 4.4 %shard_map.100 = f32[128,8,128]{2,1,0:T(8,128)S(1)} custom-call(bf16[8,32,128]{2,1,0:T(8,128)(2,1)S(1)} %all-to-all-done.4.arrived, s32[512,1]{1,0:T(8,128)S(1)} %copy-done.8, s32[1,512]{1,0:T(1,128)S(1)} %copy-done.27, bf16[512,128,128]{2,1,0:T(8,128)(2,1)S(1)} %copy-done.1), custom_call_target="tpu_custom_call" | custom-call | tf_op jit(solution)/shard_map/pallas_call | solution.py:305
  107.9 17.4 %all_to_all.68.arrived = f32[128,8,128]{2,1,0:T(8,128)S(1)} all-to-all(f32[128,8,128]{2,1,0:T(8,128)S(1)} %shard_map.100), channel_id=1, replica_groups=mesh['row_0'=4,'row_1'=4,'col_0'=4,'col_1'=2] {'row_0','row_1','col_0','..., dimensions={0} | all-to-all | bytes 1048576 | tf_op jit(solution)/shard_map/all_to_all | solution.py:316
  126.0 13.8 %all_to_all.69.arrived = f32[128,1,128]{2,1,0:T(1,128)S(1)} all-to-all(f32[128,1,128]{2,1,0:T(1,128)S(1)} %get-tuple-element.48), channel_id=1, replica_groups=mesh['row_0'=4,'row_1'=4,'col_0'=4,'col_1'=2] {'row_0','row_1','col_0','..., dimensions={0} | all-to-all | bytes 131072 | tf_op jit(solution)/shard_map/all_to_all | solution.py:316
  140.3 15.5 %all_to_all.70.arrived = bf16[128,8,128]{2,1,0:T(8,128)(2,1)S(1)} all-to-all(bf16[128,8,128]{2,1,0:T(8,128)(2,1)S(1)} %get-tuple-element.51), channel_id=1, replica_groups=mesh['row_0'=4,'row_1'=4,'col_0'=4,'col_1'=2] {'row_0','row_1','col_0','..., dimensions={0} | all-to-all | bytes 524288 | tf_op jit(solution)/shard_map/all_to_all | solution.py:316
  155.8 5.8 %copy-done.2 = bf16[512,128,128]{2,1,0:T(8,128)(2,1)S(1)} copy-done((bf16[512,128,128]{2,1,0:T(8,128)(2,1)S(1)}, bf16[512,128,128]{2,1,0:T(8,128)(2,1)}, u32[]{:S(2)}) %copy-start.2) | copy-done | bytes 16777240
  161.6 6.3 %shard_map.103 = f32[8,32,128]{2,1,0:T(8,128)S(1)} custom-call(bf16[128,8,128]{2,1,0:T(8,128)(2,1)S(1)} %all_to_all.70.arrived, s32[512,1]{1,0:T(8,128)S(1)} %copy-done.12, s32[1,512]{1,0:T(1,128)S(1)} %bitcast.12, bf16[512,128,128]{2,1,0:T(8,128)(2,1)S(1)} %copy-done.2), custom_call_target="tpu_custom_call" | custom-call | tf_op jit(solution)/shard_map/pallas_call | solution.py:305
  167.9 8.9 %all_to_all.71.arrived = f32[8,32,128]{2,1,0:T(8,128)S(1)} all-to-all(f32[8,32,128]{2,1,0:T(8,128)S(1)} %shard_map.103), channel_id=1, replica_groups=mesh['row_0'=4,'row_1'=4,'col_0'=4,'col_1'=2] {'col_0','col_1'}, dimensions={0} | all-to-all | bytes 262144 | tf_op jit(solution)/shard_map/all_to_all | solution.py:320
  177.1 13.4 %all_to_all.72.arrived = f32[128,1,128]{2,1,0:T(1,128)S(1)} all-to-all(f32[128,1,128]{2,1,0:T(1,128)S(1)} %get-tuple-element.54), channel_id=1, replica_groups=mesh['row_0'=4,'row_1'=4,'col_0'=4,'col_1'=2] {'row_0','row_1','col_0','..., dimensions={0} | all-to-all | bytes 131072 | tf_op jit(solution)/shard_map/all_to_all | solution.py:316
  190.6 0.9 shard_map.105
  191.5 8.4 %all_to_all.73.arrived = bf16[8,32,128]{2,1,0:T(8,128)(2,1)S(1)} all-to-all(bf16[8,32,128]{2,1,0:T(8,128)(2,1)S(1)} %get-tuple-element.58), channel_id=1, replica_groups=mesh['row_0'=4,'row_1'=4,'col_0'=4,'col_1'=2] {'col_0','col_1'}, dimensions={0} | all-to-all | bytes 131072 | tf_op jit(solution)/shard_map/all_to_all | solution.py:320
  199.9 5.8 %copy-done.3 = bf16[512,128,128]{2,1,0:T(8,128)(2,1)S(1)} copy-done((bf16[512,128,128]{2,1,0:T(8,128)(2,1)S(1)}, bf16[512,128,128]{2,1,0:T(8,128)(2,1)}, u32[]{:S(2)}) %copy-start.3) | copy-done | bytes 16777240
  205.7 4.4 %shard_map.106 = f32[128,8,128]{2,1,0:T(8,128)S(1)} custom-call(bf16[8,32,128]{2,1,0:T(8,128)(2,1)S(1)} %all_to_all.73.arrived, s32[512,1]{1,0:T(8,128)S(1)} %copy-done.9, s32[1,512]{1,0:T(1,128)S(1)} %copy-done.28, bf16[512,128,128]{2,1,0:T(8,128)(2,1)S(1)} %copy-done.3), custom_call_target="tpu_custom_call" | custom-call | tf_op jit(solution)/shard_map/pallas_call | solution.py:305
  210.2 17.7 %all_to_all.74.arrived = f32[128,8,128]{2,1,0:T(8,128)S(1)} all-to-all(f32[128,8,128]{2,1,0:T(8,128)S(1)} %shard_map.106), channel_id=1, replica_groups=mesh['row_0'=4,'row_1'=4,'col_0'=4,'col_1'=2] {'row_0','row_1','col_0','..., dimensions={0} | all-to-all | bytes 1048576 | tf_op jit(solution)/shard_map/all_to_all | solution.py:316
  228.5 13.8 %all_to_all.75.arrived = f32[128,1,128]{2,1,0:T(1,128)S(1)} all-to-all(f32[128,1,128]{2,1,0:T(1,128)S(1)} %get-tuple-element.61), channel_id=1, replica_groups=mesh['row_0'=4,'row_1'=4,'col_0'=4,'col_1'=2] {'row_0','row_1','col_0','..., dimensions={0} | all-to-all | bytes 131072 | tf_op jit(solution)/shard_map/all_to_all | solution.py:316
  242.2 0.9 shard_map.108
  (66 shorter events, 8.3 us)
Async XLA Ops:
  0.6 15.5 %copy-start.21 = (s32[512]{0:T(512)S(1)}, s32[512]{0:T(512)}, u32[]{:S(2)}) copy-start(s32[512]{0:T(512)} %param.9) | copy-start | bytes 6148
  0.6 1.5 copy-start.4
  2.1 0.7 copy-start.13
  2.8 0.7 copy-start.20
  3.5 13.5 %copy-start.5 = (f32[100,4096]{1,0:T(8,128)S(1)}, f32[100,4096]{1,0:T(8,128)}, u32[]{:S(2)}) copy-start(f32[100,4096]{1,0:T(8,128)} %basis.19) | copy-start | bytes 4915204
  4.6 20.9 %all-to-all-start = ((f32[128,1,128]{2,1,0:T(1,128)}), f32[128,1,128]{2,1,0:T(1,128)S(1)}, u32[]{:S(2)}, u32[]{:S(2)}) async-start(f32[128,1,128]{2,1,0:T(1,128)} %shard_map.94), calls=%async_computation | async-start | bytes 131072 | tf_op jit(solution)/shard_map/all_to_all | solution.py:316
  17.0 1.5 copy-start.6
  18.4 7.1 %copy-start.14 = (f32[4096]{0:T(1024)S(1)}, f32[4096]{0:T(1024)}, u32[]{:S(2)}) copy-start(f32[4096]{0:T(1024)} %param.13) | copy-start | bytes 49156
  21.6 0.7 copy-start.10
  22.9 26.4 %copy-start.22 = (s32[512]{0:T(512)S(1)}, s32[512]{0:T(512)}, u32[]{:S(2)}) copy-start(s32[512]{0:T(512)} %param.8) | copy-start | bytes 6148
  25.5 23.8 %copy-start.11 = (s32[512,1]{1,0:T(8,128)S(1)}, s32[512,1]{1,0:T(8,128)}, u32[]{:S(2)}) copy-start(s32[512,1]{1,0:T(8,128)} %copy-done.10) | copy-start | bytes 6148
  26.5 22.8 %copy-start.18 = (s32[1,1024]{1,0:T(1,128)}, s32[1,1024]{1,0:T(1,128)S(1)}, u32[]{:S(2)}) copy-start(s32[1,1024]{1,0:T(1,128)S(1)} %get-tuple-element.44.place_row) | copy-start | bytes 12292
  26.5 22.8 %copy-start.24 = (f32[32,128]{1,0:T(8,128)}, f32[32,128]{1,0:T(8,128)S(1)}, u32[]{:S(2)}) copy-start(f32[32,128]{1,0:T(8,128)S(1)} %get-tuple-element.45.earlier) | copy-start | bytes 49156
  49.3 5.8 %copy-start = (bf16[512,128,128]{2,1,0:T(8,128)(2,1)S(1)}, bf16[512,128,128]{2,1,0:T(8,128)(2,1)}, u32[]{:S(2)}) copy-start(bf16[512,128,128]{2,1,0:T(8,128)(2,1)} %tiles.7) | copy-start | bytes 50331652
  55.1 15.1 %copy-start.7 = (f32[100,4096]{1,0:T(8,128)S(1)}, f32[100,4096]{1,0:T(8,128)}, u32[]{:S(2)}) copy-start(f32[100,4096]{1,0:T(8,128)} %basis.17) | copy-start | bytes 4915204
  61.4 23.5 %copy-start.29 = (f32[1,128]{1,0:T(1,128)}, f32[1,128]{1,0:T(1,128)S(1)}, u32[]{:S(2)}) copy-start(f32[1,128]{1,0:T(1,128)S(1)} %get-tuple-element.46.by.rest_0_) | copy-start | bytes 1540
  85.8 0.6 copy-start.17
  87.0 9.1 %all-to-all-start.4 = ((bf16[8,32,128]{2,1,0:T(8,128)(2,1)}), bf16[8,32,128]{2,1,0:T(8,128)(2,1)S(1)}, u32[]{:S(2)}, u32[]{:S(2)}) async-start(bf16[8,32,128]{2,1,0:T(8,128)(2,1)} %copy-done.17), calls=%async_computation.4 | async-start | bytes 131072 | tf_op jit(solution)/shard_map/all_to_all | solution.py:320
  96.1 5.8 %copy-start.1 = (bf16[512,128,128]{2,1,0:T(8,128)(2,1)S(1)}, bf16[512,128,128]{2,1,0:T(8,128)(2,1)}, u32[]{:S(2)}) copy-start(bf16[512,128,128]{2,1,0:T(8,128)(2,1)} %tiles.7) | copy-start | bytes 50331652
  101.9 0.9 copy-start.8
  102.8 0.7 copy-start.27
  103.5 21.8 %copy-start.19 = (s32[1,1024]{1,0:T(1,128)S(1)}, s32[1,1024]{1,0:T(1,128)}, u32[]{:S(2)}) copy-start(s32[1,1024]{1,0:T(1,128)} %copy-done.18) | copy-start | bytes 12292
  103.5 21.8 %copy-start.25 = (f32[32,128]{1,0:T(8,128)S(1)}, f32[32,128]{1,0:T(8,128)}, u32[]{:S(2)}) copy-start(f32[32,128]{1,0:T(8,128)} %copy-done.24) | copy-start | bytes 49156
  103.5 21.8 %copy-start.30 = (f32[1,128]{1,0:T(1,128)S(1)}, f32[1,128]{1,0:T(1,128)}, u32[]{:S(2)}) copy-start(f32[1,128]{1,0:T(1,128)} %copy-done.29) | copy-start | bytes 1540
  103.5 21.8 %copy-start.32 = (f32[1,128]{1,0:T(1,128)S(1)}, f32[1,128]{1,0:T(1,128)}, u32[]{:S(2)}) copy-start(f32[1,128]{1,0:T(1,128)} %copy-done.31) | copy-start | bytes 1540
  126.0 29.8 %copy-start.12 = (s32[512,1]{1,0:T(8,128)S(1)}, s32[512,1]{1,0:T(8,128)}, u32[]{:S(2)}) copy-start(s32[512,1]{1,0:T(8,128)} %copy-done.10) | copy-start | bytes 6148
  126.0 29.8 %copy-start.23 = (s32[512]{0:T(512)S(1)}, s32[512]{0:T(512)}, u32[]{:S(2)}) copy-start(s32[512]{0:T(512)} %param.8) | copy-start | bytes 6148
  155.8 5.8 %copy-start.2 = (bf16[512,128,128]{2,1,0:T(8,128)(2,1)S(1)}, bf16[512,128,128]{2,1,0:T(8,128)(2,1)}, u32[]{:S(2)}) copy-start(bf16[512,128,128]{2,1,0:T(8,128)(2,1)} %tiles.7) | copy-start | bytes 50331652
  167.9 22.7 %copy-start.16 = (f32[128,128]{1,0:T(8,128)S(1)}, f32[128,128]{1,0:T(8,128)}, u32[]{:S(2)}) copy-start(f32[128,128]{1,0:T(8,128)} %copy-done.15) | copy-start | bytes 196612
  176.8 23.2 %copy-start.9 = (s32[512,1]{1,0:T(8,128)S(1)}, s32[512,1]{1,0:T(8,128)}, u32[]{:S(2)}) copy-start(s32[512,1]{1,0:T(8,128)} %copy.11.row_col) | copy-start | bytes 6148
  176.8 23.2 %copy-start.28 = (s32[1,512]{1,0:T(1,128)S(1)}, s32[1,512]{1,0:T(1,128)}, u32[]{:S(2)}) copy-start(s32[1,512]{1,0:T(1,128)} %copy-done.26) | copy-start | bytes 6148
  199.9 5.8 %copy-start.3 = (bf16[512,128,128]{2,1,0:T(8,128)(2,1)S(1)}, bf16[512,128,128]{2,1,0:T(8,128)(2,1)}, u32[]{:S(2)}) copy-start(bf16[512,128,128]{2,1,0:T(8,128)(2,1)} %tiles.7) | copy-start | bytes 50331652
  (3 other events, 1.8 us)
where the time goes:
time: 244 us; the launch traced here: 243 us
  blocking collectives  155 us (64%)
  local copies, waits for them, and re-layouts  33.8 us (14%)
  Pallas kernels  31.5 us (13%)
  starting transfers between devices  15.7 us (6%)
  waiting for transfers between devices  5.89 us (2%)
    all_to_all x8, blocking collectives, to_all(): return lax.all_to_all(value, ALL, 0, 0, tiled=True)  129 us
    unnamed x66, local copies, waits for them, and re-layouts  32.2 us
    pallas_call x15, Pallas kernels, call(): pl.pallas_call(body, out_shape=shapes, in_specs=in_specs or [VMEM] * len(...  31.5 us
    all_to_all x3, blocking collectives, in_group(): return lax.all_to_all(value, COL, 0, 0, tiled=True)  26.1 us
    all_to_all x1, starting transfers between devices, to_all(): return lax.all_to_all(value, ALL, 0, 0, tiled=True)  11.5 us
  transfers between devices with their start and end apart: 2, of which 2 were waited for; matrix products, arithmetic and copies ran while one was open for 1% of the time, Pallas kernels for 1%

commit v1 on v0

--- a/solution.py
+++ b/solution.py
@@ -21,6 +21,8 @@
 GROUP = 256
 NAMED = DEV * PEER_TILES
 PLACE = 104
+PARTS = 4
+CHUNK = 64
 EXTRA = PEER_TILES + 3
 
 
@@ -46,10 +48,12 @@
     return dot(hot, third) + dot(hot, second) + dot(hot, first)
 
 
-def products_row(basis, vector, held):
+def products_row(basis, vector, held, copies=()):
     size = basis.shape[0]
-    total = basis[:, 0:TILE] * vector[0:1, :]
-    for k in range(1, OWN):
+    total = jnp.zeros((size, TILE), F32)
+    for k in range(OWN):
+        if copies and k % (OWN // PARTS) == 0:
+            copies[k // (OWN // PARTS)].wait()
         total = total + basis[:, k * TILE : (k + 1) * TILE] * vector[k : k + 1, :]
     held[...] = jnp.zeros_like(held)
     held[0:size, :] = total
@@ -84,14 +88,26 @@
     return jnp.sqrt(left / row_total + 1e-06)
 
 
-def first_sums(col_row, basis, start, out, held):
+def first_sums(col_hbm, basis_hbm, start_hbm, out, held, col_row, basis, start, sems):
+    wide = basis.shape[1] // PARTS
+    parts = [pl.ds(i * wide, wide) for i in range(PARTS)]
+    copies = [pltpu.make_async_copy(col_hbm, col_row, sems.at[0])]
+    copies += [pltpu.make_async_copy(start_hbm, start, sems.at[1])]
+    copies += [
+        pltpu.make_async_copy(basis_hbm.at[:, part], basis.at[:, part], sems.at[2 + i])
+        for i, part in enumerate(parts)
+    ]
+    for copy in copies:
+        copy.start()
+    copies[0].wait()
     owner, place = col_row[...] // OWN, col_row[...] % OWN
     owners = one_hot(iota((DEV, SLOTS), 0) == owner)
     places = one_hot(iota((OWN, SLOTS), 0) == place)
     touched = dot(places, owners, 1, 1) > 0.5
     below = one_hot(iota((OWN, OWN), 1) < iota((OWN, OWN), 0))
     rank = dot(below, one_hot(touched))
-    row = products_row(basis, start[...], held)
+    copies[1].wait()
+    row = products_row(basis, start[...], held, copies[2:])
     held[...] = jnp.zeros_like(held)
     number = (iota((OWN, DEV), 0) + 1).astype(F32)
     for k in range(PEER_TILES):
@@ -101,8 +117,19 @@
     out[:, 0, :] = held[...].T + row
 
 
-def tables(counts, col_row, col_col, right, left, pos_row, pos_col, gram_r, gram_l):
+def as_column(row):
+    return jnp.broadcast_to(row.astype(F32), (TILE, SLOTS)).T[:, 0:1].astype(I32)
+
+
+def tables(counts, col_hbm, row_hbm, right_hbm, left_hbm, *refs):
+    pos_row, pos_col, row_row, row_col, gram_r, gram_l, col_row, right, left, sems = refs
+    sources = (col_hbm, row_hbm, right_hbm, left_hbm)
+    targets = (col_row, row_row, right, left)
+    copies = [pltpu.make_async_copy(a, b, sems.at[i]) for i, (a, b) in enumerate(zip(sources, targets))]
+    for copy in copies:
+        copy.start()
     count = counts[0]
+    copies[0].wait()
     owner, place = col_row[...] // OWN, col_row[...] % OWN
     owners = one_hot(iota((DEV, SLOTS), 0) == owner)
     in_place = iota((OWN, SLOTS), 0) == place
@@ -112,14 +139,13 @@
     mine = dot(rank, owners)
     mine = jnp.sum(jnp.where(in_place, mine, 0.0), axis=0, keepdims=True)
     position = owner * PEER_TILES + mine.astype(I32)
-    pos_row[...] = jnp.where(iota((1, SLOTS), 1) < count, position, -1)
-    owner, place = col_col[...] // OWN, col_col[...] % OWN
-    owners = one_hot(iota((SLOTS, DEV), 1) == owner)
-    mine = dot(owners, rank, 1, 1)
-    mine = jnp.where(iota((SLOTS, OWN), 1) == place, mine, 0.0)
-    position = owner * PEER_TILES + jnp.sum(mine, axis=1, keepdims=True).astype(I32)
-    pos_col[...] = jnp.where(iota((SLOTS, 1), 0) < count, position, -1)
-    for basis, gram in ((right, gram_r), (left, gram_l)):
+    position = jnp.where(iota((1, SLOTS), 1) < count, position, -1)
+    pos_row[...] = position
+    pos_col[...] = as_column(position)
+    copies[1].wait()
+    row_col[...] = as_column(row_row[...])
+    for copy, basis, gram in ((copies[2], right, gram_r), (copies[3], left, gram_l)):
+        copy.wait()
         size = basis.shape[0]
         gram[...] = jnp.zeros_like(gram)
         gram[0:size, 0:size] = dot(basis[...], basis[...], 1, 1, HIGH)
@@ -133,15 +159,24 @@
     return jnp.round(row).astype(I32)
 
 
-def first_vector(row_total, arrived, start, basis, gram_r, gram_l, rest, send, place_row):
+def first_vector(row_total, arrived, start_hbm, basis_hbm, gram_r, gram_l, *refs):
+    rest, send, place_row, start, basis, sems = refs
+    copies = [
+        pltpu.make_async_copy(start_hbm, start, sems.at[0]),
+        pltpu.make_async_copy(basis_hbm, basis, sems.at[1]),
+    ]
+    for copy in copies:
+        copy.start()
     size = basis.shape[0]
     got = arrived[:, 0, :]
     total = jnp.sum(got, axis=0, keepdims=True)
     _, _, _, column = coefficients_of(total, size, row_total)
+    named = place_row_of(got)
+    place_row[...] = named
+    for copy in copies:
+        copy.wait()
     subtract_basis(rest, start, basis, column)
     vector = rest[...]
-    named = place_row_of(got)
-    place_row[...] = named
     hot = jnp.where(iota((OWN, NAMED), 0) == named, 1.0, 0.0)
     blocks = dot(hot, vector, 0, 0, HIGH).reshape(DEV, PEER_TILES, TILE)
     for k in range(PEER_TILES):
@@ -152,36 +187,39 @@
     send[:, PEER_TILES + 2, 0, :] = gram_l[...]
 
 
-def tiles_times(sources, tiles, products):
+def tiles_times(sources, tiles, products, copies=None):
     many = 16
-
-    def step(i, carry):
-        at = pl.multiple_of(i * many, many)
-        block = tiles[pl.ds(at, many)].reshape(many * TILE, TILE)
-        wide = dot(sources[pl.ds(at, many), :], block, 1, 1)
-        row = iota((many, TILE), 0)
-        total = jnp.where(row == 0, wide[:, 0:TILE], 0.0)
-        for j in range(1, many):
-            total = jnp.where(row == j, wide[:, j * TILE : (j + 1) * TILE], total)
-        products[pl.ds(at, many), :] = total
+    row = iota((many, TILE), 0)
+
+    def step(chunk, carry):
+        if copies:
+            copies(chunk).wait()
+        for i in range(0, CHUNK, many):
+            at = pl.multiple_of(chunk * CHUNK + i, many)
+            block = tiles[pl.ds(at, many)].reshape(many * TILE, TILE)
+            wide = dot(sources[pl.ds(at, many), :], block, 1, 1)
+            total = wide[:, 0:TILE]
+            for j in range(1, many):
+                total = jnp.where(row == j, wide[:, j * TILE : (j + 1) * TILE], total)
+            products[pl.ds(at, many), :] = total
         return carry
 
-    lax.fori_loop(0, SLOTS // many, step, 0, unroll=4)
+    lax.fori_loop(0, SLOTS // CHUNK, step, 0, unroll=1 if copies else 2)
 
 
 def times_tiles(sources, tiles, products):
     many = 16
+    row = iota((many, TILE), 0)
 
     def step(i, carry):
         at = pl.multiple_of(i * many, many)
         block = tiles[pl.ds(at, many)].reshape(many * TILE, TILE)
         mine = sources[pl.ds(at, many), :]
-        row = iota((many, TILE), 0)
         parts = [jnp.where(row == j, mine, jnp.zeros_like(mine)) for j in range(many)]
         products[pl.ds(at, many), :] = dot(jnp.concatenate(parts, axis=1), block)
         return carry
 
-    lax.fori_loop(0, SLOTS // many, step, 0, unroll=4)
+    lax.fori_loop(0, SLOTS // many, step, 0, unroll=8)
 
 
 def summed_by_row(row_row, products, out):
@@ -190,8 +228,14 @@
 
 
 def rows_product_first(
-    row_total, arrived, pos_col, row_row, tiles, out, norm, grams, sources, products
+    row_total, arrived, pos_col, row_row, tiles, out, norm, grams, kept, sources, products, sems
 ):
+    def copy(chunk):
+        part = pl.ds(pl.multiple_of(chunk * CHUNK, CHUNK), CHUNK)
+        return pltpu.make_async_copy(tiles.at[part], kept.at[part], sems.at[chunk])
+
+    for chunk in range(SLOTS // CHUNK):
+        copy(chunk).start()
     total = jnp.sum(arrived[:, PEER_TILES, 0, :], axis=0, keepdims=True)
     size = jnp.sqrt(total / row_total + 1e-06)
     norm[...] = size
@@ -203,7 +247,7 @@
         hot = one_hot(iota((SLOTS, DEV), 1) * PEER_TILES + k == pos_col[...])
         values = values + dot(hot, vector)
     sources[...] = values.astype(BF16)
-    tiles_times(sources, tiles, products)
+    tiles_times(sources, kept, products, copy)
     summed_by_row(row_row, products, out)
 
 
@@ -297,19 +341,25 @@
 
 
 VMEM = pl.BlockSpec(memory_space=pltpu.VMEM)
+HBM = pl.BlockSpec(memory_space=pltpu.HBM)
 SMEM = pl.BlockSpec(memory_space=pltpu.SMEM)
 
 
-def call(body, outs, args, scratch=(), in_specs=None, out_specs=None, mib=24):
+def in_hbm(value):
+    return pltpu.with_memory_space_constraint(value, pltpu.HBM)
+
+
+def call(body, outs, args, scratch=(), in_specs=None, out_specs=None, semaphores=0):
     shapes = [jax.ShapeDtypeStruct(s, d) for s, d in outs]
     return pl.pallas_call(
         body,
         out_shape=shapes,
         in_specs=in_specs or [VMEM] * len(args),
         out_specs=out_specs or [VMEM] * len(outs),
-        scratch_shapes=[pltpu.VMEM(s, d) for s, d in scratch],
-        compiler_params=pltpu.CompilerParams(vmem_limit_bytes=mib << 20),
-    )(*args)
+        scratch_shapes=[pltpu.VMEM(s, d) for s, d in scratch]
+        + [pltpu.SemaphoreType.DMA((semaphores,))] * (semaphores > 0),
+        compiler_params=pltpu.CompilerParams(vmem_limit_bytes=8 << 20),
+    )(*(in_hbm(a) if spec is HBM else a for a, spec in zip(args, in_specs or args)))
 
 
 def to_all(value):
@@ -333,27 +383,40 @@
     work = [((SLOTS, TILE), BF16), ((SLOTS, TILE), F32)]
     right, left = right_basis, left_basis
     begin = start.reshape(OWN, TILE)
-    col_row, col_col = col_tiles.reshape(1, SLOTS), col_tiles.reshape(SLOTS, 1)
-    row_row, row_col = row_tiles.reshape(1, SLOTS), row_tiles.reshape(SLOTS, 1)
-
-    (pay,) = call(first_sums, [sums], (col_row, right, begin), [square])
+    col_row, row_row = col_tiles.reshape(1, SLOTS), row_tiles.reshape(1, SLOTS)
+
+    (pay,) = call(
+        first_sums,
+        [sums],
+        (col_row, right, begin),
+        [square, ((1, SLOTS), I32), (right.shape, F32), own],
+        in_specs=[HBM] * 3,
+        semaphores=2 + PARTS,
+    )
     arrived = to_all(pay)
-    pos_row, pos_col, gram_r, gram_l = call(
+    pos_row, pos_col, row_row, row_col, gram_r, gram_l = call(
         tables,
-        [((1, SLOTS), I32), ((SLOTS, 1), I32), square, square],
-        (counts, col_row, col_col, right, left),
-        in_specs=[SMEM] + [VMEM] * 4,
+        [((1, SLOTS), I32), ((SLOTS, 1), I32)] * 2 + [square, square],
+        (counts, col_row, row_row, right, left),
+        [((1, SLOTS), I32), (right.shape, F32), (left.shape, F32)],
+        in_specs=[SMEM] + [HBM] * 4,
+        semaphores=4,
     )
     rest, send, place_row = call(
         with_total(first_vector),
         [own, ((DEV, EXTRA, 1, TILE), F32), ((1, NAMED), I32)],
         (arrived, begin, right, gram_r, gram_l),
-    )
-    partial, beta_zero, grams = call(
+        [own, (right.shape, F32)],
+        in_specs=[VMEM, HBM, HBM, VMEM, VMEM],
+        semaphores=2,
+    )
+    partial, beta_zero, grams, tiles = call(
         with_total(rows_product_first),
-        [in_rows, line, ((2, TILE), F32)],
+        [in_rows, line, ((2, TILE), F32), (tiles.shape, BF16)],
         (to_all(send), pos_col, row_row, tiles),
         work,
+        in_specs=[VMEM] * 3 + [HBM],
+        semaphores=SLOTS // CHUNK,
     )
     image, pay = call(
         image_sums_first,

time: 244 us -> 217 us (0.89)
  local copies, waits for them, and re-layouts: 33.8 us -> 0.01 us
  blocking collectives: 155 us -> 164 us
  Pallas kernels: 31.5 us -> 38 us
  waiting for transfers between devices: 5.89 us -> 1.65 us
  starting transfers between devices: 15.7 us -> 11.5 us
    unnamed x66 -> x4, local copies, waits for them, and re-layouts: 32.2 us -> 0.01 us
    all_to_all x3 -> x4, blocking collectives: 26.1 us -> 34.1 us  [in_group(): return lax.all_to_all(value, COL, 0, 0, tiled=True)]
    pallas_call x15, Pallas kernels: 31.5 us -> 38 us  [call(): pl.pallas_call(body, out_shape=shapes, in_specs=in_specs or [VMEM] * len(...]
    all_to_all x1 -> x0, starting transfers between devices: 4.18 us -> none  [in_group(): return lax.all_to_all(value, COL, 0, 0, tiled=True)]
    all_to_all x1 -> x0, waiting for transfers between devices: 3.32 us -> none  [in_group(): return lax.all_to_all(value, COL, 0, 0, tiled=True)]
  transfers between devices with their start and end apart: 2 -> 1, of which waited for: 2 -> 1; matrix products, arithmetic and copies ran while one was open for 1% -> 0% of each run, Pallas kernels for 1% -> 3%
where the time goes in v1:
time: 217 us
  blocking collectives  164 us (76%)
  Pallas kernels  38 us (18%)
  starting transfers between devices  11.5 us (5%)
    all_to_all x8, blocking collectives, to_all(): return lax.all_to_all(value, ALL, 0, 0, tiled=True)  130 us
    pallas_call x15, Pallas kernels, call(): pl.pallas_call(body, out_shape=shapes, in_specs=in_specs or [VMEM] * len(...  38 us
    all_to_all x4, blocking collectives, in_group(): return lax.all_to_all(value, COL, 0, 0, tiled=True)  34.1 us
    all_to_all x1, starting transfers between devices, to_all(): return lax.all_to_all(value, ALL, 0, 0, tiled=True)  11.5 us
  transfers between devices with their start and end apart: 1, of which 1 were waited for; matrix products, arithmetic and copies ran while one was open for 0% of the time, Pallas kernels for 3%

profile of v1, /device:TPU:1, one launch (start us, length us, event | category | flops | bytes accessed | tf_op | source)
XLA Modules:
  0.0 216.6 jit_solution(10657836119743164466)
XLA Ops:
  0.6 0.0 copy-start.1
  0.6 2.6 %shard_map.94 = f32[128,1,128]{2,1,0:T(1,128)} custom-call(s32[1,512]{1,0:T(1,128)} %bitcast.5, f32[100,4096]{1,0:T(8,128)} %basis.15, f32[32,128]{1,0:T(8,128)} %bitcast.3), custom_call_target="tpu_custom_call" | custom-call | tf_op jit(solution)/shard_map/pallas_call | solution.py:354
  3.2 11.5 %all-to-all-start = ((f32[128,1,128]{2,1,0:T(1,128)}), f32[128,1,128]{2,1,0:T(1,128)S(1)}, u32[]{:S(2)}, u32[]{:S(2)}) async-start(f32[128,1,128]{2,1,0:T(1,128)} %shard_map.94), calls=%async_computation | async-start | bytes 131072 | tf_op jit(solution)/shard_map/all_to_all | solution.py:366
  15.4 7.1 %shard_map.95 = (s32[1,512]{1,0:T(1,128)S(1)}, s32[512,1]{1,0:T(8,128)S(1)}, s32[1,512]{1,0:T(1,128)S(1)}, s32[512,1]{1,0:T(8,128)S(1)}, f32[128,128]{1,0:T(8,128)S(1)}, /*index=5*/f32[128,128]{1,0:T(8,128)S(1)}) custom-call(s32[1]{0:T(128)S(6)} %copy.10.counts, s32[1,512]{1,0:T(1,128)} %bitcast.6, s32[1,512]{1,0:T(1,128)} %bitcast.7, f32[100,4096]{1,0:T(8,128)} %basis.15, ...), custom_call_target="tpu_custom_call" | custom-call | tf_op jit(solution)/shard_map/pallas_call | solution.py:354
  22.4 1.6 all-to-all-done.arrived
  24.1 2.4 %shard_map.96 = (f32[32,128]{1,0:T(8,128)S(1)}, f32[128,11,1,128]{3,2,1,0:T(1,128)S(1)}, s32[1,1024]{1,0:T(1,128)S(1)}) custom-call(f32[128,1,128]{2,1,0:T(1,128)S(1)} %all-to-all-done.arrived, f32[32,128]{1,0:T(8,128)} %bitcast.4, f32[100,4096]{1,0:T(8,128)} %basis.15, f32[128,128]{1,0:T(8,128)S(1)} %get-tuple-element.37.gram_r, ...), custom_call_target="tpu_custom_call" | custom-call | tf_op jit(solution)/shard_map/pallas_call | solution.py:354
  26.5 23.7 %all_to_all.65.arrived = f32[128,11,1,128]{3,2,1,0:T(1,128)S(1)} all-to-all(f32[128,11,1,128]{3,2,1,0:T(1,128)S(1)} %get-tuple-element.39), channel_id=1, replica_groups=mesh['row_0'=4,'row_1'=4,'col_0'=4,'col_1'=2] {'row_0','row_1','col_0','..., dimensions={0} | all-to-all | bytes 1441792 | tf_op jit(solution)/shard_map/all_to_all | solution.py:366
  50.2 7.5 %shard_map.97 = (f32[8,32,128]{2,1,0:T(8,128)S(1)}, f32[1,128]{1,0:T(1,128)S(1)}, f32[2,128]{1,0:T(2,128)S(1)}, bf16[512,128,128]{2,1,0:T(8,128)(2,1)S(1)}) custom-call(f32[128,11,1,128]{3,2,1,0:T(1,128)S(1)} %all_to_all.65.arrived, s32[512,1]{1,0:T(8,128)S(1)} %get-tuple-element.40.pos_col, s32[1,512]{1,0:T(1,128)S(1)} %get-tuple-element.41.row_row, ...), custom_call_target="tpu_custom_call" | custom-call | tf_op jit(solution)/shard_map/pallas_call | solution.py:354
  57.6 8.8 %all_to_all.66.arrived = f32[8,32,128]{2,1,0:T(8,128)S(1)} all-to-all(f32[8,32,128]{2,1,0:T(8,128)S(1)} %get-tuple-element.42), channel_id=1, replica_groups=mesh['row_0'=4,'row_1'=4,'col_0'=4,'col_1'=2] {'col_0','col_1'}, dimensions={0} | all-to-all | bytes 262144 | tf_op jit(solution)/shard_map/all_to_all | solution.py:370
  66.5 0.0 copy-done.1
  66.5 0.4 shard_map.98
  66.9 14.3 %all_to_all.67.arrived = f32[128,1,384]{2,1,0:T(1,128)S(1)} all-to-all(f32[128,1,384]{2,1,0:T(1,128)S(1)} %get-tuple-element.44), channel_id=1, replica_groups=mesh['row_0'=4,'row_1'=4,'col_0'=4,'col_1'=2] {'row_0','row_1','col_0','..., dimensions={0} | all-to-all | bytes 393216 | tf_op jit(solution)/shard_map/all_to_all | solution.py:366
  81.2 0.3 shard_map.99
  81.5 8.2 %all_to_all.68.arrived = bf16[8,32,128]{2,1,0:T(8,128)(2,1)S(1)} all-to-all(bf16[8,32,128]{2,1,0:T(8,128)(2,1)S(1)} %get-tuple-element.46), channel_id=1, replica_groups=mesh['row_0'=4,'row_1'=4,'col_0'=4,'col_1'=2] {'col_0','col_1'}, dimensions={0} | all-to-all | bytes 131072 | tf_op jit(solution)/shard_map/all_to_all | solution.py:370
  89.7 3.9 %shard_map.100 = f32[128,8,128]{2,1,0:T(8,128)S(1)} custom-call(bf16[8,32,128]{2,1,0:T(8,128)(2,1)S(1)} %all_to_all.68.arrived, s32[512,1]{1,0:T(8,128)S(1)} %get-tuple-element.47.row_col, s32[1,512]{1,0:T(1,128)S(1)} %get-tuple-element.48.pos_row, bf16[512,128,128]{2,1,0:T(8,128)(2,1)S(1)} %get-tuple-element.49.tiles), custom_call_target="tpu_custom_call" | custom-call | tf_op jit(solution)/shard_map/pallas_call | solution.py:354
  93.6 17.7 %all_to_all.69.arrived = f32[128,8,128]{2,1,0:T(8,128)S(1)} all-to-all(f32[128,8,128]{2,1,0:T(8,128)S(1)} %shard_map.100), channel_id=1, replica_groups=mesh['row_0'=4,'row_1'=4,'col_0'=4,'col_1'=2] {'row_0','row_1','col_0','..., dimensions={0} | all-to-all | bytes 1048576 | tf_op jit(solution)/shard_map/all_to_all | solution.py:366
  111.3 0.0 copy-done
  111.3 0.7 shard_map.101
  111.9 13.8 %all_to_all.70.arrived = f32[128,1,128]{2,1,0:T(1,128)S(1)} all-to-all(f32[128,1,128]{2,1,0:T(1,128)S(1)} %get-tuple-element.54), channel_id=1, replica_groups=mesh['row_0'=4,'row_1'=4,'col_0'=4,'col_1'=2] {'row_0','row_1','col_0','..., dimensions={0} | all-to-all | bytes 131072 | tf_op jit(solution)/shard_map/all_to_all | solution.py:366
  125.7 0.5 shard_map.102
  126.2 15.5 %all_to_all.71.arrived = bf16[128,8,128]{2,1,0:T(8,128)(2,1)S(1)} all-to-all(bf16[128,8,128]{2,1,0:T(8,128)(2,1)S(1)} %get-tuple-element.57), channel_id=1, replica_groups=mesh['row_0'=4,'row_1'=4,'col_0'=4,'col_1'=2] {'row_0','row_1','col_0','..., dimensions={0} | all-to-all | bytes 524288 | tf_op jit(solution)/shard_map/all_to_all | solution.py:366
  141.7 5.8 %shard_map.103 = f32[8,32,128]{2,1,0:T(8,128)S(1)} custom-call(bf16[128,8,128]{2,1,0:T(8,128)(2,1)S(1)} %all_to_all.71.arrived, s32[512,1]{1,0:T(8,128)S(1)} %get-tuple-element.40.pos_col, s32[1,512]{1,0:T(1,128)S(1)} %get-tuple-element.41.row_row, bf16[512,128,128]{2,1,0:T(8,128)(2,1)S(1)} %get-tuple-element.49.tiles), custom_call_target="tpu_custom_call" | custom-call | tf_op jit(solution)/shard_map/pallas_call | solution.py:354
  147.5 8.7 %all_to_all.72.arrived = f32[8,32,128]{2,1,0:T(8,128)S(1)} all-to-all(f32[8,32,128]{2,1,0:T(8,128)S(1)} %shard_map.103), channel_id=1, replica_groups=mesh['row_0'=4,'row_1'=4,'col_0'=4,'col_1'=2] {'col_0','col_1'}, dimensions={0} | all-to-all | bytes 262144 | tf_op jit(solution)/shard_map/all_to_all | solution.py:370
  156.3 0.4 shard_map.104
  156.7 13.4 %all_to_all.73.arrived = f32[128,1,128]{2,1,0:T(1,128)S(1)} all-to-all(f32[128,1,128]{2,1,0:T(1,128)S(1)} %get-tuple-element.60), channel_id=1, replica_groups=mesh['row_0'=4,'row_1'=4,'col_0'=4,'col_1'=2] {'row_0','row_1','col_0','..., dimensions={0} | all-to-all | bytes 131072 | tf_op jit(solution)/shard_map/all_to_all | solution.py:366
  170.1 0.9 shard_map.105
  171.0 8.4 %all_to_all.74.arrived = bf16[8,32,128]{2,1,0:T(8,128)(2,1)S(1)} all-to-all(bf16[8,32,128]{2,1,0:T(8,128)(2,1)S(1)} %get-tuple-element.64), channel_id=1, replica_groups=mesh['row_0'=4,'row_1'=4,'col_0'=4,'col_1'=2] {'col_0','col_1'}, dimensions={0} | all-to-all | bytes 131072 | tf_op jit(solution)/shard_map/all_to_all | solution.py:370
  179.5 3.9 %shard_map.106 = f32[128,8,128]{2,1,0:T(8,128)S(1)} custom-call(bf16[8,32,128]{2,1,0:T(8,128)(2,1)S(1)} %all_to_all.74.arrived, s32[512,1]{1,0:T(8,128)S(1)} %get-tuple-element.47.row_col, s32[1,512]{1,0:T(1,128)S(1)} %get-tuple-element.48.pos_row, bf16[512,128,128]{2,1,0:T(8,128)(2,1)S(1)} %get-tuple-element.49.tiles), custom_call_target="tpu_custom_call" | custom-call | tf_op jit(solution)/shard_map/pallas_call | solution.py:354
  183.4 17.7 %all_to_all.75.arrived = f32[128,8,128]{2,1,0:T(8,128)S(1)} all-to-all(f32[128,8,128]{2,1,0:T(8,128)S(1)} %shard_map.106), channel_id=1, replica_groups=mesh['row_0'=4,'row_1'=4,'col_0'=4,'col_1'=2] {'row_0','row_1','col_0','..., dimensions={0} | all-to-all | bytes 1048576 | tf_op jit(solution)/shard_map/all_to_all | solution.py:366
  201.1 0.7 shard_map.107
  201.7 13.8 %all_to_all.76.arrived = f32[128,1,128]{2,1,0:T(1,128)S(1)} all-to-all(f32[128,1,128]{2,1,0:T(1,128)S(1)} %get-tuple-element.67), channel_id=1, replica_groups=mesh['row_0'=4,'row_1'=4,'col_0'=4,'col_1'=2] {'row_0','row_1','col_0','..., dimensions={0} | all-to-all | bytes 131072 | tf_op jit(solution)/shard_map/all_to_all | solution.py:366
  215.5 1.0 shard_map.108
  (1 shorter events, 0.0 us)
Async XLA Ops:
  0.6 65.8 %copy-start.1 = (f32[100,4096]{1,0:T(8,128)S(1)}, f32[100,4096]{1,0:T(8,128)}, u32[]{:S(2)}) copy-start(f32[100,4096]{1,0:T(8,128)} %basis.13) | copy-start | bytes 4915204
  3.2 20.9 %all-to-all-start = ((f32[128,1,128]{2,1,0:T(1,128)}), f32[128,1,128]{2,1,0:T(1,128)S(1)}, u32[]{:S(2)}, u32[]{:S(2)}) async-start(f32[128,1,128]{2,1,0:T(1,128)} %shard_map.94), calls=%async_computation | async-start | bytes 131072 | tf_op jit(solution)/shard_map/all_to_all | solution.py:366
  50.2 61.1 %copy-start = (f32[100,4096]{1,0:T(8,128)S(1)}, f32[100,4096]{1,0:T(8,128)}, u32[]{:S(2)}) copy-start(f32[100,4096]{1,0:T(8,128)} %basis.15) | copy-start | bytes 4915204

commit v2 on v1

--- a/solution.py
+++ b/solution.py
@@ -88,7 +88,7 @@
     return jnp.sqrt(left / row_total + 1e-06)
 
 
-def first_sums(col_hbm, basis_hbm, start_hbm, out, held, col_row, basis, start, sems):
+def first_sums(col_hbm, basis_hbm, start_hbm, out, rank, col_row, start, basis, held, sems):
     wide = basis.shape[1] // PARTS
     parts = [pl.ds(i * wide, wide) for i in range(PARTS)]
     copies = [pltpu.make_async_copy(col_hbm, col_row, sems.at[0])]
@@ -105,50 +105,58 @@
     places = one_hot(iota((OWN, SLOTS), 0) == place)
     touched = dot(places, owners, 1, 1) > 0.5
     below = one_hot(iota((OWN, OWN), 1) < iota((OWN, OWN), 0))
-    rank = dot(below, one_hot(touched))
+    places = dot(below, one_hot(touched))
+    rank[...] = places.astype(BF16)
     copies[1].wait()
     row = products_row(basis, start[...], held, copies[2:])
     held[...] = jnp.zeros_like(held)
     number = (iota((OWN, DEV), 0) + 1).astype(F32)
     for k in range(PEER_TILES):
-        here = touched & (rank > k - 0.5) & (rank < k + 0.5)
+        here = touched & (places > k - 0.5) & (places < k + 0.5)
         named = jnp.sum(jnp.where(here, number, 0.0), axis=0, keepdims=True)
         held[PLACE + k : PLACE + k + 1, :] = named - 1.0
     out[:, 0, :] = held[...].T + row
 
 
-def as_column(row):
-    return jnp.broadcast_to(row.astype(F32), (TILE, SLOTS)).T[:, 0:1].astype(I32)
-
-
-def tables(counts, col_hbm, row_hbm, right_hbm, left_hbm, *refs):
-    pos_row, pos_col, row_row, row_col, gram_r, gram_l, col_row, right, left, sems = refs
-    sources = (col_hbm, row_hbm, right_hbm, left_hbm)
-    targets = (col_row, row_row, right, left)
-    copies = [pltpu.make_async_copy(a, b, sems.at[i]) for i, (a, b) in enumerate(zip(sources, targets))]
+def gram_of(basis):
+    value = basis[...]
+    first = value.astype(BF16)
+    rest = value - first.astype(F32)
+    second = rest.astype(BF16)
+    third = (rest - second.astype(F32)).astype(BF16)
+    low = dot(third, first, 1, 1)
+    middle = dot(second, first, 1, 1)
+    both = low + middle
+    return dot(second, second, 1, 1) + (both + both.T) + dot(first, first, 1, 1)
+
+
+def tables(counts, rank, col_row, right, row_hbm, left_hbm, *refs):
+    pos_row, pos_col, row_row, row_col, gram_r, gram_l, left, sems = refs
+    copies = [
+        pltpu.make_async_copy(left_hbm, left, sems.at[0]),
+        pltpu.make_async_copy(row_hbm, row_row, sems.at[1]),
+    ]
     for copy in copies:
         copy.start()
+    for basis, gram in ((right, gram_r), (left, gram_l)):
+        if basis is left:
+            copies[0].wait()
+        size = basis.shape[0]
+        gram[...] = jnp.zeros_like(gram)
+        gram[0:size, 0:size] = gram_of(basis)
+    copies[1].wait()
     count = counts[0]
-    copies[0].wait()
     owner, place = col_row[...] // OWN, col_row[...] % OWN
     owners = one_hot(iota((DEV, SLOTS), 0) == owner)
-    in_place = iota((OWN, SLOTS), 0) == place
-    touched = one_hot(dot(one_hot(in_place), owners, 1, 1) > 0.5)
-    below = one_hot(iota((OWN, OWN), 1) < iota((OWN, OWN), 0))
-    rank = dot(below, touched).astype(BF16)
-    mine = dot(rank, owners)
-    mine = jnp.sum(jnp.where(in_place, mine, 0.0), axis=0, keepdims=True)
-    position = owner * PEER_TILES + mine.astype(I32)
+    mine = dot(rank[...], owners)
+    mine = jnp.where(iota((OWN, SLOTS), 0) == place, mine, 0.0)
+    position = owner * PEER_TILES + jnp.sum(mine, axis=0, keepdims=True).astype(I32)
     position = jnp.where(iota((1, SLOTS), 1) < count, position, -1)
     pos_row[...] = position
-    pos_col[...] = as_column(position)
-    copies[1].wait()
-    row_col[...] = as_column(row_row[...])
-    for copy, basis, gram in ((copies[2], right, gram_r), (copies[3], left, gram_l)):
-        copy.wait()
-        size = basis.shape[0]
-        gram[...] = jnp.zeros_like(gram)
-        gram[0:size, 0:size] = dot(basis[...], basis[...], 1, 1, HIGH)
+    both = jnp.where(iota((8, SLOTS), 0) == 0, position, row_row[...])
+    columns = both.astype(F32).T.astype(I32)
+    pos_col[...] = columns[:, 0:1]
+    row_col[...] = columns[:, 1:2]
 
 
 def place_row_of(arrived):
@@ -159,22 +167,13 @@
     return jnp.round(row).astype(I32)
 
 
-def first_vector(row_total, arrived, start_hbm, basis_hbm, gram_r, gram_l, *refs):
-    rest, send, place_row, start, basis, sems = refs
-    copies = [
-        pltpu.make_async_copy(start_hbm, start, sems.at[0]),
-        pltpu.make_async_copy(basis_hbm, basis, sems.at[1]),
-    ]
-    for copy in copies:
-        copy.start()
+def first_vector(row_total, arrived, start, basis, gram_r, gram_l, rest, send, place_row):
     size = basis.shape[0]
     got = arrived[:, 0, :]
     total = jnp.sum(got, axis=0, keepdims=True)
     _, _, _, column = coefficients_of(total, size, row_total)
     named = place_row_of(got)
     place_row[...] = named
-    for copy in copies:
-        copy.wait()
     subtract_basis(rest, start, basis, column)
     vector = rest[...]
     hot = jnp.where(iota((OWN, NAMED), 0) == named, 1.0, 0.0)
@@ -385,11 +384,11 @@
     begin = start.reshape(OWN, TILE)
     col_row, row_row = col_tiles.reshape(1, SLOTS), row_tiles.reshape(1, SLOTS)
 
-    (pay,) = call(
+    pay, rank, col_row, begin, right = call(
         first_sums,
-        [sums],
+        [sums, ((OWN, DEV), BF16), ((1, SLOTS), I32), own, (right.shape, F32)],
         (col_row, right, begin),
-        [square, ((1, SLOTS), I32), (right.shape, F32), own],
+        [square],
         in_specs=[HBM] * 3,
         semaphores=2 + PARTS,
     )
@@ -397,18 +396,15 @@
     pos_row, pos_col, row_row, row_col, gram_r, gram_l = call(
         tables,
         [((1, SLOTS), I32), ((SLOTS, 1), I32)] * 2 + [square, square],
-        (counts, col_row, row_row, right, left),
-        [((1, SLOTS), I32), (right.shape, F32), (left.shape, F32)],
-        in_specs=[SMEM] + [HBM] * 4,
-        semaphores=4,
+        (counts, rank, col_row, right, row_row, left),
+        [(left.shape, F32)],
+        in_specs=[SMEM] + [VMEM] * 3 + [HBM] * 2,
+        semaphores=2,
     )
     rest, send, place_row = call(
         with_total(first_vector),
         [own, ((DEV, EXTRA, 1, TILE), F32), ((1, NAMED), I32)],
         (arrived, begin, right, gram_r, gram_l),
-        [own, (right.shape, F32)],
-        in_specs=[VMEM, HBM, HBM, VMEM, VMEM],
-        semaphores=2,
     )
     partial, beta_zero, grams, tiles = call(
         with_total(rows_product_first),

time: 217 us -> 212 us (0.977)
  Pallas kernels: 38 us -> 32.5 us
  waiting for transfers between devices: 1.65 us -> 5.63 us
  blocking collectives: 164 us -> 161 us
    pallas_call x15, Pallas kernels: 38 us -> 32.5 us  [call(): pl.pallas_call(body, out_shape=shapes, in_specs=in_specs or [VMEM] * len(...]
    all_to_all x1, waiting for transfers between devices: 1.65 us -> 5.63 us  [to_all(): return lax.all_to_all(value, ALL, 0, 0, tiled=True)]
    all_to_all x8, blocking collectives: 130 us -> 126 us  [to_all(): return lax.all_to_all(value, ALL, 0, 0, tiled=True)]
  transfers between devices with their start and end apart: 1 -> 1, of which waited for: 1 -> 1; matrix products, arithmetic and copies ran while one was open for 0% -> 0% of each run, Pallas kernels for 3% -> 1%
where the time goes in v2:
time: 212 us
  blocking collectives  161 us (76%)
  Pallas kernels  32.5 us (15%)
  starting transfers between devices  11.5 us (5%)
  waiting for transfers between devices  5.63 us (3%)
    all_to_all x8, blocking collectives, to_all(): return lax.all_to_all(value, ALL, 0, 0, tiled=True)  126 us
    all_to_all x4, blocking collectives, in_group(): return lax.all_to_all(value, COL, 0, 0, tiled=True)  34.1 us
    pallas_call x15, Pallas kernels, call(): pl.pallas_call(body, out_shape=shapes, in_specs=in_specs or [VMEM] * len(...  32.5 us
    all_to_all x1, starting transfers between devices, to_all(): return lax.all_to_all(value, ALL, 0, 0, tiled=True)  11.5 us
    all_to_all x1, waiting for transfers between devices, to_all(): return lax.all_to_all(value, ALL, 0, 0, tiled=True)  5.63 us
  transfers between devices with their start and end apart: 1, of which 1 were waited for; matrix products, arithmetic and copies ran while one was open for 0% of the time, Pallas kernels for 1%

profile of v2, /device:TPU:1, one launch (start us, length us, event | category | flops | bytes accessed | tf_op | source)
XLA Modules:
  0.0 211.7 jit_solution(3420293442248037790)
XLA Ops:
  0.6 2.4 %shard_map.94 = (f32[128,1,128]{2,1,0:T(1,128)}, bf16[32,128]{1,0:T(8,128)(2,1)S(1)}, s32[1,512]{1,0:T(1,128)S(1)}, f32[32,128]{1,0:T(8,128)S(1)}, f32[100,4096]{1,0:T(8,128)S(1)}) custom-call(s32[1,512]{1,0:T(1,128)} %bitcast.4, f32[100,4096]{1,0:T(8,128)} %basis_hbm.1, f32[32,128]{1,0:T(8,128)} %bitcast.3), custom_call_target="tpu_custom_call" | custom-call | tf_op jit(solution)/shard_map/pallas_call | solution.py:353
  3.1 11.5 %all-to-all-start = ((f32[128,1,128]{2,1,0:T(1,128)}), f32[128,1,128]{2,1,0:T(1,128)S(1)}, u32[]{:S(2)}, u32[]{:S(2)}) async-start(f32[128,1,128]{2,1,0:T(1,128)} %get-tuple-element.42), calls=%async_computation | async-start | bytes 131072 | tf_op jit(solution)/shard_map/all_to_all | solution.py:365
  15.2 3.1 %shard_map.95 = (s32[1,512]{1,0:T(1,128)S(1)}, s32[512,1]{1,0:T(8,128)S(1)}, s32[1,512]{1,0:T(1,128)S(1)}, s32[512,1]{1,0:T(8,128)S(1)}, f32[128,128]{1,0:T(8,128)S(1)}, /*index=5*/f32[128,128]{1,0:T(8,128)S(1)}) custom-call(s32[1]{0:T(128)S(6)} %copy.10.counts, bf16[32,128]{1,0:T(8,128)(2,1)S(1)} %get-tuple-element.45.rank, ...), custom_call_target="tpu_custom_call" | custom-call | tf_op jit(solution)/shard_map/pallas_call | solution.py:353
  18.3 5.6 %all-to-all-done.arrived = f32[128,1,128]{2,1,0:T(1,128)S(1)} async-done(((f32[128,1,128]{2,1,0:T(1,128)}), f32[128,1,128]{2,1,0:T(1,128)S(1)}, u32[]{:S(2)}, u32[]{:S(2)}) %all-to-all-start) | async-done | bytes 65568 | tf_op jit(solution)/shard_map/all_to_all | solution.py:365
  23.9 1.0 shard_map.96
  24.9 20.3 %all_to_all.65.arrived = f32[128,11,1,128]{3,2,1,0:T(1,128)S(1)} all-to-all(f32[128,11,1,128]{3,2,1,0:T(1,128)S(1)} %get-tuple-element.49), channel_id=1, replica_groups=mesh['row_0'=4,'row_1'=4,'col_0'=4,'col_1'=2] {'row_0','row_1','col_0','..., dimensions={0} | all-to-all | bytes 1441792 | tf_op jit(solution)/shard_map/all_to_all | solution.py:365
  45.3 0.0 copy-start
  45.3 7.5 %shard_map.97 = (f32[8,32,128]{2,1,0:T(8,128)S(1)}, f32[1,128]{1,0:T(1,128)S(1)}, f32[2,128]{1,0:T(2,128)S(1)}, bf16[512,128,128]{2,1,0:T(8,128)(2,1)S(1)}) custom-call(f32[128,11,1,128]{3,2,1,0:T(1,128)S(1)} %all_to_all.65.arrived, s32[512,1]{1,0:T(8,128)S(1)} %get-tuple-element.50.pos_col, s32[1,512]{1,0:T(1,128)S(1)} %get-tuple-element.51.row_row, ...), custom_call_target="tpu_custom_call" | custom-call | tf_op jit(solution)/shard_map/pallas_call | solution.py:353
  52.8 8.8 %all_to_all.66.arrived = f32[8,32,128]{2,1,0:T(8,128)S(1)} all-to-all(f32[8,32,128]{2,1,0:T(8,128)S(1)} %get-tuple-element.52), channel_id=1, replica_groups=mesh['row_0'=4,'row_1'=4,'col_0'=4,'col_1'=2] {'col_0','col_1'}, dimensions={0} | all-to-all | bytes 262144 | tf_op jit(solution)/shard_map/all_to_all | solution.py:369
  61.6 0.0 copy-done
  61.6 0.4 shard_map.98
  62.0 14.3 %all_to_all.67.arrived = f32[128,1,384]{2,1,0:T(1,128)S(1)} all-to-all(f32[128,1,384]{2,1,0:T(1,128)S(1)} %get-tuple-element.54), channel_id=1, replica_groups=mesh['row_0'=4,'row_1'=4,'col_0'=4,'col_1'=2] {'row_0','row_1','col_0','..., dimensions={0} | all-to-all | bytes 393216 | tf_op jit(solution)/shard_map/all_to_all | solution.py:365
  76.3 0.3 shard_map.99
  76.6 8.2 %all_to_all.68.arrived = bf16[8,32,128]{2,1,0:T(8,128)(2,1)S(1)} all-to-all(bf16[8,32,128]{2,1,0:T(8,128)(2,1)S(1)} %get-tuple-element.56), channel_id=1, replica_groups=mesh['row_0'=4,'row_1'=4,'col_0'=4,'col_1'=2] {'col_0','col_1'}, dimensions={0} | all-to-all | bytes 131072 | tf_op jit(solution)/shard_map/all_to_all | solution.py:369
  84.8 3.9 %shard_map.100 = f32[128,8,128]{2,1,0:T(8,128)S(1)} custom-call(bf16[8,32,128]{2,1,0:T(8,128)(2,1)S(1)} %all_to_all.68.arrived, s32[512,1]{1,0:T(8,128)S(1)} %get-tuple-element.57.row_col, s32[1,512]{1,0:T(1,128)S(1)} %get-tuple-element.58.pos_row, bf16[512,128,128]{2,1,0:T(8,128)(2,1)S(1)} %get-tuple-element.59.tiles), custom_call_target="tpu_custom_call" | custom-call | tf_op jit(solution)/shard_map/pallas_call | solution.py:353
  88.7 17.7 %all_to_all.69.arrived = f32[128,8,128]{2,1,0:T(8,128)S(1)} all-to-all(f32[128,8,128]{2,1,0:T(8,128)S(1)} %shard_map.100), channel_id=1, replica_groups=mesh['row_0'=4,'row_1'=4,'col_0'=4,'col_1'=2] {'row_0','row_1','col_0','..., dimensions={0} | all-to-all | bytes 1048576 | tf_op jit(solution)/shard_map/all_to_all | solution.py:365
  106.4 0.6 shard_map.101
  107.0 13.8 %all_to_all.70.arrived = f32[128,1,128]{2,1,0:T(1,128)S(1)} all-to-all(f32[128,1,128]{2,1,0:T(1,128)S(1)} %get-tuple-element.64), channel_id=1, replica_groups=mesh['row_0'=4,'row_1'=4,'col_0'=4,'col_1'=2] {'row_0','row_1','col_0','..., dimensions={0} | all-to-all | bytes 131072 | tf_op jit(solution)/shard_map/all_to_all | solution.py:365
  120.8 0.5 shard_map.102
  121.3 15.5 %all_to_all.71.arrived = bf16[128,8,128]{2,1,0:T(8,128)(2,1)S(1)} all-to-all(bf16[128,8,128]{2,1,0:T(8,128)(2,1)S(1)} %get-tuple-element.67), channel_id=1, replica_groups=mesh['row_0'=4,'row_1'=4,'col_0'=4,'col_1'=2] {'row_0','row_1','col_0','..., dimensions={0} | all-to-all | bytes 524288 | tf_op jit(solution)/shard_map/all_to_all | solution.py:365
  136.8 5.8 %shard_map.103 = f32[8,32,128]{2,1,0:T(8,128)S(1)} custom-call(bf16[128,8,128]{2,1,0:T(8,128)(2,1)S(1)} %all_to_all.71.arrived, s32[512,1]{1,0:T(8,128)S(1)} %get-tuple-element.50.pos_col, s32[1,512]{1,0:T(1,128)S(1)} %get-tuple-element.51.row_row, bf16[512,128,128]{2,1,0:T(8,128)(2,1)S(1)} %get-tuple-element.59.tiles), custom_call_target="tpu_custom_call" | custom-call | tf_op jit(solution)/shard_map/pallas_call | solution.py:353
  142.7 8.7 %all_to_all.72.arrived = f32[8,32,128]{2,1,0:T(8,128)S(1)} all-to-all(f32[8,32,128]{2,1,0:T(8,128)S(1)} %shard_map.103), channel_id=1, replica_groups=mesh['row_0'=4,'row_1'=4,'col_0'=4,'col_1'=2] {'col_0','col_1'}, dimensions={0} | all-to-all | bytes 262144 | tf_op jit(solution)/shard_map/all_to_all | solution.py:369
  151.4 0.4 shard_map.104
  151.8 13.4 %all_to_all.73.arrived = f32[128,1,128]{2,1,0:T(1,128)S(1)} all-to-all(f32[128,1,128]{2,1,0:T(1,128)S(1)} %get-tuple-element.70), channel_id=1, replica_groups=mesh['row_0'=4,'row_1'=4,'col_0'=4,'col_1'=2] {'row_0','row_1','col_0','..., dimensions={0} | all-to-all | bytes 131072 | tf_op jit(solution)/shard_map/all_to_all | solution.py:365
  165.2 1.0 shard_map.105
  166.2 8.4 %all_to_all.74.arrived = bf16[8,32,128]{2,1,0:T(8,128)(2,1)S(1)} all-to-all(bf16[8,32,128]{2,1,0:T(8,128)(2,1)S(1)} %get-tuple-element.74), channel_id=1, replica_groups=mesh['row_0'=4,'row_1'=4,'col_0'=4,'col_1'=2] {'col_0','col_1'}, dimensions={0} | all-to-all | bytes 131072 | tf_op jit(solution)/shard_map/all_to_all | solution.py:369
  174.6 3.9 %shard_map.106 = f32[128,8,128]{2,1,0:T(8,128)S(1)} custom-call(bf16[8,32,128]{2,1,0:T(8,128)(2,1)S(1)} %all_to_all.74.arrived, s32[512,1]{1,0:T(8,128)S(1)} %get-tuple-element.57.row_col, s32[1,512]{1,0:T(1,128)S(1)} %get-tuple-element.58.pos_row, bf16[512,128,128]{2,1,0:T(8,128)(2,1)S(1)} %get-tuple-element.59.tiles), custom_call_target="tpu_custom_call" | custom-call | tf_op jit(solution)/shard_map/pallas_call | solution.py:353
  178.5 17.7 %all_to_all.75.arrived = f32[128,8,128]{2,1,0:T(8,128)S(1)} all-to-all(f32[128,8,128]{2,1,0:T(8,128)S(1)} %shard_map.106), channel_id=1, replica_groups=mesh['row_0'=4,'row_1'=4,'col_0'=4,'col_1'=2] {'row_0','row_1','col_0','..., dimensions={0} | all-to-all | bytes 1048576 | tf_op jit(solution)/shard_map/all_to_all | solution.py:365
  196.2 0.6 shard_map.107
  196.8 13.8 %all_to_all.76.arrived = f32[128,1,128]{2,1,0:T(1,128)S(1)} all-to-all(f32[128,1,128]{2,1,0:T(1,128)S(1)} %get-tuple-element.77), channel_id=1, replica_groups=mesh['row_0'=4,'row_1'=4,'col_0'=4,'col_1'=2] {'row_0','row_1','col_0','..., dimensions={0} | all-to-all | bytes 131072 | tf_op jit(solution)/shard_map/all_to_all | solution.py:365
  210.6 1.0 shard_map.108
Async XLA Ops:
  3.1 20.9 %all-to-all-start = ((f32[128,1,128]{2,1,0:T(1,128)}), f32[128,1,128]{2,1,0:T(1,128)S(1)}, u32[]{:S(2)}, u32[]{:S(2)}) async-start(f32[128,1,128]{2,1,0:T(1,128)} %get-tuple-element.42), calls=%async_computation | async-start | bytes 131072 | tf_op jit(solution)/shard_map/all_to_all | solution.py:365
  45.3 16.3 %copy-start = (f32[100,4096]{1,0:T(8,128)S(1)}, f32[100,4096]{1,0:T(8,128)}, u32[]{:S(2)}) copy-start(f32[100,4096]{1,0:T(8,128)} %basis.7) | copy-start | bytes 4915204

commit v3 on v2

--- a/solution.py
+++ b/solution.py
@@ -9,8 +9,9 @@
 from jax.sharding import PartitionSpec as P
 
 PEER_TILES = 8
-COL = ("col_0", "col_1")
 ALL = ("row_0", "row_1", "col_0", "col_1")
+SEND_ALL = ("col_1", "col_0", "row_1", "row_0")
+SEND_COL = ("col_1", "col_0")
 HIGH = lax.Precision.HIGHEST
 F32, BF16, I32 = jnp.float32, jnp.bfloat16, jnp.int32
 
@@ -23,11 +24,22 @@
 PLACE = 104
 PARTS = 4
 CHUNK = 64
+AHEAD = 4
 EXTRA = PEER_TILES + 3
 
 
 def iota(shape, dim):
     return lax.broadcasted_iota(I32, shape, dim)
+
+
+def block_of(device):
+    near = (device % 2) * 64 + (device // 2 % 4) * 16
+    return near + (device // 8 % 4) * 4 + device // 32
+
+
+def group_row_of(row):
+    owner = row // OWN
+    return ((owner % 2) * 4 + owner // 2) * OWN + row % OWN
 
 
 def one_hot(condition):
@@ -100,7 +112,7 @@
     for copy in copies:
         copy.start()
     copies[0].wait()
-    owner, place = col_row[...] // OWN, col_row[...] % OWN
+    owner, place = block_of(col_row[...] // OWN), col_row[...] % OWN
     owners = one_hot(iota((DEV, SLOTS), 0) == owner)
     places = one_hot(iota((OWN, SLOTS), 0) == place)
     touched = dot(places, owners, 1, 1) > 0.5
@@ -131,10 +143,10 @@
 
 
 def tables(counts, rank, col_row, right, row_hbm, left_hbm, *refs):
-    pos_row, pos_col, row_row, row_col, gram_r, gram_l, left, sems = refs
+    pos_row, pos_col, row_row, row_col, gram_r, gram_l, left, given_row, sems = refs
     copies = [
         pltpu.make_async_copy(left_hbm, left, sems.at[0]),
-        pltpu.make_async_copy(row_hbm, row_row, sems.at[1]),
+        pltpu.make_async_copy(row_hbm, given_row, sems.at[1]),
     ]
     for copy in copies:
         copy.start()
@@ -145,15 +157,17 @@
         gram[...] = jnp.zeros_like(gram)
         gram[0:size, 0:size] = gram_of(basis)
     copies[1].wait()
+    row = group_row_of(given_row[...])
+    row_row[...] = row
     count = counts[0]
-    owner, place = col_row[...] // OWN, col_row[...] % OWN
+    owner, place = block_of(col_row[...] // OWN), col_row[...] % OWN
     owners = one_hot(iota((DEV, SLOTS), 0) == owner)
     mine = dot(rank[...], owners)
     mine = jnp.where(iota((OWN, SLOTS), 0) == place, mine, 0.0)
     position = owner * PEER_TILES + jnp.sum(mine, axis=0, keepdims=True).astype(I32)
     position = jnp.where(iota((1, SLOTS), 1) < count, position, -1)
     pos_row[...] = position
-    both = jnp.where(iota((8, SLOTS), 0) == 0, position, row_row[...])
+    both = jnp.where(iota((8, SLOTS), 0) == 0, position, row)
     columns = both.astype(F32).T.astype(I32)
     pos_col[...] = columns[:, 0:1]
     row_col[...] = columns[:, 1:2]
@@ -190,20 +204,17 @@
     many = 16
     row = iota((many, TILE), 0)
 
-    def step(chunk, carry):
-        if copies:
-            copies(chunk).wait()
-        for i in range(0, CHUNK, many):
-            at = pl.multiple_of(chunk * CHUNK + i, many)
-            block = tiles[pl.ds(at, many)].reshape(many * TILE, TILE)
-            wide = dot(sources[pl.ds(at, many), :], block, 1, 1)
-            total = wide[:, 0:TILE]
-            for j in range(1, many):
-                total = jnp.where(row == j, wide[:, j * TILE : (j + 1) * TILE], total)
-            products[pl.ds(at, many), :] = total
-        return carry
-
-    lax.fori_loop(0, SLOTS // CHUNK, step, 0, unroll=1 if copies else 2)
+    for at in range(0, SLOTS, many):
+        if copies and at % CHUNK == 0:
+            copies[at // CHUNK].wait()
+            for copy in copies[at // CHUNK + AHEAD : at // CHUNK + AHEAD + 1]:
+                copy.start()
+        block = tiles[pl.ds(at, many)].reshape(many * TILE, TILE)
+        wide = dot(sources[pl.ds(at, many), :], block, 1, 1)
+        total = wide[:, 0:TILE]
+        for j in range(1, many):
+            total = jnp.where(row == j, wide[:, j * TILE : (j + 1) * TILE], total)
+        products[pl.ds(at, many), :] = total
 
 
 def times_tiles(sources, tiles, products):
@@ -218,7 +229,7 @@
         products[pl.ds(at, many), :] = dot(jnp.concatenate(parts, axis=1), block)
         return carry
 
-    lax.fori_loop(0, SLOTS // many, step, 0, unroll=8)
+    lax.fori_loop(0, SLOTS // many, step, 0, unroll=True)
 
 
 def summed_by_row(row_row, products, out):
@@ -229,24 +240,27 @@
 def rows_product_first(
     row_total, arrived, pos_col, row_row, tiles, out, norm, grams, kept, sources, products, sems
 ):
-    def copy(chunk):
-        part = pl.ds(pl.multiple_of(chunk * CHUNK, CHUNK), CHUNK)
-        return pltpu.make_async_copy(tiles.at[part], kept.at[part], sems.at[chunk])
-
-    for chunk in range(SLOTS // CHUNK):
-        copy(chunk).start()
-    total = jnp.sum(arrived[:, PEER_TILES, 0, :], axis=0, keepdims=True)
-    size = jnp.sqrt(total / row_total + 1e-06)
+    parts = [pl.ds(at, CHUNK) for at in range(0, SLOTS, CHUNK)]
+    copies = [
+        pltpu.make_async_copy(tiles.at[part], kept.at[part], sems.at[i])
+        for i, part in enumerate(parts)
+    ]
+    for copy in copies[:AHEAD]:
+        copy.start()
+    part = lambda k: arrived[pl.ds(k, DEV, stride=EXTRA), :]
+    add = lambda k: jnp.sum(part(PEER_TILES + k), axis=0, keepdims=True)
+    size = jnp.sqrt(add(0) / row_total + 1e-06)
     norm[...] = size
-    grams[0:1, :] = jnp.sum(arrived[:, PEER_TILES + 1, 0, :], axis=0, keepdims=True)
-    grams[1:2, :] = jnp.sum(arrived[:, PEER_TILES + 2, 0, :], axis=0, keepdims=True)
+    grams[0:1, :] = add(1)
+    grams[1:2, :] = add(2)
     values = jnp.zeros((SLOTS, TILE), F32)
+    position = pos_col[...]
     for k in range(PEER_TILES):
-        vector = (arrived[:, k, 0, :] / size).astype(BF16)
-        hot = one_hot(iota((SLOTS, DEV), 1) * PEER_TILES + k == pos_col[...])
+        vector = (part(k) / size).astype(BF16)
+        hot = one_hot(iota((SLOTS, DEV), 1) * PEER_TILES + k == position)
         values = values + dot(hot, vector)
     sources[...] = values.astype(BF16)
-    tiles_times(sources, kept, products, copy)
+    tiles_times(sources, kept, products, copies)
     summed_by_row(row_row, products, out)
 
 
@@ -362,11 +376,11 @@
 
 
 def to_all(value):
-    return lax.all_to_all(value, ALL, 0, 0, tiled=True)
+    return lax.all_to_all(value, SEND_ALL, 0, 0, tiled=True)
 
 
 def in_group(value):
-    return lax.all_to_all(value, COL, 0, 0, tiled=True)
+    return lax.all_to_all(value, SEND_COL, 0, 0, tiled=True)
 
 
 def shards(tiles, row_tiles, col_tiles, counts, right_basis, left_basis, start):
@@ -397,7 +411,7 @@
         tables,
         [((1, SLOTS), I32), ((SLOTS, 1), I32)] * 2 + [square, square],
         (counts, rank, col_row, right, row_row, left),
-        [(left.shape, F32)],
+        [(left.shape, F32), ((1, SLOTS), I32)],
         in_specs=[SMEM] + [VMEM] * 3 + [HBM] * 2,
         semaphores=2,
     )
@@ -409,7 +423,7 @@
     partial, beta_zero, grams, tiles = call(
         with_total(rows_product_first),
         [in_rows, line, ((2, TILE), F32), (tiles.shape, BF16)],
-        (to_all(send), pos_col, row_row, tiles),
+        (to_all(send).reshape(DEV * EXTRA, TILE), pos_col, row_row, tiles),
         work,
         in_specs=[VMEM] * 3 + [HBM],
         semaphores=SLOTS // CHUNK,

time: 212 us -> 208 us (0.981)
  blocking collectives: 161 us -> 157 us
    all_to_all x12, blocking collectives: 161 us -> 157 us  [the longest x8 124 us: to_all(): return lax.all_to_all(value, SEND_ALL, 0, 0, tiled=True)]
where the time goes in v3:
time: 208 us
  blocking collectives  157 us (75%)
  Pallas kernels  31.6 us (15%)
  starting transfers between devices  11.5 us (6%)
  waiting for transfers between devices  5.77 us (3%)
    all_to_all x8, blocking collectives, to_all(): return lax.all_to_all(value, SEND_ALL, 0, 0, tiled=True)  124 us
    all_to_all x4, blocking collectives, in_group(): return lax.all_to_all(value, SEND_COL, 0, 0, tiled=True)  33.3 us
    pallas_call x15, Pallas kernels, call(): pl.pallas_call(body, out_shape=shapes, in_specs=in_specs or [VMEM] * len(...  31.6 us
    all_to_all x1, starting transfers between devices, to_all(): return lax.all_to_all(value, SEND_ALL, 0, 0, tiled=True)  11.5 us
    all_to_all x1, waiting for transfers between devices, to_all(): return lax.all_to_all(value, SEND_ALL, 0, 0, tiled=True)  5.77 us
  transfers between devices with their start and end apart: 1, of which 1 were waited for; matrix products, arithmetic and copies ran while one was open for 0% of the time, Pallas kernels for 1%

profile of v3, /device:TPU:1, one launch (start us, length us, event | category | flops | bytes accessed | tf_op | source)
XLA Modules:
  0.0 207.7 jit_solution(14217068664897178637)
XLA Ops:
  0.6 2.4 %shard_map.94 = (f32[128,1,128]{2,1,0:T(1,128)}, bf16[32,128]{1,0:T(8,128)(2,1)S(1)}, s32[1,512]{1,0:T(1,128)S(1)}, f32[32,128]{1,0:T(8,128)S(1)}, f32[100,4096]{1,0:T(8,128)S(1)}) custom-call(s32[1,512]{1,0:T(1,128)} %bitcast.6, f32[100,4096]{1,0:T(8,128)} %basis_hbm.1, f32[32,128]{1,0:T(8,128)} %bitcast.5), custom_call_target="tpu_custom_call" | custom-call | tf_op jit(solution)/shard_map/pallas_call | solution.py:367
  3.1 11.5 %all-to-all-start = ((f32[128,1,128]{2,1,0:T(1,128)}), f32[128,1,128]{2,1,0:T(1,128)S(1)}, u32[]{:S(2)}, u32[]{:S(2)}) async-start(f32[128,1,128]{2,1,0:T(1,128)} %get-tuple-element.42), calls=%async_computation | async-start | bytes 131072 | tf_op jit(solution)/shard_map/all_to_all | solution.py:379
  15.2 3.1 %shard_map.95 = (s32[1,512]{1,0:T(1,128)S(1)}, s32[512,1]{1,0:T(8,128)S(1)}, s32[1,512]{1,0:T(1,128)S(1)}, s32[512,1]{1,0:T(8,128)S(1)}, f32[128,128]{1,0:T(8,128)S(1)}, /*index=5*/f32[128,128]{1,0:T(8,128)S(1)}) custom-call(s32[1]{0:T(128)S(6)} %copy.10.counts, bf16[32,128]{1,0:T(8,128)(2,1)S(1)} %get-tuple-element.45.rank, ...), custom_call_target="tpu_custom_call" | custom-call | tf_op jit(solution)/shard_map/pallas_call | solution.py:367
  18.3 5.8 %all-to-all-done.arrived = f32[128,1,128]{2,1,0:T(1,128)S(1)} async-done(((f32[128,1,128]{2,1,0:T(1,128)}), f32[128,1,128]{2,1,0:T(1,128)S(1)}, u32[]{:S(2)}, u32[]{:S(2)}) %all-to-all-start) | async-done | bytes 65568 | tf_op jit(solution)/shard_map/all_to_all | solution.py:379
  24.1 1.0 shard_map.96
  25.1 19.2 %all_to_all.65 = f32[128,11,1,128]{3,2,1,0:T(1,128)S(1)} all-to-all(f32[128,11,1,128]{3,2,1,0:T(1,128)S(1)} %get-tuple-element.49), channel_id=1, replica_groups=mesh['row_0'=4,'row_1'=4,'col_0'=4,'col_1'=2] {'col_1','col_0','row_1','..., dimensions={0} | all-to-all | bytes 1441792 | tf_op jit(solution)/shard_map/all_to_all | solution.py:379
  44.3 0.0 copy-start
  44.3 7.7 %shard_map.97 = (f32[8,32,128]{2,1,0:T(8,128)S(1)}, f32[1,128]{1,0:T(1,128)S(1)}, f32[2,128]{1,0:T(2,128)S(1)}, bf16[512,128,128]{2,1,0:T(8,128)(2,1)S(1)}) custom-call(f32[1408,128]{1,0:T(8,128)S(1)} %bitcast.4, s32[512,1]{1,0:T(8,128)S(1)} %get-tuple-element.50.pos_col, s32[1,512]{1,0:T(1,128)S(1)} %get-tuple-element.51.row_row, bf16[512,128,128]{2,1,0:T(8,128)(2,1)} %tiles.1), custom_call_target="tpu_custom_call" | custom-call | tf_op jit(solution)/shard_map/pallas_call | solution.py:367
  52.0 8.4 %all_to_all.66.arrived = f32[8,32,128]{2,1,0:T(8,128)S(1)} all-to-all(f32[8,32,128]{2,1,0:T(8,128)S(1)} %get-tuple-element.52), channel_id=1, replica_groups=mesh['row_0'=4,'row_1'=4,'col_0'=4,'col_1'=2] {'col_1','col_0'}, dimensions={0} | all-to-all | bytes 262144 | tf_op jit(solution)/shard_map/all_to_all | solution.py:383
  60.5 0.0 copy-done
  60.5 0.4 shard_map.98
  60.9 14.6 %all_to_all.67.arrived = f32[128,1,384]{2,1,0:T(1,128)S(1)} all-to-all(f32[128,1,384]{2,1,0:T(1,128)S(1)} %get-tuple-element.54), channel_id=1, replica_groups=mesh['row_0'=4,'row_1'=4,'col_0'=4,'col_1'=2] {'col_1','col_0','row_1','..., dimensions={0} | all-to-all | bytes 393216 | tf_op jit(solution)/shard_map/all_to_all | solution.py:379
  75.5 0.3 shard_map.99
  75.8 8.2 %all_to_all.68.arrived = bf16[8,32,128]{2,1,0:T(8,128)(2,1)S(1)} all-to-all(bf16[8,32,128]{2,1,0:T(8,128)(2,1)S(1)} %get-tuple-element.56), channel_id=1, replica_groups=mesh['row_0'=4,'row_1'=4,'col_0'=4,'col_1'=2] {'col_1','col_0'}, dimensions={0} | all-to-all | bytes 131072 | tf_op jit(solution)/shard_map/all_to_all | solution.py:383
  84.0 3.5 %shard_map.100 = f32[128,8,128]{2,1,0:T(8,128)S(1)} custom-call(bf16[8,32,128]{2,1,0:T(8,128)(2,1)S(1)} %all_to_all.68.arrived, s32[512,1]{1,0:T(8,128)S(1)} %get-tuple-element.57.row_col, s32[1,512]{1,0:T(1,128)S(1)} %get-tuple-element.58.pos_row, bf16[512,128,128]{2,1,0:T(8,128)(2,1)S(1)} %get-tuple-element.59.tiles), custom_call_target="tpu_custom_call" | custom-call | tf_op jit(solution)/shard_map/pallas_call | solution.py:367
  87.4 17.3 %all_to_all.69.arrived = f32[128,8,128]{2,1,0:T(8,128)S(1)} all-to-all(f32[128,8,128]{2,1,0:T(8,128)S(1)} %shard_map.100), channel_id=1, replica_groups=mesh['row_0'=4,'row_1'=4,'col_0'=4,'col_1'=2] {'col_1','col_0','row_1','..., dimensions={0} | all-to-all | bytes 1048576 | tf_op jit(solution)/shard_map/all_to_all | solution.py:379
  104.8 0.6 shard_map.101
  105.4 13.5 %all_to_all.70.arrived = f32[128,1,128]{2,1,0:T(1,128)S(1)} all-to-all(f32[128,1,128]{2,1,0:T(1,128)S(1)} %get-tuple-element.64), channel_id=1, replica_groups=mesh['row_0'=4,'row_1'=4,'col_0'=4,'col_1'=2] {'col_1','col_0','row_1','..., dimensions={0} | all-to-all | bytes 131072 | tf_op jit(solution)/shard_map/all_to_all | solution.py:379
  118.9 0.5 shard_map.102
  119.5 14.7 %all_to_all.71.arrived = bf16[128,8,128]{2,1,0:T(8,128)(2,1)S(1)} all-to-all(bf16[128,8,128]{2,1,0:T(8,128)(2,1)S(1)} %get-tuple-element.67), channel_id=1, replica_groups=mesh['row_0'=4,'row_1'=4,'col_0'=4,'col_1'=2] {'col_1','col_0','row_1','..., dimensions={0} | all-to-all | bytes 524288 | tf_op jit(solution)/shard_map/all_to_all | solution.py:379
  134.2 5.7 %shard_map.103 = f32[8,32,128]{2,1,0:T(8,128)S(1)} custom-call(bf16[128,8,128]{2,1,0:T(8,128)(2,1)S(1)} %all_to_all.71.arrived, s32[512,1]{1,0:T(8,128)S(1)} %get-tuple-element.50.pos_col, s32[1,512]{1,0:T(1,128)S(1)} %get-tuple-element.51.row_row, bf16[512,128,128]{2,1,0:T(8,128)(2,1)S(1)} %get-tuple-element.59.tiles), custom_call_target="tpu_custom_call" | custom-call | tf_op jit(solution)/shard_map/pallas_call | solution.py:367
  139.9 8.4 %all_to_all.72.arrived = f32[8,32,128]{2,1,0:T(8,128)S(1)} all-to-all(f32[8,32,128]{2,1,0:T(8,128)S(1)} %shard_map.103), channel_id=1, replica_groups=mesh['row_0'=4,'row_1'=4,'col_0'=4,'col_1'=2] {'col_1','col_0'}, dimensions={0} | all-to-all | bytes 262144 | tf_op jit(solution)/shard_map/all_to_all | solution.py:383
  148.3 0.4 shard_map.104
  148.7 13.7 %all_to_all.73.arrived = f32[128,1,128]{2,1,0:T(1,128)S(1)} all-to-all(f32[128,1,128]{2,1,0:T(1,128)S(1)} %get-tuple-element.70), channel_id=1, replica_groups=mesh['row_0'=4,'row_1'=4,'col_0'=4,'col_1'=2] {'col_1','col_0','row_1','..., dimensions={0} | all-to-all | bytes 131072 | tf_op jit(solution)/shard_map/all_to_all | solution.py:379
  162.4 1.0 shard_map.105
  163.3 8.3 %all_to_all.74.arrived = bf16[8,32,128]{2,1,0:T(8,128)(2,1)S(1)} all-to-all(bf16[8,32,128]{2,1,0:T(8,128)(2,1)S(1)} %get-tuple-element.74), channel_id=1, replica_groups=mesh['row_0'=4,'row_1'=4,'col_0'=4,'col_1'=2] {'col_1','col_0'}, dimensions={0} | all-to-all | bytes 131072 | tf_op jit(solution)/shard_map/all_to_all | solution.py:383
  171.6 3.5 %shard_map.106 = f32[128,8,128]{2,1,0:T(8,128)S(1)} custom-call(bf16[8,32,128]{2,1,0:T(8,128)(2,1)S(1)} %all_to_all.74.arrived, s32[512,1]{1,0:T(8,128)S(1)} %get-tuple-element.57.row_col, s32[1,512]{1,0:T(1,128)S(1)} %get-tuple-element.58.pos_row, bf16[512,128,128]{2,1,0:T(8,128)(2,1)S(1)} %get-tuple-element.59.tiles), custom_call_target="tpu_custom_call" | custom-call | tf_op jit(solution)/shard_map/pallas_call | solution.py:367
  175.1 17.3 %all_to_all.75.arrived = f32[128,8,128]{2,1,0:T(8,128)S(1)} all-to-all(f32[128,8,128]{2,1,0:T(8,128)S(1)} %shard_map.106), channel_id=1, replica_groups=mesh['row_0'=4,'row_1'=4,'col_0'=4,'col_1'=2] {'col_1','col_0','row_1','..., dimensions={0} | all-to-all | bytes 1048576 | tf_op jit(solution)/shard_map/all_to_all | solution.py:379
  192.4 0.6 shard_map.107
  193.0 13.5 %all_to_all.76.arrived = f32[128,1,128]{2,1,0:T(1,128)S(1)} all-to-all(f32[128,1,128]{2,1,0:T(1,128)S(1)} %get-tuple-element.77), channel_id=1, replica_groups=mesh['row_0'=4,'row_1'=4,'col_0'=4,'col_1'=2] {'col_1','col_0','row_1','..., dimensions={0} | all-to-all | bytes 131072 | tf_op jit(solution)/shard_map/all_to_all | solution.py:379
  206.5 1.0 shard_map.108
Async XLA Ops:
  3.1 21.0 %all-to-all-start = ((f32[128,1,128]{2,1,0:T(1,128)}), f32[128,1,128]{2,1,0:T(1,128)S(1)}, u32[]{:S(2)}, u32[]{:S(2)}) async-start(f32[128,1,128]{2,1,0:T(1,128)} %get-tuple-element.42), calls=%async_computation | async-start | bytes 131072 | tf_op jit(solution)/shard_map/all_to_all | solution.py:379
  44.3 16.1 %copy-start = (f32[100,4096]{1,0:T(8,128)S(1)}, f32[100,4096]{1,0:T(8,128)}, u32[]{:S(2)}) copy-start(f32[100,4096]{1,0:T(8,128)} %basis.7) | copy-start | bytes 4915204

commit v4 on v3

--- a/solution.py
+++ b/solution.py
@@ -23,9 +23,8 @@
 NAMED = DEV * PEER_TILES
 PLACE = 104
 PARTS = 4
-CHUNK = 64
-AHEAD = 4
-EXTRA = PEER_TILES + 3
+SQUARE, DIAGONAL = 126, 127
+EXTRA = PEER_TILES + 1
 
 
 def iota(shape, dim):
@@ -181,7 +180,7 @@
     return jnp.round(row).astype(I32)
 
 
-def first_vector(row_total, arrived, start, basis, gram_r, gram_l, rest, send, place_row):
+def first_vector(row_total, arrived, start, basis, gram_r, gram_l, _, rest, send, place_row):
     size = basis.shape[0]
     got = arrived[:, 0, :]
     total = jnp.sum(got, axis=0, keepdims=True)
@@ -195,20 +194,18 @@
     for k in range(PEER_TILES):
         send[:, k, 0, :] = blocks[:, k, :]
     square = jnp.sum(vector * vector, keepdims=True)
-    send[:, PEER_TILES, 0, :] = jnp.broadcast_to(square, (DEV, TILE))
-    send[:, PEER_TILES + 1, 0, :] = gram_r[...]
-    send[:, PEER_TILES + 2, 0, :] = gram_l[...]
-
-
-def tiles_times(sources, tiles, products, copies=None):
+    row, lane = iota((DEV, TILE), 0), iota((DEV, TILE), 1)
+    diagonal = jnp.sum(jnp.where(row == lane, gram_r[...], 0.0), axis=1, keepdims=True)
+    packed = jnp.where(row > lane, gram_r[...], gram_l[...])
+    packed = jnp.where(lane == DIAGONAL, diagonal, packed)
+    send[:, PEER_TILES, 0, :] = jnp.where(lane == SQUARE, square, packed)
+
+
+def tiles_times(sources, tiles, products):
     many = 16
     row = iota((many, TILE), 0)
 
     for at in range(0, SLOTS, many):
-        if copies and at % CHUNK == 0:
-            copies[at // CHUNK].wait()
-            for copy in copies[at // CHUNK + AHEAD : at // CHUNK + AHEAD + 1]:
-                copy.start()
         block = tiles[pl.ds(at, many)].reshape(many * TILE, TILE)
         wide = dot(sources[pl.ds(at, many), :], block, 1, 1)
         total = wide[:, 0:TILE]
@@ -238,21 +235,14 @@
 
 
 def rows_product_first(
-    row_total, arrived, pos_col, row_row, tiles, out, norm, grams, kept, sources, products, sems
+    row_total, arrived, pos_col, row_row, tiles, out, norm, gram_row, sources, products
 ):
-    parts = [pl.ds(at, CHUNK) for at in range(0, SLOTS, CHUNK)]
-    copies = [
-        pltpu.make_async_copy(tiles.at[part], kept.at[part], sems.at[i])
-        for i, part in enumerate(parts)
-    ]
-    for copy in copies[:AHEAD]:
-        copy.start()
     part = lambda k: arrived[pl.ds(k, DEV, stride=EXTRA), :]
-    add = lambda k: jnp.sum(part(PEER_TILES + k), axis=0, keepdims=True)
-    size = jnp.sqrt(add(0) / row_total + 1e-06)
-    norm[...] = size
-    grams[0:1, :] = add(1)
-    grams[1:2, :] = add(2)
+    total = jnp.sum(part(PEER_TILES), axis=0, keepdims=True)
+    gram_row[...] = total
+    total = jnp.sum(jnp.where(iota((1, TILE), 1) == SQUARE, total, 0.0), axis=1, keepdims=True)
+    size = jnp.sqrt(total / row_total + 1e-06)
+    norm[...] = jnp.broadcast_to(size, (1, TILE))
     values = jnp.zeros((SLOTS, TILE), F32)
     position = pos_col[...]
     for k in range(PEER_TILES):
@@ -260,7 +250,7 @@
         hot = one_hot(iota((SLOTS, DEV), 1) * PEER_TILES + k == position)
         values = values + dot(hot, vector)
     sources[...] = values.astype(BF16)
-    tiles_times(sources, kept, products, copies)
+    tiles_times(sources, tiles, products)
     summed_by_row(row_row, products, out)
 
 
@@ -281,13 +271,12 @@
     out[...] = selected(hot, products[...]).reshape(out.shape)
 
 
-def image_sums_first(arrived, basis, grams, image, out, held):
+def image_sums_first(arrived, basis, gram_row, image, out, held):
     vector = jnp.sum(arrived[...], axis=0)
     image[...] = vector
     row = products_row(basis, vector, held)
     out[:, 0, 0:TILE] = jnp.broadcast_to(row, (DEV, TILE))
-    out[:, 0, TILE : 2 * TILE] = jnp.broadcast_to(grams[0:1, :], (DEV, TILE))
-    out[:, 0, 2 * TILE : 3 * TILE] = jnp.broadcast_to(grams[1:2, :], (DEV, TILE))
+    out[:, 0, TILE : 2 * TILE] = jnp.broadcast_to(gram_row[...], (DEV, TILE))
 
 
 def image_sums(arrived, basis, earlier, factor, image, out, held):
@@ -306,8 +295,12 @@
 
 def left_vector_first(row_total, arrived, image, basis, new, copies, norm, gram_r, gram_l):
     got = arrived[:, 0, :]
-    gram_r[...] = got[:, TILE : 2 * TILE]
-    gram_l[...] = got[:, 2 * TILE : 3 * TILE]
+    both = got[:, TILE : 2 * TILE]
+    row, lane = iota((DEV, TILE), 0), iota((DEV, TILE), 1)
+    diagonal = jnp.sum(jnp.where(lane == DIAGONAL, both, 0.0), axis=1, keepdims=True)
+    gram_r[...] = jnp.where(row > lane, both + both, jnp.where(row == lane, diagonal, 0.0))
+    upper = jnp.where(row < lane, both + both, jnp.where(row == lane, both, 0.0))
+    gram_l[...] = jnp.where(lane < basis.shape[0], upper, 0.0)
     total = jnp.sum(got[:, 0:TILE], axis=0, keepdims=True)
     finish(row_total, total, image, basis, gram_l, new, norm)
     copies[...] = jnp.broadcast_to(new[...].astype(BF16), copies.shape)
@@ -322,17 +315,10 @@
     new[...] = new[...] / factor
 
 
-def lines(out, at, vector):
-    for k in range(OWN):
-        out[at : at + 1, k * TILE : (k + 1) * TILE] = vector[k : k + 1, :]
-
-
-def left_vector(row_total, arrived, image, basis, gram, earlier, new_pair, copies, norm, new):
+def left_vector(row_total, arrived, image, basis, gram, new, copies, norm):
     total = jnp.sum(arrived[:, 0, :], axis=0, keepdims=True)
     finish(row_total, total, image, basis, gram, new, norm)
     copies[...] = jnp.broadcast_to(new[...].astype(BF16), copies.shape)
-    lines(new_pair, 0, earlier)
-    lines(new_pair, 1, new)
 
 
 def right_vector(row_total, arrived, back, basis, gram, place_row, new, send, norm):
@@ -343,12 +329,14 @@
     send[...] = blocks.astype(BF16).reshape(send.shape)
 
 
-def last_vector(row_total, arrived, back, basis, gram, earlier, *rest):
-    norms, (new_pair, factors, new, norm) = rest[:4], rest[4:]
+def last_vector(row_total, arrived, back, basis, gram, earlier, left_one, left_two, *rest):
+    norms, (left_pair, new_pair, factors, new, norm) = rest[:4], rest[4:]
+    left_pair[:, 0, :] = left_one[...]
+    left_pair[:, 1, :] = left_two[...]
     total = jnp.sum(arrived[:, 0, :], axis=0, keepdims=True)
     finish(row_total, total, back, basis, gram, new, norm)
-    lines(new_pair, 0, earlier)
-    lines(new_pair, 1, new)
+    new_pair[:, 0, :] = earlier[...]
+    new_pair[:, 1, :] = new[...]
     for i, value in enumerate((*norms, norm)):
         factors[i] = jnp.max(value[...])
 
@@ -418,20 +406,19 @@
     rest, send, place_row = call(
         with_total(first_vector),
         [own, ((DEV, EXTRA, 1, TILE), F32), ((1, NAMED), I32)],
-        (arrived, begin, right, gram_r, gram_l),
-    )
-    partial, beta_zero, grams, tiles = call(
+        (arrived, begin, right, gram_r, gram_l, tiles),
+        in_specs=[VMEM] * 5 + [HBM],
+    )
+    partial, beta_zero, gram_row = call(
         with_total(rows_product_first),
-        [in_rows, line, ((2, TILE), F32), (tiles.shape, BF16)],
+        [in_rows, line, line],
         (to_all(send).reshape(DEV * EXTRA, TILE), pos_col, row_row, tiles),
         work,
-        in_specs=[VMEM] * 3 + [HBM],
-        semaphores=SLOTS // CHUNK,
     )
     image, pay = call(
         image_sums_first,
-        [own, ((DEV, 1, 3 * TILE), F32)],
-        (in_group(partial), left, grams),
+        [own, ((DEV, 1, 2 * TILE), F32)],
+        (in_group(partial), left, gram_row),
         [square],
     )
     left_one, copies, alpha_one, gram_r, gram_l = call(
@@ -457,11 +444,8 @@
     image, pay = call(
         image_sums, [own, sums], (in_group(partial), left, left_one, beta_one), [square]
     )
-    lefts, copies, alpha_two = call(
-        with_total(left_vector),
-        [((2, OWN * TILE), F32), copied, line],
-        (to_all(pay), image, left, gram_l, left_one),
-        [own],
+    left_two, copies, alpha_two = call(
+        with_total(left_vector), [own, copied, line], (to_all(pay), image, left, gram_l)
     )
     (outgoing,) = call(
         column_product, [(blocks, F32)], (in_group(copies), row_col, pos_row, tiles), work
@@ -472,14 +456,16 @@
         (to_all(outgoing), right, place_row, right_two, beta_one, alpha_two),
         [square],
     )
-    rights, factors = call(
+    norms = (beta_zero, alpha_one, beta_one, alpha_two)
+    lefts, rights, factors = call(
         with_total(last_vector),
-        [((2, OWN * TILE), F32), ((5,), F32)],
-        (to_all(pay), back, right, gram_r, right_two, beta_zero, alpha_one, beta_one, alpha_two),
+        [((OWN, 2, TILE), F32)] * 2 + [((5,), F32)],
+        (to_all(pay), back, right, gram_r, right_two, left_one, left_two, *norms),
         [own, line],
-        out_specs=[VMEM, SMEM],
-    )
-    return lefts, rights, factors
+        out_specs=[VMEM, VMEM, SMEM],
+    )
+    as_rows = lambda pair: pair.transpose(1, 0, 2).reshape(2, OWN * TILE)
+    return as_rows(lefts), as_rows(rights), factors
 
 
 def solution(mesh):

time: 208 us -> 204 us (0.981)
  Pallas kernels: 31.6 us -> 29 us
    pallas_call x15, Pallas kernels: 31.6 us -> 29 us  [call(): pl.pallas_call(body, out_shape=shapes, in_specs=in_specs or [VMEM] * len(...]
  transfers between devices with their start and end apart: 1 -> 1, of which waited for: 1 -> 1; matrix products, arithmetic and copies ran while one was open for 0% -> 0% of each run, Pallas kernels for 1% -> 2%
where the time goes in v4:
time: 204 us; the launch traced here: 203 us
  blocking collectives  156 us (76%)
  Pallas kernels  29 us (14%)
  starting transfers between devices  11.5 us (6%)
  waiting for transfers between devices  5.78 us (3%)
    all_to_all x8, blocking collectives, to_all(): return lax.all_to_all(value, SEND_ALL, 0, 0, tiled=True)  122 us
    all_to_all x4, blocking collectives, in_group(): return lax.all_to_all(value, SEND_COL, 0, 0, tiled=True)  33.2 us
    pallas_call x15, Pallas kernels, call(): pl.pallas_call(body, out_shape=shapes, in_specs=in_specs or [VMEM] * len(...  29 us
    all_to_all x1, starting transfers between devices, to_all(): return lax.all_to_all(value, SEND_ALL, 0, 0, tiled=True)  11.5 us
    all_to_all x1, waiting for transfers between devices, to_all(): return lax.all_to_all(value, SEND_ALL, 0, 0, tiled=True)  5.78 us
  transfers between devices with their start and end apart: 1, of which 1 were waited for; matrix products, arithmetic and copies ran while one was open for 0% of the time, Pallas kernels for 2%

profile of v4, /device:TPU:1, one launch (start us, length us, event | category | flops | bytes accessed | tf_op | source)
XLA Modules:
  0.0 203.4 jit_solution(16471826384282596187)
XLA Ops:
  0.6 2.4 %shard_map.94 = (f32[128,1,128]{2,1,0:T(1,128)}, bf16[32,128]{1,0:T(8,128)(2,1)S(1)}, s32[1,512]{1,0:T(1,128)S(1)}, f32[32,128]{1,0:T(8,128)S(1)}, f32[100,4096]{1,0:T(8,128)S(1)}) custom-call(s32[1,512]{1,0:T(1,128)} %bitcast.12, f32[100,4096]{1,0:T(8,128)} %basis_hbm.1, f32[32,128]{1,0:T(8,128)} %bitcast.11), custom_call_target="tpu_custom_call" | custom-call | tf_op jit(solution)/shard_map/pallas_call | solution.py:355
  3.1 11.5 %all-to-all-start = ((f32[128,1,128]{2,1,0:T(1,128)}), f32[128,1,128]{2,1,0:T(1,128)S(1)}, u32[]{:S(2)}, u32[]{:S(2)}) async-start(f32[128,1,128]{2,1,0:T(1,128)} %get-tuple-element.42), calls=%async_computation | async-start | bytes 131072 | tf_op jit(solution)/shard_map/all_to_all | solution.py:367
  15.2 3.1 %shard_map.95 = (s32[1,512]{1,0:T(1,128)S(1)}, s32[512,1]{1,0:T(8,128)S(1)}, s32[1,512]{1,0:T(1,128)S(1)}, s32[512,1]{1,0:T(8,128)S(1)}, f32[128,128]{1,0:T(8,128)S(1)}, /*index=5*/f32[128,128]{1,0:T(8,128)S(1)}) custom-call(s32[1]{0:T(128)S(6)} %copy.10.counts, bf16[32,128]{1,0:T(8,128)(2,1)S(1)} %get-tuple-element.45.rank, ...), custom_call_target="tpu_custom_call" | custom-call | tf_op jit(solution)/shard_map/pallas_call | solution.py:355
  18.3 5.8 %all-to-all-done.arrived = f32[128,1,128]{2,1,0:T(1,128)S(1)} async-done(((f32[128,1,128]{2,1,0:T(1,128)}), f32[128,1,128]{2,1,0:T(1,128)S(1)}, u32[]{:S(2)}, u32[]{:S(2)}) %all-to-all-start) | async-done | bytes 65568 | tf_op jit(solution)/shard_map/all_to_all | solution.py:367
  24.1 0.0 copy-start
  24.1 0.9 shard_map.96
  25.0 18.1 %all_to_all.65 = f32[128,9,1,128]{3,2,1,0:T(1,128)S(1)} all-to-all(f32[128,9,1,128]{3,2,1,0:T(1,128)S(1)} %get-tuple-element.49), channel_id=1, replica_groups=mesh['row_0'=4,'row_1'=4,'col_0'=4,'col_1'=2] {'col_1','col_0','row_1','..., dimensions={0} | all-to-all | bytes 1179648 | tf_op jit(solution)/shard_map/all_to_all | solution.py:367
  43.1 0.0 copy-done
  43.1 5.8 %shard_map.97 = (f32[8,32,128]{2,1,0:T(8,128)S(1)}, f32[1,128]{1,0:T(1,128)S(1)}, f32[1,128]{1,0:T(1,128)S(1)}) custom-call(f32[1152,128]{1,0:T(8,128)S(1)} %bitcast.10, s32[512,1]{1,0:T(8,128)S(1)} %get-tuple-element.50.pos_col, s32[1,512]{1,0:T(1,128)S(1)} %get-tuple-element.51.row_row, bf16[512,128,128]{2,1,0:T(8,128)(2,1)S(1)} %copy-done), custom_call_target="tpu_custom_call" | custom-call | tf_op jit(solution)/shard_map/pallas_call | solution.py:355
  48.9 8.3 %all_to_all.66.arrived = f32[8,32,128]{2,1,0:T(8,128)S(1)} all-to-all(f32[8,32,128]{2,1,0:T(8,128)S(1)} %get-tuple-element.52), channel_id=1, replica_groups=mesh['row_0'=4,'row_1'=4,'col_0'=4,'col_1'=2] {'col_1','col_0'}, dimensions={0} | all-to-all | bytes 262144 | tf_op jit(solution)/shard_map/all_to_all | solution.py:371
  57.2 0.0 copy-done.1
  57.2 0.4 shard_map.98
  57.6 14.3 %all_to_all.67.arrived = f32[128,1,256]{2,1,0:T(1,128)S(1)} all-to-all(f32[128,1,256]{2,1,0:T(1,128)S(1)} %get-tuple-element.54), channel_id=1, replica_groups=mesh['row_0'=4,'row_1'=4,'col_0'=4,'col_1'=2] {'col_1','col_0','row_1','..., dimensions={0} | all-to-all | bytes 262144 | tf_op jit(solution)/shard_map/all_to_all | solution.py:367
  71.9 0.3 shard_map.99
  72.3 8.1 %all_to_all.68.arrived = bf16[8,32,128]{2,1,0:T(8,128)(2,1)S(1)} all-to-all(bf16[8,32,128]{2,1,0:T(8,128)(2,1)S(1)} %get-tuple-element.56), channel_id=1, replica_groups=mesh['row_0'=4,'row_1'=4,'col_0'=4,'col_1'=2] {'col_1','col_0'}, dimensions={0} | all-to-all | bytes 131072 | tf_op jit(solution)/shard_map/all_to_all | solution.py:371
  80.4 3.5 %shard_map.100 = f32[128,8,128]{2,1,0:T(8,128)S(1)} custom-call(bf16[8,32,128]{2,1,0:T(8,128)(2,1)S(1)} %all_to_all.68.arrived, s32[512,1]{1,0:T(8,128)S(1)} %get-tuple-element.57.row_col, s32[1,512]{1,0:T(1,128)S(1)} %get-tuple-element.58.pos_row, bf16[512,128,128]{2,1,0:T(8,128)(2,1)S(1)} %copy-done), custom_call_target="tpu_custom_call" | custom-call | tf_op jit(solution)/shard_map/pallas_call | solution.py:355
  83.8 17.3 %all_to_all.69.arrived = f32[128,8,128]{2,1,0:T(8,128)S(1)} all-to-all(f32[128,8,128]{2,1,0:T(8,128)S(1)} %shard_map.100), channel_id=1, replica_groups=mesh['row_0'=4,'row_1'=4,'col_0'=4,'col_1'=2] {'col_1','col_0','row_1','..., dimensions={0} | all-to-all | bytes 1048576 | tf_op jit(solution)/shard_map/all_to_all | solution.py:367
  101.1 0.6 shard_map.101
  101.8 13.5 %all_to_all.70.arrived = f32[128,1,128]{2,1,0:T(1,128)S(1)} all-to-all(f32[128,1,128]{2,1,0:T(1,128)S(1)} %get-tuple-element.63), channel_id=1, replica_groups=mesh['row_0'=4,'row_1'=4,'col_0'=4,'col_1'=2] {'col_1','col_0','row_1','..., dimensions={0} | all-to-all | bytes 131072 | tf_op jit(solution)/shard_map/all_to_all | solution.py:367
  115.3 0.5 shard_map.102
  115.9 14.7 %all_to_all.71.arrived = bf16[128,8,128]{2,1,0:T(8,128)(2,1)S(1)} all-to-all(bf16[128,8,128]{2,1,0:T(8,128)(2,1)S(1)} %get-tuple-element.66), channel_id=1, replica_groups=mesh['row_0'=4,'row_1'=4,'col_0'=4,'col_1'=2] {'col_1','col_0','row_1','..., dimensions={0} | all-to-all | bytes 524288 | tf_op jit(solution)/shard_map/all_to_all | solution.py:367
  130.6 5.7 %shard_map.103 = f32[8,32,128]{2,1,0:T(8,128)S(1)} custom-call(bf16[128,8,128]{2,1,0:T(8,128)(2,1)S(1)} %all_to_all.71.arrived, s32[512,1]{1,0:T(8,128)S(1)} %get-tuple-element.50.pos_col, s32[1,512]{1,0:T(1,128)S(1)} %get-tuple-element.51.row_row, bf16[512,128,128]{2,1,0:T(8,128)(2,1)S(1)} %copy-done), custom_call_target="tpu_custom_call" | custom-call | tf_op jit(solution)/shard_map/pallas_call | solution.py:355
  136.2 8.4 %all_to_all.72.arrived = f32[8,32,128]{2,1,0:T(8,128)S(1)} all-to-all(f32[8,32,128]{2,1,0:T(8,128)S(1)} %shard_map.103), channel_id=1, replica_groups=mesh['row_0'=4,'row_1'=4,'col_0'=4,'col_1'=2] {'col_1','col_0'}, dimensions={0} | all-to-all | bytes 262144 | tf_op jit(solution)/shard_map/all_to_all | solution.py:371
  144.7 0.4 shard_map.104
  145.1 13.7 %all_to_all.73.arrived = f32[128,1,128]{2,1,0:T(1,128)S(1)} all-to-all(f32[128,1,128]{2,1,0:T(1,128)S(1)} %get-tuple-element.69), channel_id=1, replica_groups=mesh['row_0'=4,'row_1'=4,'col_0'=4,'col_1'=2] {'col_1','col_0','row_1','..., dimensions={0} | all-to-all | bytes 131072 | tf_op jit(solution)/shard_map/all_to_all | solution.py:367
  158.8 0.3 shard_map.105
  159.1 8.3 %all_to_all.74.arrived = bf16[8,32,128]{2,1,0:T(8,128)(2,1)S(1)} all-to-all(bf16[8,32,128]{2,1,0:T(8,128)(2,1)S(1)} %get-tuple-element.72), channel_id=1, replica_groups=mesh['row_0'=4,'row_1'=4,'col_0'=4,'col_1'=2] {'col_1','col_0'}, dimensions={0} | all-to-all | bytes 131072 | tf_op jit(solution)/shard_map/all_to_all | solution.py:371
  167.4 3.5 %shard_map.106 = f32[128,8,128]{2,1,0:T(8,128)S(1)} custom-call(bf16[8,32,128]{2,1,0:T(8,128)(2,1)S(1)} %all_to_all.74.arrived, s32[512,1]{1,0:T(8,128)S(1)} %get-tuple-element.57.row_col, s32[1,512]{1,0:T(1,128)S(1)} %get-tuple-element.58.pos_row, bf16[512,128,128]{2,1,0:T(8,128)(2,1)S(1)} %copy-done), custom_call_target="tpu_custom_call" | custom-call | tf_op jit(solution)/shard_map/pallas_call | solution.py:355
  170.8 17.3 %all_to_all.75.arrived = f32[128,8,128]{2,1,0:T(8,128)S(1)} all-to-all(f32[128,8,128]{2,1,0:T(8,128)S(1)} %shard_map.106), channel_id=1, replica_groups=mesh['row_0'=4,'row_1'=4,'col_0'=4,'col_1'=2] {'col_1','col_0','row_1','..., dimensions={0} | all-to-all | bytes 1048576 | tf_op jit(solution)/shard_map/all_to_all | solution.py:367
  188.1 0.6 shard_map.107
  188.8 13.5 %all_to_all.76.arrived = f32[128,1,128]{2,1,0:T(1,128)S(1)} all-to-all(f32[128,1,128]{2,1,0:T(1,128)S(1)} %get-tuple-element.75), channel_id=1, replica_groups=mesh['row_0'=4,'row_1'=4,'col_0'=4,'col_1'=2] {'col_1','col_0','row_1','..., dimensions={0} | all-to-all | bytes 131072 | tf_op jit(solution)/shard_map/all_to_all | solution.py:367
  202.3 0.9 shard_map.108
  (1 shorter events, 0.0 us)
Async XLA Ops:
  3.1 21.0 %all-to-all-start = ((f32[128,1,128]{2,1,0:T(1,128)}), f32[128,1,128]{2,1,0:T(1,128)S(1)}, u32[]{:S(2)}, u32[]{:S(2)}) async-start(f32[128,1,128]{2,1,0:T(1,128)} %get-tuple-element.42), calls=%async_computation | async-start | bytes 131072 | tf_op jit(solution)/shard_map/all_to_all | solution.py:367
  24.1 19.0 %copy-start = (bf16[512,128,128]{2,1,0:T(8,128)(2,1)S(1)}, bf16[512,128,128]{2,1,0:T(8,128)(2,1)}, u32[]{:S(2)}) copy-start(bf16[512,128,128]{2,1,0:T(8,128)(2,1)} %tiles.7) | copy-start | bytes 50331652
  43.1 14.1 %copy-start.1 = (f32[100,4096]{1,0:T(8,128)S(1)}, f32[100,4096]{1,0:T(8,128)}, u32[]{:S(2)}) copy-start(f32[100,4096]{1,0:T(8,128)} %basis.7) | copy-start | bytes 4915204

commit v5 on v4

--- a/solution.py
+++ b/solution.py
@@ -214,6 +214,19 @@
         products[pl.ds(at, many), :] = total
 
 
+def tiles_times_turned(sources, tiles, products, turned):
+    many = 16
+    row = iota((many, TILE), 0)
+    for at in range(0, SLOTS, many):
+        mine = sources[pl.ds(at, many), :]
+        blocks = [tiles[at + j].T for j in range(many)]
+        for j in range(many):
+            turned[at + j] = blocks[j]
+        parts = [jnp.where(row == j, mine, jnp.zeros_like(mine)) for j in range(many)]
+        block = jnp.concatenate(blocks, axis=0)
+        products[pl.ds(at, many), :] = dot(jnp.concatenate(parts, axis=1), block)
+
+
 def times_tiles(sources, tiles, products):
     many = 16
     row = iota((many, TILE), 0)
@@ -235,7 +248,7 @@
 
 
 def rows_product_first(
-    row_total, arrived, pos_col, row_row, tiles, out, norm, gram_row, sources, products
+    row_total, arrived, pos_col, row_row, tiles, out, norm, gram_row, turned, sources, products
 ):
     part = lambda k: arrived[pl.ds(k, DEV, stride=EXTRA), :]
     total = jnp.sum(part(PEER_TILES), axis=0, keepdims=True)
@@ -250,7 +263,7 @@
         hot = one_hot(iota((SLOTS, DEV), 1) * PEER_TILES + k == position)
         values = values + dot(hot, vector)
     sources[...] = values.astype(BF16)
-    tiles_times(sources, tiles, products)
+    tiles_times_turned(sources, tiles, products, turned)
     summed_by_row(row_row, products, out)
 
 
@@ -258,7 +271,7 @@
     hot = one_hot(iota((SLOTS, NAMED), 1) == pos_col[...])
     vector = arrived[...].reshape(NAMED, TILE)
     sources[...] = dot(hot, vector).astype(BF16)
-    tiles_times(sources, tiles, products)
+    times_tiles(sources, tiles, products)
     summed_by_row(row_row, products, out)
 
 
@@ -409,9 +422,9 @@
         (arrived, begin, right, gram_r, gram_l, tiles),
         in_specs=[VMEM] * 5 + [HBM],
     )
-    partial, beta_zero, gram_row = call(
+    partial, beta_zero, gram_row, turned = call(
         with_total(rows_product_first),
-        [in_rows, line, line],
+        [in_rows, line, line, (tiles.shape, BF16)],
         (to_all(send).reshape(DEV * EXTRA, TILE), pos_col, row_row, tiles),
         work,
     )
@@ -440,7 +453,7 @@
         [own, (blocks, BF16), line],
         (to_all(pay), back, right, gram_r, place_row),
     )
-    (partial,) = call(rows_product, [in_rows], (to_all(send), pos_col, row_row, tiles), work)
+    (partial,) = call(rows_product, [in_rows], (to_all(send), pos_col, row_row, turned), work)
     image, pay = call(
         image_sums, [own, sums], (in_group(partial), left, left_one, beta_one), [square]
     )

time: 204 us -> 201 us (0.985)
  Pallas kernels: 29 us -> 26.1 us
    pallas_call x15, Pallas kernels: 29 us -> 26.1 us  [call(): pl.pallas_call(body, out_shape=shapes, in_specs=in_specs or [VMEM] * len(...]
where the time goes in v5:
time: 201 us
  blocking collectives  156 us (78%)
  Pallas kernels  26.1 us (13%)
  starting transfers between devices  11.5 us (6%)
  waiting for transfers between devices  5.78 us (3%)
    all_to_all x8, blocking collectives, to_all(): return lax.all_to_all(value, SEND_ALL, 0, 0, tiled=True)  122 us
    all_to_all x4, blocking collectives, in_group(): return lax.all_to_all(value, SEND_COL, 0, 0, tiled=True)  33.2 us
    pallas_call x15, Pallas kernels, call(): pl.pallas_call(body, out_shape=shapes, in_specs=in_specs or [VMEM] * len(...  26.1 us
    all_to_all x1, starting transfers between devices, to_all(): return lax.all_to_all(value, SEND_ALL, 0, 0, tiled=True)  11.5 us
    all_to_all x1, waiting for transfers between devices, to_all(): return lax.all_to_all(value, SEND_ALL, 0, 0, tiled=True)  5.78 us
  transfers between devices with their start and end apart: 1, of which 1 were waited for; matrix products, arithmetic and copies ran while one was open for 0% of the time, Pallas kernels for 2%

profile of v5, /device:TPU:1, one launch (start us, length us, event | category | flops | bytes accessed | tf_op | source)
XLA Modules:
  0.0 200.6 jit_solution(10161125932365098365)
XLA Ops:
  0.6 2.4 %shard_map.94 = (f32[128,1,128]{2,1,0:T(1,128)}, bf16[32,128]{1,0:T(8,128)(2,1)S(1)}, s32[1,512]{1,0:T(1,128)S(1)}, f32[32,128]{1,0:T(8,128)S(1)}, f32[100,4096]{1,0:T(8,128)S(1)}) custom-call(s32[1,512]{1,0:T(1,128)} %bitcast.12, f32[100,4096]{1,0:T(8,128)} %basis_hbm.1, f32[32,128]{1,0:T(8,128)} %bitcast.11), custom_call_target="tpu_custom_call" | custom-call | tf_op jit(solution)/shard_map/pallas_call | solution.py:368
  3.1 11.5 %all-to-all-start = ((f32[128,1,128]{2,1,0:T(1,128)}), f32[128,1,128]{2,1,0:T(1,128)S(1)}, u32[]{:S(2)}, u32[]{:S(2)}) async-start(f32[128,1,128]{2,1,0:T(1,128)} %get-tuple-element.43), calls=%async_computation | async-start | bytes 131072 | tf_op jit(solution)/shard_map/all_to_all | solution.py:380
  15.2 3.1 %shard_map.95 = (s32[1,512]{1,0:T(1,128)S(1)}, s32[512,1]{1,0:T(8,128)S(1)}, s32[1,512]{1,0:T(1,128)S(1)}, s32[512,1]{1,0:T(8,128)S(1)}, f32[128,128]{1,0:T(8,128)S(1)}, /*index=5*/f32[128,128]{1,0:T(8,128)S(1)}) custom-call(s32[1]{0:T(128)S(6)} %copy.10.counts, bf16[32,128]{1,0:T(8,128)(2,1)S(1)} %get-tuple-element.46.rank, ...), custom_call_target="tpu_custom_call" | custom-call | tf_op jit(solution)/shard_map/pallas_call | solution.py:368
  18.3 5.8 %all-to-all-done.arrived = f32[128,1,128]{2,1,0:T(1,128)S(1)} async-done(((f32[128,1,128]{2,1,0:T(1,128)}), f32[128,1,128]{2,1,0:T(1,128)S(1)}, u32[]{:S(2)}, u32[]{:S(2)}) %all-to-all-start) | async-done | bytes 65568 | tf_op jit(solution)/shard_map/all_to_all | solution.py:380
  24.1 0.0 copy-start
  24.1 0.9 shard_map.96
  25.0 18.1 %all_to_all.65 = f32[128,9,1,128]{3,2,1,0:T(1,128)S(1)} all-to-all(f32[128,9,1,128]{3,2,1,0:T(1,128)S(1)} %get-tuple-element.50), channel_id=1, replica_groups=mesh['row_0'=4,'row_1'=4,'col_0'=4,'col_1'=2] {'col_1','col_0','row_1','..., dimensions={0} | all-to-all | bytes 1179648 | tf_op jit(solution)/shard_map/all_to_all | solution.py:380
  43.1 0.0 copy-done
  43.1 5.0 %shard_map.97 = (f32[8,32,128]{2,1,0:T(8,128)S(1)}, f32[1,128]{1,0:T(1,128)S(1)}, f32[1,128]{1,0:T(1,128)S(1)}, bf16[512,128,128]{2,1,0:T(8,128)(2,1)S(1)}) custom-call(f32[1152,128]{1,0:T(8,128)S(1)} %bitcast.10, s32[512,1]{1,0:T(8,128)S(1)} %get-tuple-element.51.pos_col, s32[1,512]{1,0:T(1,128)S(1)} %get-tuple-element.52.row_row, ...), custom_call_target="tpu_custom_call" | custom-call | tf_op jit(solution)/shard_map/pallas_call | solution.py:368
  48.1 8.4 %all_to_all.66.arrived = f32[8,32,128]{2,1,0:T(8,128)S(1)} all-to-all(f32[8,32,128]{2,1,0:T(8,128)S(1)} %get-tuple-element.53), channel_id=1, replica_groups=mesh['row_0'=4,'row_1'=4,'col_0'=4,'col_1'=2] {'col_1','col_0'}, dimensions={0} | all-to-all | bytes 262144 | tf_op jit(solution)/shard_map/all_to_all | solution.py:384
  56.5 0.0 copy-done.1
  56.5 0.4 shard_map.98
  56.9 14.3 %all_to_all.67.arrived = f32[128,1,256]{2,1,0:T(1,128)S(1)} all-to-all(f32[128,1,256]{2,1,0:T(1,128)S(1)} %get-tuple-element.55), channel_id=1, replica_groups=mesh['row_0'=4,'row_1'=4,'col_0'=4,'col_1'=2] {'col_1','col_0','row_1','..., dimensions={0} | all-to-all | bytes 262144 | tf_op jit(solution)/shard_map/all_to_all | solution.py:380
  71.2 0.3 shard_map.99
  71.5 8.1 %all_to_all.68.arrived = bf16[8,32,128]{2,1,0:T(8,128)(2,1)S(1)} all-to-all(bf16[8,32,128]{2,1,0:T(8,128)(2,1)S(1)} %get-tuple-element.57), channel_id=1, replica_groups=mesh['row_0'=4,'row_1'=4,'col_0'=4,'col_1'=2] {'col_1','col_0'}, dimensions={0} | all-to-all | bytes 131072 | tf_op jit(solution)/shard_map/all_to_all | solution.py:384
  79.6 3.5 %shard_map.100 = f32[128,8,128]{2,1,0:T(8,128)S(1)} custom-call(bf16[8,32,128]{2,1,0:T(8,128)(2,1)S(1)} %all_to_all.68.arrived, s32[512,1]{1,0:T(8,128)S(1)} %get-tuple-element.58.row_col, s32[1,512]{1,0:T(1,128)S(1)} %get-tuple-element.59.pos_row, bf16[512,128,128]{2,1,0:T(8,128)(2,1)S(1)} %copy-done), custom_call_target="tpu_custom_call" | custom-call | tf_op jit(solution)/shard_map/pallas_call | solution.py:368
  83.1 17.3 %all_to_all.69.arrived = f32[128,8,128]{2,1,0:T(8,128)S(1)} all-to-all(f32[128,8,128]{2,1,0:T(8,128)S(1)} %shard_map.100), channel_id=1, replica_groups=mesh['row_0'=4,'row_1'=4,'col_0'=4,'col_1'=2] {'col_1','col_0','row_1','..., dimensions={0} | all-to-all | bytes 1048576 | tf_op jit(solution)/shard_map/all_to_all | solution.py:380
  100.4 0.6 shard_map.101
  101.1 13.5 %all_to_all.70.arrived = f32[128,1,128]{2,1,0:T(1,128)S(1)} all-to-all(f32[128,1,128]{2,1,0:T(1,128)S(1)} %get-tuple-element.64), channel_id=1, replica_groups=mesh['row_0'=4,'row_1'=4,'col_0'=4,'col_1'=2] {'col_1','col_0','row_1','..., dimensions={0} | all-to-all | bytes 131072 | tf_op jit(solution)/shard_map/all_to_all | solution.py:380
  114.6 0.5 shard_map.102
  115.1 14.7 %all_to_all.71.arrived = bf16[128,8,128]{2,1,0:T(8,128)(2,1)S(1)} all-to-all(bf16[128,8,128]{2,1,0:T(8,128)(2,1)S(1)} %get-tuple-element.67), channel_id=1, replica_groups=mesh['row_0'=4,'row_1'=4,'col_0'=4,'col_1'=2] {'col_1','col_0','row_1','..., dimensions={0} | all-to-all | bytes 524288 | tf_op jit(solution)/shard_map/all_to_all | solution.py:380
  129.8 3.6 %shard_map.103 = f32[8,32,128]{2,1,0:T(8,128)S(1)} custom-call(bf16[128,8,128]{2,1,0:T(8,128)(2,1)S(1)} %all_to_all.71.arrived, s32[512,1]{1,0:T(8,128)S(1)} %get-tuple-element.51.pos_col, s32[1,512]{1,0:T(1,128)S(1)} %get-tuple-element.52.row_row, bf16[512,128,128]{2,1,0:T(8,128)(2,1)S(1)} %get-tuple-element.68.tiles), custom_call_target="tpu_custom_call" | custom-call | tf_op jit(solution)/shard_map/pallas_call | solution.py:368
  133.4 8.4 %all_to_all.72.arrived = f32[8,32,128]{2,1,0:T(8,128)S(1)} all-to-all(f32[8,32,128]{2,1,0:T(8,128)S(1)} %shard_map.103), channel_id=1, replica_groups=mesh['row_0'=4,'row_1'=4,'col_0'=4,'col_1'=2] {'col_1','col_0'}, dimensions={0} | all-to-all | bytes 262144 | tf_op jit(solution)/shard_map/all_to_all | solution.py:384
  141.8 0.4 shard_map.104
  142.2 13.7 %all_to_all.73.arrived = f32[128,1,128]{2,1,0:T(1,128)S(1)} all-to-all(f32[128,1,128]{2,1,0:T(1,128)S(1)} %get-tuple-element.71), channel_id=1, replica_groups=mesh['row_0'=4,'row_1'=4,'col_0'=4,'col_1'=2] {'col_1','col_0','row_1','..., dimensions={0} | all-to-all | bytes 131072 | tf_op jit(solution)/shard_map/all_to_all | solution.py:380
  155.9 0.3 shard_map.105
  156.2 8.3 %all_to_all.74.arrived = bf16[8,32,128]{2,1,0:T(8,128)(2,1)S(1)} all-to-all(bf16[8,32,128]{2,1,0:T(8,128)(2,1)S(1)} %get-tuple-element.74), channel_id=1, replica_groups=mesh['row_0'=4,'row_1'=4,'col_0'=4,'col_1'=2] {'col_1','col_0'}, dimensions={0} | all-to-all | bytes 131072 | tf_op jit(solution)/shard_map/all_to_all | solution.py:384
  164.5 3.5 %shard_map.106 = f32[128,8,128]{2,1,0:T(8,128)S(1)} custom-call(bf16[8,32,128]{2,1,0:T(8,128)(2,1)S(1)} %all_to_all.74.arrived, s32[512,1]{1,0:T(8,128)S(1)} %get-tuple-element.58.row_col, s32[1,512]{1,0:T(1,128)S(1)} %get-tuple-element.59.pos_row, bf16[512,128,128]{2,1,0:T(8,128)(2,1)S(1)} %copy-done), custom_call_target="tpu_custom_call" | custom-call | tf_op jit(solution)/shard_map/pallas_call | solution.py:368
  168.0 17.3 %all_to_all.75.arrived = f32[128,8,128]{2,1,0:T(8,128)S(1)} all-to-all(f32[128,8,128]{2,1,0:T(8,128)S(1)} %shard_map.106), channel_id=1, replica_groups=mesh['row_0'=4,'row_1'=4,'col_0'=4,'col_1'=2] {'col_1','col_0','row_1','..., dimensions={0} | all-to-all | bytes 1048576 | tf_op jit(solution)/shard_map/all_to_all | solution.py:380
  185.3 0.6 shard_map.107
  185.9 13.5 %all_to_all.76.arrived = f32[128,1,128]{2,1,0:T(1,128)S(1)} all-to-all(f32[128,1,128]{2,1,0:T(1,128)S(1)} %get-tuple-element.77), channel_id=1, replica_groups=mesh['row_0'=4,'row_1'=4,'col_0'=4,'col_1'=2] {'col_1','col_0','row_1','..., dimensions={0} | all-to-all | bytes 131072 | tf_op jit(solution)/shard_map/all_to_all | solution.py:380
  199.5 0.9 shard_map.108
  (1 shorter events, 0.0 us)
Async XLA Ops:
  3.1 21.0 %all-to-all-start = ((f32[128,1,128]{2,1,0:T(1,128)}), f32[128,1,128]{2,1,0:T(1,128)S(1)}, u32[]{:S(2)}, u32[]{:S(2)}) async-start(f32[128,1,128]{2,1,0:T(1,128)} %get-tuple-element.43), calls=%async_computation | async-start | bytes 131072 | tf_op jit(solution)/shard_map/all_to_all | solution.py:380
  24.1 19.0 %copy-start = (bf16[512,128,128]{2,1,0:T(8,128)(2,1)S(1)}, bf16[512,128,128]{2,1,0:T(8,128)(2,1)}, u32[]{:S(2)}) copy-start(bf16[512,128,128]{2,1,0:T(8,128)(2,1)} %tiles.5) | copy-start | bytes 50331652
  43.1 13.4 %copy-start.1 = (f32[100,4096]{1,0:T(8,128)S(1)}, f32[100,4096]{1,0:T(8,128)}, u32[]{:S(2)}) copy-start(f32[100,4096]{1,0:T(8,128)} %basis.7) | copy-start | bytes 4915204

commit v6 on v5

--- a/solution.py
+++ b/solution.py
@@ -68,7 +68,7 @@
         total = total + basis[:, k * TILE : (k + 1) * TILE] * vector[k : k + 1, :]
     held[...] = jnp.zeros_like(held)
     held[0:size, :] = total
-    row = dot(jnp.ones((8, TILE), F32), held[...], 1, 1, HIGH)[0:1, :]
+    row = jnp.sum(held[...].T, axis=0, keepdims=True)
     square = jnp.sum(vector * vector, keepdims=True)
     return jnp.where(iota((1, TILE), 1) == size, square, row)
 
@@ -143,22 +143,23 @@
 
 def tables(counts, rank, col_row, right, row_hbm, left_hbm, *refs):
     pos_row, pos_col, row_row, row_col, gram_r, gram_l, left, given_row, sems = refs
-    copies = [
-        pltpu.make_async_copy(left_hbm, left, sems.at[0]),
-        pltpu.make_async_copy(row_hbm, given_row, sems.at[1]),
+    wide = left.shape[1] // PARTS
+    parts = [pl.ds(i * wide, wide) for i in range(PARTS)]
+    copies = [pltpu.make_async_copy(row_hbm, given_row, sems.at[PARTS])]
+    copies += [
+        pltpu.make_async_copy(left_hbm.at[:, part], left.at[:, part], sems.at[i])
+        for i, part in enumerate(parts)
     ]
     for copy in copies:
         copy.start()
-    for basis, gram in ((right, gram_r), (left, gram_l)):
-        if basis is left:
-            copies[0].wait()
-        size = basis.shape[0]
-        gram[...] = jnp.zeros_like(gram)
-        gram[0:size, 0:size] = gram_of(basis)
-    copies[1].wait()
+    gram_r[...] = jnp.zeros_like(gram_r)
+    gram_l[...] = jnp.zeros_like(gram_l)
+    size = right.shape[0]
+    gram_r[0:size, 0:size] = gram_of(right)
+    copies[0].wait()
     row = group_row_of(given_row[...])
     row_row[...] = row
-    count = counts[0]
+    count = counts[...]
     owner, place = block_of(col_row[...] // OWN), col_row[...] % OWN
     owners = one_hot(iota((DEV, SLOTS), 0) == owner)
     mine = dot(rank[...], owners)
@@ -170,6 +171,9 @@
     columns = both.astype(F32).T.astype(I32)
     pos_col[...] = columns[:, 0:1]
     row_col[...] = columns[:, 1:2]
+    for copy in copies[1:]:
+        copy.wait()
+    gram_l[0:size, 0:size] = gram_of(left)
 
 
 def place_row_of(arrived):
@@ -411,10 +415,10 @@
     pos_row, pos_col, row_row, row_col, gram_r, gram_l = call(
         tables,
         [((1, SLOTS), I32), ((SLOTS, 1), I32)] * 2 + [square, square],
-        (counts, rank, col_row, right, row_row, left),
+        (counts.reshape(1, 1), rank, col_row, right, row_row, left),
         [(left.shape, F32), ((1, SLOTS), I32)],
-        in_specs=[SMEM] + [VMEM] * 3 + [HBM] * 2,
-        semaphores=2,
+        in_specs=[VMEM] * 4 + [HBM] * 2,
+        semaphores=PARTS + 1,
     )
     rest, send, place_row = call(
         with_total(first_vector),

time: 201 us -> 201 us (level)
  no operation moved by 1% of the time
where the time goes in v6:
time: 201 us; the launch traced here: 200 us
  blocking collectives  156 us (78%)
  Pallas kernels  25.8 us (13%)
  starting transfers between devices  11.5 us (6%)
  waiting for transfers between devices  5.47 us (3%)
    all_to_all x8, blocking collectives, to_all(): return lax.all_to_all(value, SEND_ALL, 0, 0, tiled=True)  123 us
    all_to_all x4, blocking collectives, in_group(): return lax.all_to_all(value, SEND_COL, 0, 0, tiled=True)  33.2 us
    pallas_call x15, Pallas kernels, call(): pl.pallas_call(body, out_shape=shapes, in_specs=in_specs or [VMEM] * len(...  25.8 us
    all_to_all x1, starting transfers between devices, to_all(): return lax.all_to_all(value, SEND_ALL, 0, 0, tiled=True)  11.5 us
    all_to_all x1, waiting for transfers between devices, to_all(): return lax.all_to_all(value, SEND_ALL, 0, 0, tiled=True)  5.47 us
  transfers between devices with their start and end apart: 1, of which 1 were waited for; matrix products, arithmetic and copies ran while one was open for 0% of the time, Pallas kernels for 2%

profile of v6, /device:TPU:1, one launch (start us, length us, event | category | flops | bytes accessed | tf_op | source)
XLA Modules:
  0.0 200.2 jit_solution(1666931994346982626)
XLA Ops:
  0.6 2.3 %shard_map.94 = (f32[128,1,128]{2,1,0:T(1,128)}, bf16[32,128]{1,0:T(8,128)(2,1)S(1)}, s32[1,512]{1,0:T(1,128)S(1)}, f32[32,128]{1,0:T(8,128)S(1)}, f32[100,4096]{1,0:T(8,128)S(1)}) custom-call(s32[1,512]{1,0:T(1,128)} %bitcast.14, f32[100,4096]{1,0:T(8,128)} %basis_hbm.1, f32[32,128]{1,0:T(8,128)} %bitcast.13), custom_call_target="tpu_custom_call" | custom-call | tf_op jit(solution)/shard_map/pallas_call | solution.py:372
  2.9 11.5 %all-to-all-start = ((f32[128,1,128]{2,1,0:T(1,128)}), f32[128,1,128]{2,1,0:T(1,128)S(1)}, u32[]{:S(2)}, u32[]{:S(2)}) async-start(f32[128,1,128]{2,1,0:T(1,128)} %get-tuple-element.43), calls=%async_computation | async-start | bytes 131072 | tf_op jit(solution)/shard_map/all_to_all | solution.py:384
  15.1 3.4 %shard_map.95 = (s32[1,512]{1,0:T(1,128)S(1)}, s32[512,1]{1,0:T(8,128)S(1)}, s32[1,512]{1,0:T(1,128)S(1)}, s32[512,1]{1,0:T(8,128)S(1)}, f32[128,128]{1,0:T(8,128)S(1)}, /*index=5*/f32[128,128]{1,0:T(8,128)S(1)}) custom-call(s32[1,1]{1,0:T(1,128)} %bitcast.11.counts, bf16[32,128]{1,0:T(8,128)(2,1)S(1)} %get-tuple-element.46.rank, ...), custom_call_target="tpu_custom_call" | custom-call | tf_op jit(solution)/shard_map/pallas_call | solution.py:372
  18.5 5.5 %all-to-all-done.arrived = f32[128,1,128]{2,1,0:T(1,128)S(1)} async-done(((f32[128,1,128]{2,1,0:T(1,128)}), f32[128,1,128]{2,1,0:T(1,128)S(1)}, u32[]{:S(2)}, u32[]{:S(2)}) %all-to-all-start) | async-done | bytes 65568 | tf_op jit(solution)/shard_map/all_to_all | solution.py:384
  23.9 0.0 copy-start
  23.9 0.9 shard_map.96
  24.9 18.3 %all_to_all.65 = f32[128,9,1,128]{3,2,1,0:T(1,128)S(1)} all-to-all(f32[128,9,1,128]{3,2,1,0:T(1,128)S(1)} %get-tuple-element.50), channel_id=1, replica_groups=mesh['row_0'=4,'row_1'=4,'col_0'=4,'col_1'=2] {'col_1','col_0','row_1','..., dimensions={0} | all-to-all | bytes 1179648 | tf_op jit(solution)/shard_map/all_to_all | solution.py:384
  43.2 0.0 copy-done
  43.2 5.0 %shard_map.97 = (f32[8,32,128]{2,1,0:T(8,128)S(1)}, f32[1,128]{1,0:T(1,128)S(1)}, f32[1,128]{1,0:T(1,128)S(1)}, bf16[512,128,128]{2,1,0:T(8,128)(2,1)S(1)}) custom-call(f32[1152,128]{1,0:T(8,128)S(1)} %bitcast.12, s32[512,1]{1,0:T(8,128)S(1)} %get-tuple-element.51.pos_col, s32[1,512]{1,0:T(1,128)S(1)} %get-tuple-element.52.row_row, ...), custom_call_target="tpu_custom_call" | custom-call | tf_op jit(solution)/shard_map/pallas_call | solution.py:372
  48.2 8.3 %all_to_all.66.arrived = f32[8,32,128]{2,1,0:T(8,128)S(1)} all-to-all(f32[8,32,128]{2,1,0:T(8,128)S(1)} %get-tuple-element.53), channel_id=1, replica_groups=mesh['row_0'=4,'row_1'=4,'col_0'=4,'col_1'=2] {'col_1','col_0'}, dimensions={0} | all-to-all | bytes 262144 | tf_op jit(solution)/shard_map/all_to_all | solution.py:388
  56.6 0.0 copy-done.1
  56.6 0.3 shard_map.98
  56.9 14.3 %all_to_all.67.arrived = f32[128,1,256]{2,1,0:T(1,128)S(1)} all-to-all(f32[128,1,256]{2,1,0:T(1,128)S(1)} %get-tuple-element.55), channel_id=1, replica_groups=mesh['row_0'=4,'row_1'=4,'col_0'=4,'col_1'=2] {'col_1','col_0','row_1','..., dimensions={0} | all-to-all | bytes 262144 | tf_op jit(solution)/shard_map/all_to_all | solution.py:384
  71.2 0.3 shard_map.99
  71.5 8.1 %all_to_all.68.arrived = bf16[8,32,128]{2,1,0:T(8,128)(2,1)S(1)} all-to-all(bf16[8,32,128]{2,1,0:T(8,128)(2,1)S(1)} %get-tuple-element.57), channel_id=1, replica_groups=mesh['row_0'=4,'row_1'=4,'col_0'=4,'col_1'=2] {'col_1','col_0'}, dimensions={0} | all-to-all | bytes 131072 | tf_op jit(solution)/shard_map/all_to_all | solution.py:388
  79.6 3.5 %shard_map.100 = f32[128,8,128]{2,1,0:T(8,128)S(1)} custom-call(bf16[8,32,128]{2,1,0:T(8,128)(2,1)S(1)} %all_to_all.68.arrived, s32[512,1]{1,0:T(8,128)S(1)} %get-tuple-element.58.row_col, s32[1,512]{1,0:T(1,128)S(1)} %get-tuple-element.59.pos_row, bf16[512,128,128]{2,1,0:T(8,128)(2,1)S(1)} %copy-done), custom_call_target="tpu_custom_call" | custom-call | tf_op jit(solution)/shard_map/pallas_call | solution.py:372
  83.1 17.3 %all_to_all.69.arrived = f32[128,8,128]{2,1,0:T(8,128)S(1)} all-to-all(f32[128,8,128]{2,1,0:T(8,128)S(1)} %shard_map.100), channel_id=1, replica_groups=mesh['row_0'=4,'row_1'=4,'col_0'=4,'col_1'=2] {'col_1','col_0','row_1','..., dimensions={0} | all-to-all | bytes 1048576 | tf_op jit(solution)/shard_map/all_to_all | solution.py:384
  100.4 0.5 shard_map.101
  100.9 13.5 %all_to_all.70.arrived = f32[128,1,128]{2,1,0:T(1,128)S(1)} all-to-all(f32[128,1,128]{2,1,0:T(1,128)S(1)} %get-tuple-element.64), channel_id=1, replica_groups=mesh['row_0'=4,'row_1'=4,'col_0'=4,'col_1'=2] {'col_1','col_0','row_1','..., dimensions={0} | all-to-all | bytes 131072 | tf_op jit(solution)/shard_map/all_to_all | solution.py:384
  114.5 0.5 shard_map.102
  115.0 14.7 %all_to_all.71.arrived = bf16[128,8,128]{2,1,0:T(8,128)(2,1)S(1)} all-to-all(bf16[128,8,128]{2,1,0:T(8,128)(2,1)S(1)} %get-tuple-element.67), channel_id=1, replica_groups=mesh['row_0'=4,'row_1'=4,'col_0'=4,'col_1'=2] {'col_1','col_0','row_1','..., dimensions={0} | all-to-all | bytes 524288 | tf_op jit(solution)/shard_map/all_to_all | solution.py:384
  129.7 3.5 %shard_map.103 = f32[8,32,128]{2,1,0:T(8,128)S(1)} custom-call(bf16[128,8,128]{2,1,0:T(8,128)(2,1)S(1)} %all_to_all.71.arrived, s32[512,1]{1,0:T(8,128)S(1)} %get-tuple-element.51.pos_col, s32[1,512]{1,0:T(1,128)S(1)} %get-tuple-element.52.row_row, bf16[512,128,128]{2,1,0:T(8,128)(2,1)S(1)} %get-tuple-element.68.tiles), custom_call_target="tpu_custom_call" | custom-call | tf_op jit(solution)/shard_map/pallas_call | solution.py:372
  133.2 8.4 %all_to_all.72.arrived = f32[8,32,128]{2,1,0:T(8,128)S(1)} all-to-all(f32[8,32,128]{2,1,0:T(8,128)S(1)} %shard_map.103), channel_id=1, replica_groups=mesh['row_0'=4,'row_1'=4,'col_0'=4,'col_1'=2] {'col_1','col_0'}, dimensions={0} | all-to-all | bytes 262144 | tf_op jit(solution)/shard_map/all_to_all | solution.py:388
  141.7 0.3 shard_map.104
  142.0 13.7 %all_to_all.73.arrived = f32[128,1,128]{2,1,0:T(1,128)S(1)} all-to-all(f32[128,1,128]{2,1,0:T(1,128)S(1)} %get-tuple-element.71), channel_id=1, replica_groups=mesh['row_0'=4,'row_1'=4,'col_0'=4,'col_1'=2] {'col_1','col_0','row_1','..., dimensions={0} | all-to-all | bytes 131072 | tf_op jit(solution)/shard_map/all_to_all | solution.py:384
  155.6 0.3 shard_map.105
  156.0 8.3 %all_to_all.74.arrived = bf16[8,32,128]{2,1,0:T(8,128)(2,1)S(1)} all-to-all(bf16[8,32,128]{2,1,0:T(8,128)(2,1)S(1)} %get-tuple-element.74), channel_id=1, replica_groups=mesh['row_0'=4,'row_1'=4,'col_0'=4,'col_1'=2] {'col_1','col_0'}, dimensions={0} | all-to-all | bytes 131072 | tf_op jit(solution)/shard_map/all_to_all | solution.py:388
  164.2 3.5 %shard_map.106 = f32[128,8,128]{2,1,0:T(8,128)S(1)} custom-call(bf16[8,32,128]{2,1,0:T(8,128)(2,1)S(1)} %all_to_all.74.arrived, s32[512,1]{1,0:T(8,128)S(1)} %get-tuple-element.58.row_col, s32[1,512]{1,0:T(1,128)S(1)} %get-tuple-element.59.pos_row, bf16[512,128,128]{2,1,0:T(8,128)(2,1)S(1)} %copy-done), custom_call_target="tpu_custom_call" | custom-call | tf_op jit(solution)/shard_map/pallas_call | solution.py:372
  167.7 17.3 %all_to_all.75.arrived = f32[128,8,128]{2,1,0:T(8,128)S(1)} all-to-all(f32[128,8,128]{2,1,0:T(8,128)S(1)} %shard_map.106), channel_id=1, replica_groups=mesh['row_0'=4,'row_1'=4,'col_0'=4,'col_1'=2] {'col_1','col_0','row_1','..., dimensions={0} | all-to-all | bytes 1048576 | tf_op jit(solution)/shard_map/all_to_all | solution.py:384
  185.0 0.5 shard_map.107
  185.5 13.5 %all_to_all.76.arrived = f32[128,1,128]{2,1,0:T(1,128)S(1)} all-to-all(f32[128,1,128]{2,1,0:T(1,128)S(1)} %get-tuple-element.77), channel_id=1, replica_groups=mesh['row_0'=4,'row_1'=4,'col_0'=4,'col_1'=2] {'col_1','col_0','row_1','..., dimensions={0} | all-to-all | bytes 131072 | tf_op jit(solution)/shard_map/all_to_all | solution.py:384
  199.1 0.9 shard_map.108
  (1 shorter events, 0.0 us)
Async XLA Ops:
  2.9 21.0 %all-to-all-start = ((f32[128,1,128]{2,1,0:T(1,128)}), f32[128,1,128]{2,1,0:T(1,128)S(1)}, u32[]{:S(2)}, u32[]{:S(2)}) async-start(f32[128,1,128]{2,1,0:T(1,128)} %get-tuple-element.43), calls=%async_computation | async-start | bytes 131072 | tf_op jit(solution)/shard_map/all_to_all | solution.py:384
  23.9 19.2 %copy-start = (bf16[512,128,128]{2,1,0:T(8,128)(2,1)S(1)}, bf16[512,128,128]{2,1,0:T(8,128)(2,1)}, u32[]{:S(2)}) copy-start(bf16[512,128,128]{2,1,0:T(8,128)(2,1)} %tiles.5) | copy-start | bytes 50331652
  43.2 13.4 %copy-start.1 = (f32[100,4096]{1,0:T(8,128)S(1)}, f32[100,4096]{1,0:T(8,128)}, u32[]{:S(2)}) copy-start(f32[100,4096]{1,0:T(8,128)} %basis.7) | copy-start | bytes 4915204

commit v7 on v6

--- a/solution.py
+++ b/solution.py
@@ -99,13 +99,17 @@
     return jnp.sqrt(left / row_total + 1e-06)
 
 
-def first_sums(col_hbm, basis_hbm, start_hbm, out, rank, col_row, start, basis, held, sems):
+def first_sums(col_hbm, row_hbm, basis_hbm, start_hbm, out, pos_row, pos_col, row_row, *refs):
+    row_col, start, basis, held, listed, col_row, given_row, sems = refs
     wide = basis.shape[1] // PARTS
     parts = [pl.ds(i * wide, wide) for i in range(PARTS)]
-    copies = [pltpu.make_async_copy(col_hbm, col_row, sems.at[0])]
-    copies += [pltpu.make_async_copy(start_hbm, start, sems.at[1])]
+    copies = [
+        pltpu.make_async_copy(col_hbm, col_row, sems.at[0]),
+        pltpu.make_async_copy(row_hbm, given_row, sems.at[1]),
+        pltpu.make_async_copy(start_hbm, start, sems.at[2]),
+    ]
     copies += [
-        pltpu.make_async_copy(basis_hbm.at[:, part], basis.at[:, part], sems.at[2 + i])
+        pltpu.make_async_copy(basis_hbm.at[:, part], basis.at[:, part], sems.at[3 + i])
         for i, part in enumerate(parts)
     ]
     for copy in copies:
@@ -113,20 +117,29 @@
     copies[0].wait()
     owner, place = block_of(col_row[...] // OWN), col_row[...] % OWN
     owners = one_hot(iota((DEV, SLOTS), 0) == owner)
-    places = one_hot(iota((OWN, SLOTS), 0) == place)
-    touched = dot(places, owners, 1, 1) > 0.5
+    in_place = iota((OWN, SLOTS), 0) == place
+    touched = dot(one_hot(in_place), owners, 1, 1) > 0.5
     below = one_hot(iota((OWN, OWN), 1) < iota((OWN, OWN), 0))
-    places = dot(below, one_hot(touched))
-    rank[...] = places.astype(BF16)
-    copies[1].wait()
-    row = products_row(basis, start[...], held, copies[2:])
-    held[...] = jnp.zeros_like(held)
+    rank = dot(below, one_hot(touched))
+    listed[...] = jnp.zeros_like(listed)
     number = (iota((OWN, DEV), 0) + 1).astype(F32)
     for k in range(PEER_TILES):
-        here = touched & (places > k - 0.5) & (places < k + 0.5)
+        here = touched & (rank > k - 0.5) & (rank < k + 0.5)
         named = jnp.sum(jnp.where(here, number, 0.0), axis=0, keepdims=True)
-        held[PLACE + k : PLACE + k + 1, :] = named - 1.0
-    out[:, 0, :] = held[...].T + row
+        listed[PLACE + k : PLACE + k + 1, :] = named - 1.0
+    places = listed[...].T
+    mine = jnp.where(in_place, dot(rank.astype(BF16), owners), 0.0)
+    position = owner * PEER_TILES + jnp.sum(mine, axis=0, keepdims=True).astype(I32)
+    pos_row[...] = position
+    copies[1].wait()
+    row = group_row_of(given_row[...])
+    row_row[...] = row
+    both = jnp.where(iota((8, SLOTS), 0) == 0, position, row)
+    columns = both.astype(F32).T.astype(I32)
+    pos_col[...] = columns[:, 0:1]
+    row_col[...] = columns[:, 1:2]
+    copies[2].wait()
+    out[:, 0, :] = places + products_row(basis, start[...], held, copies[3:])
 
 
 def gram_of(basis):
@@ -141,39 +154,17 @@
     return dot(second, second, 1, 1) + (both + both.T) + dot(first, first, 1, 1)
 
 
-def tables(counts, rank, col_row, right, row_hbm, left_hbm, *refs):
-    pos_row, pos_col, row_row, row_col, gram_r, gram_l, left, given_row, sems = refs
-    wide = left.shape[1] // PARTS
-    parts = [pl.ds(i * wide, wide) for i in range(PARTS)]
-    copies = [pltpu.make_async_copy(row_hbm, given_row, sems.at[PARTS])]
-    copies += [
-        pltpu.make_async_copy(left_hbm.at[:, part], left.at[:, part], sems.at[i])
-        for i, part in enumerate(parts)
-    ]
-    for copy in copies:
-        copy.start()
+def tables(counts, all_row, all_col, right, left_hbm, pos_row, pos_col, gram_r, gram_l, left, sems):
+    copy = pltpu.make_async_copy(left_hbm, left, sems.at[0])
+    copy.start()
+    size = right.shape[0]
     gram_r[...] = jnp.zeros_like(gram_r)
     gram_l[...] = jnp.zeros_like(gram_l)
-    size = right.shape[0]
     gram_r[0:size, 0:size] = gram_of(right)
-    copies[0].wait()
-    row = group_row_of(given_row[...])
-    row_row[...] = row
-    count = counts[...]
-    owner, place = block_of(col_row[...] // OWN), col_row[...] % OWN
-    owners = one_hot(iota((DEV, SLOTS), 0) == owner)
-    mine = dot(rank[...], owners)
-    mine = jnp.where(iota((OWN, SLOTS), 0) == place, mine, 0.0)
-    position = owner * PEER_TILES + jnp.sum(mine, axis=0, keepdims=True).astype(I32)
-    position = jnp.where(iota((1, SLOTS), 1) < count, position, -1)
-    pos_row[...] = position
-    both = jnp.where(iota((8, SLOTS), 0) == 0, position, row)
-    columns = both.astype(F32).T.astype(I32)
-    pos_col[...] = columns[:, 0:1]
-    row_col[...] = columns[:, 1:2]
-    for copy in copies[1:]:
-        copy.wait()
+    copy.wait()
     gram_l[0:size, 0:size] = gram_of(left)
+    pos_row[...] = jnp.where(iota((1, SLOTS), 1) < counts[...], all_row[...], -1)
+    pos_col[...] = jnp.where(iota((SLOTS, 1), 0) < counts[...], all_col[...], -1)
 
 
 def place_row_of(arrived):
@@ -403,22 +394,23 @@
     begin = start.reshape(OWN, TILE)
     col_row, row_row = col_tiles.reshape(1, SLOTS), row_tiles.reshape(1, SLOTS)
 
-    pay, rank, col_row, begin, right = call(
+    indices = [((1, SLOTS), I32), ((SLOTS, 1), I32)]
+    pay, all_row, all_col, row_row, row_col, begin, right = call(
         first_sums,
-        [sums, ((OWN, DEV), BF16), ((1, SLOTS), I32), own, (right.shape, F32)],
-        (col_row, right, begin),
-        [square],
-        in_specs=[HBM] * 3,
-        semaphores=2 + PARTS,
+        [sums, *indices, *indices, own, (right.shape, F32)],
+        (col_row, row_row, right, begin),
+        [square, square, indices[0], indices[0]],
+        in_specs=[HBM] * 4,
+        semaphores=3 + PARTS,
     )
     arrived = to_all(pay)
-    pos_row, pos_col, row_row, row_col, gram_r, gram_l = call(
+    pos_row, pos_col, gram_r, gram_l = call(
         tables,
-        [((1, SLOTS), I32), ((SLOTS, 1), I32)] * 2 + [square, square],
-        (counts.reshape(1, 1), rank, col_row, right, row_row, left),
-        [(left.shape, F32), ((1, SLOTS), I32)],
-        in_specs=[VMEM] * 4 + [HBM] * 2,
-        semaphores=PARTS + 1,
+        [*indices, square, square],
+        (counts.reshape(1, 1), all_row, all_col, right, left),
+        [(left.shape, F32)],
+        in_specs=[VMEM] * 4 + [HBM],
+        semaphores=1,
     )
     rest, send, place_row = call(
         with_total(first_vector),

time: 201 us -> 201 us (level)
  transfers between devices with their start and end apart: 1 -> 1, of which waited for: 1 -> 1; matrix products, arithmetic and copies ran while one was open for 0% -> 0% of each run, Pallas kernels for 2% -> 1%
where the time goes in v7:
time: 201 us; the launch traced here: 200 us
  blocking collectives  156 us (78%)
  Pallas kernels  25.2 us (13%)
  starting transfers between devices  11.5 us (6%)
  waiting for transfers between devices  6.21 us (3%)
    all_to_all x8, blocking collectives, to_all(): return lax.all_to_all(value, SEND_ALL, 0, 0, tiled=True)  122 us
    all_to_all x4, blocking collectives, in_group(): return lax.all_to_all(value, SEND_COL, 0, 0, tiled=True)  33.2 us
    pallas_call x15, Pallas kernels, call(): pl.pallas_call(body, out_shape=shapes, in_specs=in_specs or [VMEM] * len(...  25.2 us
    all_to_all x1, starting transfers between devices, to_all(): return lax.all_to_all(value, SEND_ALL, 0, 0, tiled=True)  11.5 us
    all_to_all x1, waiting for transfers between devices, to_all(): return lax.all_to_all(value, SEND_ALL, 0, 0, tiled=True)  6.21 us
  transfers between devices with their start and end apart: 1, of which 1 were waited for; matrix products, arithmetic and copies ran while one was open for 0% of the time, Pallas kernels for 1%

profile of v7, /device:TPU:1, one launch (start us, length us, event | category | flops | bytes accessed | tf_op | source)
XLA Modules:
  0.0 200.1 jit_solution(13612543962818520736)
XLA Ops:
  0.6 2.4 %shard_map.94 = (f32[128,1,128]{2,1,0:T(1,128)}, s32[1,512]{1,0:T(1,128)S(1)}, s32[512,1]{1,0:T(8,128)S(1)}, s32[1,512]{1,0:T(1,128)S(1)}, s32[512,1]{1,0:T(8,12...) custom-call(s32[1,512]{1,0:T(1,128)} %bitcast.14, s32[1,512]{1,0:T(1,128)} %bitcast.15, f32[100,4096]{1,0:T(8,128)} %basis_hbm.1, ...), custom_call_target="tpu_custom_call" | custom-call | tf_op jit(solution)/shard_map/pallas_call | solution.py:363
  3.0 11.5 %all-to-all-start = ((f32[128,1,128]{2,1,0:T(1,128)}), f32[128,1,128]{2,1,0:T(1,128)S(1)}, u32[]{:S(2)}, u32[]{:S(2)}) async-start(f32[128,1,128]{2,1,0:T(1,128)} %get-tuple-element.43), calls=%async_computation | async-start | bytes 131072 | tf_op jit(solution)/shard_map/all_to_all | solution.py:375
  15.2 2.6 %shard_map.95 = (s32[1,512]{1,0:T(1,128)S(1)}, s32[512,1]{1,0:T(8,128)S(1)}, f32[128,128]{1,0:T(8,128)S(1)}, f32[128,128]{1,0:T(8,128)S(1)}) custom-call(s32[1,1]{1,0:T(1,128)} %bitcast.11.counts, s32[1,512]{1,0:T(1,128)S(1)} %get-tuple-element.46.all_row, s32[512,1]{1,0:T(8,128)S(1)} %get-tuple-element.47.all_col, ...), custom_call_target="tpu_custom_call" | custom-call | tf_op jit(solution)/shard_map/pallas_call | solution.py:363
  17.8 6.2 %all-to-all-done.arrived = f32[128,1,128]{2,1,0:T(1,128)S(1)} async-done(((f32[128,1,128]{2,1,0:T(1,128)}), f32[128,1,128]{2,1,0:T(1,128)S(1)}, u32[]{:S(2)}, u32[]{:S(2)}) %all-to-all-start) | async-done | bytes 65568 | tf_op jit(solution)/shard_map/all_to_all | solution.py:375
  24.1 0.0 copy-start
  24.1 0.9 shard_map.96
  25.0 18.1 %all_to_all.65 = f32[128,9,1,128]{3,2,1,0:T(1,128)S(1)} all-to-all(f32[128,9,1,128]{3,2,1,0:T(1,128)S(1)} %get-tuple-element.50), channel_id=1, replica_groups=mesh['row_0'=4,'row_1'=4,'col_0'=4,'col_1'=2] {'col_1','col_0','row_1','..., dimensions={0} | all-to-all | bytes 1179648 | tf_op jit(solution)/shard_map/all_to_all | solution.py:375
  43.1 0.0 copy-done
  43.1 5.0 %shard_map.97 = (f32[8,32,128]{2,1,0:T(8,128)S(1)}, f32[1,128]{1,0:T(1,128)S(1)}, f32[1,128]{1,0:T(1,128)S(1)}, bf16[512,128,128]{2,1,0:T(8,128)(2,1)S(1)}) custom-call(f32[1152,128]{1,0:T(8,128)S(1)} %bitcast.12, s32[512,1]{1,0:T(8,128)S(1)} %get-tuple-element.51.pos_col, s32[1,512]{1,0:T(1,128)S(1)} %get-tuple-element.52.row_row, ...), custom_call_target="tpu_custom_call" | custom-call | tf_op jit(solution)/shard_map/pallas_call | solution.py:363
  48.1 8.4 %all_to_all.66.arrived = f32[8,32,128]{2,1,0:T(8,128)S(1)} all-to-all(f32[8,32,128]{2,1,0:T(8,128)S(1)} %get-tuple-element.53), channel_id=1, replica_groups=mesh['row_0'=4,'row_1'=4,'col_0'=4,'col_1'=2] {'col_1','col_0'}, dimensions={0} | all-to-all | bytes 262144 | tf_op jit(solution)/shard_map/all_to_all | solution.py:379
  56.5 0.0 copy-done.1
  56.5 0.3 shard_map.98
  56.7 14.3 %all_to_all.67.arrived = f32[128,1,256]{2,1,0:T(1,128)S(1)} all-to-all(f32[128,1,256]{2,1,0:T(1,128)S(1)} %get-tuple-element.55), channel_id=1, replica_groups=mesh['row_0'=4,'row_1'=4,'col_0'=4,'col_1'=2] {'col_1','col_0','row_1','..., dimensions={0} | all-to-all | bytes 262144 | tf_op jit(solution)/shard_map/all_to_all | solution.py:375
  71.0 0.3 shard_map.99
  71.4 8.1 %all_to_all.68.arrived = bf16[8,32,128]{2,1,0:T(8,128)(2,1)S(1)} all-to-all(bf16[8,32,128]{2,1,0:T(8,128)(2,1)S(1)} %get-tuple-element.57), channel_id=1, replica_groups=mesh['row_0'=4,'row_1'=4,'col_0'=4,'col_1'=2] {'col_1','col_0'}, dimensions={0} | all-to-all | bytes 131072 | tf_op jit(solution)/shard_map/all_to_all | solution.py:379
  79.5 3.5 %shard_map.100 = f32[128,8,128]{2,1,0:T(8,128)S(1)} custom-call(bf16[8,32,128]{2,1,0:T(8,128)(2,1)S(1)} %all_to_all.68.arrived, s32[512,1]{1,0:T(8,128)S(1)} %get-tuple-element.58.row_col, s32[1,512]{1,0:T(1,128)S(1)} %get-tuple-element.59.pos_row, bf16[512,128,128]{2,1,0:T(8,128)(2,1)S(1)} %copy-done), custom_call_target="tpu_custom_call" | custom-call | tf_op jit(solution)/shard_map/pallas_call | solution.py:363
  82.9 17.3 %all_to_all.69.arrived = f32[128,8,128]{2,1,0:T(8,128)S(1)} all-to-all(f32[128,8,128]{2,1,0:T(8,128)S(1)} %shard_map.100), channel_id=1, replica_groups=mesh['row_0'=4,'row_1'=4,'col_0'=4,'col_1'=2] {'col_1','col_0','row_1','..., dimensions={0} | all-to-all | bytes 1048576 | tf_op jit(solution)/shard_map/all_to_all | solution.py:375
  100.3 0.5 shard_map.101
  100.8 13.5 %all_to_all.70.arrived = f32[128,1,128]{2,1,0:T(1,128)S(1)} all-to-all(f32[128,1,128]{2,1,0:T(1,128)S(1)} %get-tuple-element.64), channel_id=1, replica_groups=mesh['row_0'=4,'row_1'=4,'col_0'=4,'col_1'=2] {'col_1','col_0','row_1','..., dimensions={0} | all-to-all | bytes 131072 | tf_op jit(solution)/shard_map/all_to_all | solution.py:375
  114.3 0.5 shard_map.102
  114.9 14.7 %all_to_all.71.arrived = bf16[128,8,128]{2,1,0:T(8,128)(2,1)S(1)} all-to-all(bf16[128,8,128]{2,1,0:T(8,128)(2,1)S(1)} %get-tuple-element.67), channel_id=1, replica_groups=mesh['row_0'=4,'row_1'=4,'col_0'=4,'col_1'=2] {'col_1','col_0','row_1','..., dimensions={0} | all-to-all | bytes 524288 | tf_op jit(solution)/shard_map/all_to_all | solution.py:375
  129.6 3.5 %shard_map.103 = f32[8,32,128]{2,1,0:T(8,128)S(1)} custom-call(bf16[128,8,128]{2,1,0:T(8,128)(2,1)S(1)} %all_to_all.71.arrived, s32[512,1]{1,0:T(8,128)S(1)} %get-tuple-element.51.pos_col, s32[1,512]{1,0:T(1,128)S(1)} %get-tuple-element.52.row_row, bf16[512,128,128]{2,1,0:T(8,128)(2,1)S(1)} %get-tuple-element.68.tiles), custom_call_target="tpu_custom_call" | custom-call | tf_op jit(solution)/shard_map/pallas_call | solution.py:363
  133.1 8.4 %all_to_all.72.arrived = f32[8,32,128]{2,1,0:T(8,128)S(1)} all-to-all(f32[8,32,128]{2,1,0:T(8,128)S(1)} %shard_map.103), channel_id=1, replica_groups=mesh['row_0'=4,'row_1'=4,'col_0'=4,'col_1'=2] {'col_1','col_0'}, dimensions={0} | all-to-all | bytes 262144 | tf_op jit(solution)/shard_map/all_to_all | solution.py:379
  141.6 0.3 shard_map.104
  141.9 13.7 %all_to_all.73.arrived = f32[128,1,128]{2,1,0:T(1,128)S(1)} all-to-all(f32[128,1,128]{2,1,0:T(1,128)S(1)} %get-tuple-element.71), channel_id=1, replica_groups=mesh['row_0'=4,'row_1'=4,'col_0'=4,'col_1'=2] {'col_1','col_0','row_1','..., dimensions={0} | all-to-all | bytes 131072 | tf_op jit(solution)/shard_map/all_to_all | solution.py:375
  155.5 0.3 shard_map.105
  155.8 8.3 %all_to_all.74.arrived = bf16[8,32,128]{2,1,0:T(8,128)(2,1)S(1)} all-to-all(bf16[8,32,128]{2,1,0:T(8,128)(2,1)S(1)} %get-tuple-element.74), channel_id=1, replica_groups=mesh['row_0'=4,'row_1'=4,'col_0'=4,'col_1'=2] {'col_1','col_0'}, dimensions={0} | all-to-all | bytes 131072 | tf_op jit(solution)/shard_map/all_to_all | solution.py:379
  164.1 3.5 %shard_map.106 = f32[128,8,128]{2,1,0:T(8,128)S(1)} custom-call(bf16[8,32,128]{2,1,0:T(8,128)(2,1)S(1)} %all_to_all.74.arrived, s32[512,1]{1,0:T(8,128)S(1)} %get-tuple-element.58.row_col, s32[1,512]{1,0:T(1,128)S(1)} %get-tuple-element.59.pos_row, bf16[512,128,128]{2,1,0:T(8,128)(2,1)S(1)} %copy-done), custom_call_target="tpu_custom_call" | custom-call | tf_op jit(solution)/shard_map/pallas_call | solution.py:363
  167.6 17.3 %all_to_all.75.arrived = f32[128,8,128]{2,1,0:T(8,128)S(1)} all-to-all(f32[128,8,128]{2,1,0:T(8,128)S(1)} %shard_map.106), channel_id=1, replica_groups=mesh['row_0'=4,'row_1'=4,'col_0'=4,'col_1'=2] {'col_1','col_0','row_1','..., dimensions={0} | all-to-all | bytes 1048576 | tf_op jit(solution)/shard_map/all_to_all | solution.py:375
  184.9 0.5 shard_map.107
  185.4 13.5 %all_to_all.76.arrived = f32[128,1,128]{2,1,0:T(1,128)S(1)} all-to-all(f32[128,1,128]{2,1,0:T(1,128)S(1)} %get-tuple-element.77), channel_id=1, replica_groups=mesh['row_0'=4,'row_1'=4,'col_0'=4,'col_1'=2] {'col_1','col_0','row_1','..., dimensions={0} | all-to-all | bytes 131072 | tf_op jit(solution)/shard_map/all_to_all | solution.py:375
  199.0 0.9 shard_map.108
  (1 shorter events, 0.0 us)
Async XLA Ops:
  3.0 21.0 %all-to-all-start = ((f32[128,1,128]{2,1,0:T(1,128)}), f32[128,1,128]{2,1,0:T(1,128)S(1)}, u32[]{:S(2)}, u32[]{:S(2)}) async-start(f32[128,1,128]{2,1,0:T(1,128)} %get-tuple-element.43), calls=%async_computation | async-start | bytes 131072 | tf_op jit(solution)/shard_map/all_to_all | solution.py:375
  24.1 19.0 %copy-start = (bf16[512,128,128]{2,1,0:T(8,128)(2,1)S(1)}, bf16[512,128,128]{2,1,0:T(8,128)(2,1)}, u32[]{:S(2)}) copy-start(bf16[512,128,128]{2,1,0:T(8,128)(2,1)} %tiles.5) | copy-start | bytes 50331652
  43.1 13.4 %copy-start.1 = (f32[100,4096]{1,0:T(8,128)S(1)}, f32[100,4096]{1,0:T(8,128)}, u32[]{:S(2)}) copy-start(f32[100,4096]{1,0:T(8,128)} %basis.7) | copy-start | bytes 4915204

commit v8 on v7

--- a/solution.py
+++ b/solution.py
@@ -339,14 +339,15 @@
 
 def last_vector(row_total, arrived, back, basis, gram, earlier, left_one, left_two, *rest):
     norms, (left_pair, new_pair, factors, new, norm) = rest[:4], rest[4:]
+    for i, value in enumerate(norms):
+        factors[i] = value[0, 0]
     left_pair[:, 0, :] = left_one[...]
     left_pair[:, 1, :] = left_two[...]
     total = jnp.sum(arrived[:, 0, :], axis=0, keepdims=True)
     finish(row_total, total, back, basis, gram, new, norm)
     new_pair[:, 0, :] = earlier[...]
     new_pair[:, 1, :] = new[...]
-    for i, value in enumerate((*norms, norm)):
-        factors[i] = jnp.max(value[...])
+    factors[len(norms)] = norm[0, 0]
 
 
 VMEM = pl.BlockSpec(memory_space=pltpu.VMEM)

time: 201 us -> 201 us (level)
  no operation moved by 1% of the time
where the time goes in v8:
time: 201 us; the launch traced here: 200 us
  blocking collectives  156 us (78%)
  Pallas kernels  25.2 us (13%)
  starting transfers between devices  11.5 us (6%)
  waiting for transfers between devices  6.21 us (3%)
    all_to_all x8, blocking collectives, to_all(): return lax.all_to_all(value, SEND_ALL, 0, 0, tiled=True)  122 us
    all_to_all x4, blocking collectives, in_group(): return lax.all_to_all(value, SEND_COL, 0, 0, tiled=True)  33.2 us
    pallas_call x15, Pallas kernels, call(): pl.pallas_call(body, out_shape=shapes, in_specs=in_specs or [VMEM] * len(...  25.2 us
    all_to_all x1, starting transfers between devices, to_all(): return lax.all_to_all(value, SEND_ALL, 0, 0, tiled=True)  11.5 us
    all_to_all x1, waiting for transfers between devices, to_all(): return lax.all_to_all(value, SEND_ALL, 0, 0, tiled=True)  6.21 us
  transfers between devices with their start and end apart: 1, of which 1 were waited for; matrix products, arithmetic and copies ran while one was open for 0% of the time, Pallas kernels for 1%

profile of v8, /device:TPU:1, one launch (start us, length us, event | category | flops | bytes accessed | tf_op | source)
XLA Modules:
  0.0 200.1 jit_solution(13648176743011102314)
XLA Ops:
  0.6 2.4 %shard_map.94 = (f32[128,1,128]{2,1,0:T(1,128)}, s32[1,512]{1,0:T(1,128)S(1)}, s32[512,1]{1,0:T(8,128)S(1)}, s32[1,512]{1,0:T(1,128)S(1)}, s32[512,1]{1,0:T(8,12...) custom-call(s32[1,512]{1,0:T(1,128)} %bitcast.14, s32[1,512]{1,0:T(1,128)} %bitcast.15, f32[100,4096]{1,0:T(8,128)} %basis_hbm.1, ...), custom_call_target="tpu_custom_call" | custom-call | tf_op jit(solution)/shard_map/pallas_call | solution.py:364
  3.0 11.5 %all-to-all-start = ((f32[128,1,128]{2,1,0:T(1,128)}), f32[128,1,128]{2,1,0:T(1,128)S(1)}, u32[]{:S(2)}, u32[]{:S(2)}) async-start(f32[128,1,128]{2,1,0:T(1,128)} %get-tuple-element.43), calls=%async_computation | async-start | bytes 131072 | tf_op jit(solution)/shard_map/all_to_all | solution.py:376
  15.2 2.6 %shard_map.95 = (s32[1,512]{1,0:T(1,128)S(1)}, s32[512,1]{1,0:T(8,128)S(1)}, f32[128,128]{1,0:T(8,128)S(1)}, f32[128,128]{1,0:T(8,128)S(1)}) custom-call(s32[1,1]{1,0:T(1,128)} %bitcast.11.counts, s32[1,512]{1,0:T(1,128)S(1)} %get-tuple-element.46.all_row, s32[512,1]{1,0:T(8,128)S(1)} %get-tuple-element.47.all_col, ...), custom_call_target="tpu_custom_call" | custom-call | tf_op jit(solution)/shard_map/pallas_call | solution.py:364
  17.8 6.2 %all-to-all-done.arrived = f32[128,1,128]{2,1,0:T(1,128)S(1)} async-done(((f32[128,1,128]{2,1,0:T(1,128)}), f32[128,1,128]{2,1,0:T(1,128)S(1)}, u32[]{:S(2)}, u32[]{:S(2)}) %all-to-all-start) | async-done | bytes 65568 | tf_op jit(solution)/shard_map/all_to_all | solution.py:376
  24.1 0.0 copy-start
  24.1 0.9 shard_map.96
  25.0 18.1 %all_to_all.65 = f32[128,9,1,128]{3,2,1,0:T(1,128)S(1)} all-to-all(f32[128,9,1,128]{3,2,1,0:T(1,128)S(1)} %get-tuple-element.50), channel_id=1, replica_groups=mesh['row_0'=4,'row_1'=4,'col_0'=4,'col_1'=2] {'col_1','col_0','row_1','..., dimensions={0} | all-to-all | bytes 1179648 | tf_op jit(solution)/shard_map/all_to_all | solution.py:376
  43.1 0.0 copy-done
  43.1 5.0 %shard_map.97 = (f32[8,32,128]{2,1,0:T(8,128)S(1)}, f32[1,128]{1,0:T(1,128)S(1)}, f32[1,128]{1,0:T(1,128)S(1)}, bf16[512,128,128]{2,1,0:T(8,128)(2,1)S(1)}) custom-call(f32[1152,128]{1,0:T(8,128)S(1)} %bitcast.12, s32[512,1]{1,0:T(8,128)S(1)} %get-tuple-element.51.pos_col, s32[1,512]{1,0:T(1,128)S(1)} %get-tuple-element.52.row_row, ...), custom_call_target="tpu_custom_call" | custom-call | tf_op jit(solution)/shard_map/pallas_call | solution.py:364
  48.1 8.4 %all_to_all.66.arrived = f32[8,32,128]{2,1,0:T(8,128)S(1)} all-to-all(f32[8,32,128]{2,1,0:T(8,128)S(1)} %get-tuple-element.53), channel_id=1, replica_groups=mesh['row_0'=4,'row_1'=4,'col_0'=4,'col_1'=2] {'col_1','col_0'}, dimensions={0} | all-to-all | bytes 262144 | tf_op jit(solution)/shard_map/all_to_all | solution.py:380
  56.5 0.0 copy-done.1
  56.5 0.3 shard_map.98
  56.7 14.3 %all_to_all.67.arrived = f32[128,1,256]{2,1,0:T(1,128)S(1)} all-to-all(f32[128,1,256]{2,1,0:T(1,128)S(1)} %get-tuple-element.55), channel_id=1, replica_groups=mesh['row_0'=4,'row_1'=4,'col_0'=4,'col_1'=2] {'col_1','col_0','row_1','..., dimensions={0} | all-to-all | bytes 262144 | tf_op jit(solution)/shard_map/all_to_all | solution.py:376
  71.0 0.3 shard_map.99
  71.4 8.1 %all_to_all.68.arrived = bf16[8,32,128]{2,1,0:T(8,128)(2,1)S(1)} all-to-all(bf16[8,32,128]{2,1,0:T(8,128)(2,1)S(1)} %get-tuple-element.57), channel_id=1, replica_groups=mesh['row_0'=4,'row_1'=4,'col_0'=4,'col_1'=2] {'col_1','col_0'}, dimensions={0} | all-to-all | bytes 131072 | tf_op jit(solution)/shard_map/all_to_all | solution.py:380
  79.5 3.5 %shard_map.100 = f32[128,8,128]{2,1,0:T(8,128)S(1)} custom-call(bf16[8,32,128]{2,1,0:T(8,128)(2,1)S(1)} %all_to_all.68.arrived, s32[512,1]{1,0:T(8,128)S(1)} %get-tuple-element.58.row_col, s32[1,512]{1,0:T(1,128)S(1)} %get-tuple-element.59.pos_row, bf16[512,128,128]{2,1,0:T(8,128)(2,1)S(1)} %copy-done), custom_call_target="tpu_custom_call" | custom-call | tf_op jit(solution)/shard_map/pallas_call | solution.py:364
  82.9 17.3 %all_to_all.69.arrived = f32[128,8,128]{2,1,0:T(8,128)S(1)} all-to-all(f32[128,8,128]{2,1,0:T(8,128)S(1)} %shard_map.100), channel_id=1, replica_groups=mesh['row_0'=4,'row_1'=4,'col_0'=4,'col_1'=2] {'col_1','col_0','row_1','..., dimensions={0} | all-to-all | bytes 1048576 | tf_op jit(solution)/shard_map/all_to_all | solution.py:376
  100.3 0.5 shard_map.101
  100.8 13.5 %all_to_all.70.arrived = f32[128,1,128]{2,1,0:T(1,128)S(1)} all-to-all(f32[128,1,128]{2,1,0:T(1,128)S(1)} %get-tuple-element.64), channel_id=1, replica_groups=mesh['row_0'=4,'row_1'=4,'col_0'=4,'col_1'=2] {'col_1','col_0','row_1','..., dimensions={0} | all-to-all | bytes 131072 | tf_op jit(solution)/shard_map/all_to_all | solution.py:376
  114.3 0.5 shard_map.102
  114.9 14.7 %all_to_all.71.arrived = bf16[128,8,128]{2,1,0:T(8,128)(2,1)S(1)} all-to-all(bf16[128,8,128]{2,1,0:T(8,128)(2,1)S(1)} %get-tuple-element.67), channel_id=1, replica_groups=mesh['row_0'=4,'row_1'=4,'col_0'=4,'col_1'=2] {'col_1','col_0','row_1','..., dimensions={0} | all-to-all | bytes 524288 | tf_op jit(solution)/shard_map/all_to_all | solution.py:376
  129.6 3.5 %shard_map.103 = f32[8,32,128]{2,1,0:T(8,128)S(1)} custom-call(bf16[128,8,128]{2,1,0:T(8,128)(2,1)S(1)} %all_to_all.71.arrived, s32[512,1]{1,0:T(8,128)S(1)} %get-tuple-element.51.pos_col, s32[1,512]{1,0:T(1,128)S(1)} %get-tuple-element.52.row_row, bf16[512,128,128]{2,1,0:T(8,128)(2,1)S(1)} %get-tuple-element.68.tiles), custom_call_target="tpu_custom_call" | custom-call | tf_op jit(solution)/shard_map/pallas_call | solution.py:364
  133.1 8.4 %all_to_all.72.arrived = f32[8,32,128]{2,1,0:T(8,128)S(1)} all-to-all(f32[8,32,128]{2,1,0:T(8,128)S(1)} %shard_map.103), channel_id=1, replica_groups=mesh['row_0'=4,'row_1'=4,'col_0'=4,'col_1'=2] {'col_1','col_0'}, dimensions={0} | all-to-all | bytes 262144 | tf_op jit(solution)/shard_map/all_to_all | solution.py:380
  141.6 0.3 shard_map.104
  141.9 13.7 %all_to_all.73.arrived = f32[128,1,128]{2,1,0:T(1,128)S(1)} all-to-all(f32[128,1,128]{2,1,0:T(1,128)S(1)} %get-tuple-element.71), channel_id=1, replica_groups=mesh['row_0'=4,'row_1'=4,'col_0'=4,'col_1'=2] {'col_1','col_0','row_1','..., dimensions={0} | all-to-all | bytes 131072 | tf_op jit(solution)/shard_map/all_to_all | solution.py:376
  155.5 0.3 shard_map.105
  155.8 8.3 %all_to_all.74.arrived = bf16[8,32,128]{2,1,0:T(8,128)(2,1)S(1)} all-to-all(bf16[8,32,128]{2,1,0:T(8,128)(2,1)S(1)} %get-tuple-element.74), channel_id=1, replica_groups=mesh['row_0'=4,'row_1'=4,'col_0'=4,'col_1'=2] {'col_1','col_0'}, dimensions={0} | all-to-all | bytes 131072 | tf_op jit(solution)/shard_map/all_to_all | solution.py:380
  164.1 3.5 %shard_map.106 = f32[128,8,128]{2,1,0:T(8,128)S(1)} custom-call(bf16[8,32,128]{2,1,0:T(8,128)(2,1)S(1)} %all_to_all.74.arrived, s32[512,1]{1,0:T(8,128)S(1)} %get-tuple-element.58.row_col, s32[1,512]{1,0:T(1,128)S(1)} %get-tuple-element.59.pos_row, bf16[512,128,128]{2,1,0:T(8,128)(2,1)S(1)} %copy-done), custom_call_target="tpu_custom_call" | custom-call | tf_op jit(solution)/shard_map/pallas_call | solution.py:364
  167.6 17.3 %all_to_all.75.arrived = f32[128,8,128]{2,1,0:T(8,128)S(1)} all-to-all(f32[128,8,128]{2,1,0:T(8,128)S(1)} %shard_map.106), channel_id=1, replica_groups=mesh['row_0'=4,'row_1'=4,'col_0'=4,'col_1'=2] {'col_1','col_0','row_1','..., dimensions={0} | all-to-all | bytes 1048576 | tf_op jit(solution)/shard_map/all_to_all | solution.py:376
  184.9 0.5 shard_map.107
  185.4 13.5 %all_to_all.76.arrived = f32[128,1,128]{2,1,0:T(1,128)S(1)} all-to-all(f32[128,1,128]{2,1,0:T(1,128)S(1)} %get-tuple-element.77), channel_id=1, replica_groups=mesh['row_0'=4,'row_1'=4,'col_0'=4,'col_1'=2] {'col_1','col_0','row_1','..., dimensions={0} | all-to-all | bytes 131072 | tf_op jit(solution)/shard_map/all_to_all | solution.py:376
  199.0 0.9 shard_map.108
  (1 shorter events, 0.0 us)
Async XLA Ops:
  3.0 21.0 %all-to-all-start = ((f32[128,1,128]{2,1,0:T(1,128)}), f32[128,1,128]{2,1,0:T(1,128)S(1)}, u32[]{:S(2)}, u32[]{:S(2)}) async-start(f32[128,1,128]{2,1,0:T(1,128)} %get-tuple-element.43), calls=%async_computation | async-start | bytes 131072 | tf_op jit(solution)/shard_map/all_to_all | solution.py:376
  24.1 19.0 %copy-start = (bf16[512,128,128]{2,1,0:T(8,128)(2,1)S(1)}, bf16[512,128,128]{2,1,0:T(8,128)(2,1)}, u32[]{:S(2)}) copy-start(bf16[512,128,128]{2,1,0:T(8,128)(2,1)} %tiles.5) | copy-start | bytes 50331652
  43.1 13.4 %copy-start.1 = (f32[100,4096]{1,0:T(8,128)S(1)}, f32[100,4096]{1,0:T(8,128)}, u32[]{:S(2)}) copy-start(f32[100,4096]{1,0:T(8,128)} %basis.7) | copy-start | bytes 4915204
